TPU v7x, 32 devices: a whole 2x2x4 slice. The times are simulated.
32 devices in a mesh: dp: 8 (over y, x, core), tensor: 4 (over z).
Axes of the slice: x: 2, y: 2, z: 4, core: 2. Of those that a mesh axis runs over, the one named last changes fastest.
Arguments:
- tokens: bfloat16 [8192, 1536], P('dp'), may hold values from -6 to 6
- block_order: int32 [1, 8], replicated, may hold values from 0 to 7, each once within a row
- attn_gain: float32 [1536], replicated, may hold values from 0.5 to 1.5
- w_query: bfloat16 [1536, 1536], P(None, 'tensor'), may hold values from -0.15625 to 0.15625
- w_key: bfloat16 [1536, 768], P(None, 'tensor'), may hold values from -0.15625 to 0.15625
- w_value: bfloat16 [1536, 768], P(None, 'tensor'), may hold values from -0.15625 to 0.15625
- w_out: bfloat16 [1536, 1536], P('tensor'), may hold values from -1.25 to 1.25
- mlp_gain: float32 [1536], replicated, may hold values from 0.5 to 1.5
- w_gate: bfloat16 [1536, 4096], P(None, 'tensor'), may hold values from -0.15625 to 0.15625
- w_up: bfloat16 [1536, 4096], P(None, 'tensor'), may hold values from -0.15625 to 0.15625
- w_down: bfloat16 [4096, 1536], P('tensor'), may hold values from -0.09375 to 0.09375
- cotangent: bfloat16 [8192, 1536], P('dp'), may hold values from -6 to 6
Outputs:
- activations: bfloat16 [8192, 1536], P('dp')
- grad_tokens: bfloat16 [8192, 1536], P('dp')
- grad_attn_gain: float32 [1536], replicated
- grad_query: float32 [1536, 1536], P(None, 'tensor')
- grad_key: float32 [1536, 768], P(None, 'tensor')
- grad_value: float32 [1536, 768], P(None, 'tensor')
- grad_out: float32 [1536, 1536], P('tensor')
- grad_mlp_gain: float32 [1536], replicated
- grad_gate: float32 [1536, 4096], P(None, 'tensor')
- grad_up: float32 [1536, 4096], P(None, 'tensor')
- grad_down: float32 [4096, 1536], P('tensor')
Inputs may be any that keep to these rules, and one draw needn't show every extreme that they name: `block_order`: entry j of row g is the prompt block of 512 tokens held by the j-th device of group g; each row is a permutation.
All inputs are finite; a program needn't handle non-finite values.
Results may differ from a plain program's by a relative error of at most 0.02.
Values may be sent and summed in bfloat16 or wider, within the bound.
A program may use at most 192 MiB of HBM per device.

v0:
```python
import jax
import jax.numpy as jnp
from jax import lax
from jax.sharding import PartitionSpec as P

HEAD_DIM = 96
GROUP_DEVS = 8
PB = 512
CL = 512


EPSILON = 1e-05
ROTARY_BASE = 100000.0


def from_partner(value, axis, distance):
    mask = 2**distance
    pairs = [(source, source ^ mask) for source in range(lax.axis_size(axis))]
    return lax.ppermute(value, axis, pairs)


def rotary_tables(places):
    halfway = HEAD_DIM // 2
    frequency = ROTARY_BASE ** (-(jnp.arange(halfway, dtype=jnp.float32) * 2.0) / HEAD_DIM)
    angle = places.astype(jnp.float32)[:, None] * frequency[None, :]
    cosine_table = jnp.concatenate([jnp.cos(angle), jnp.cos(angle)], axis=-1)
    sine_table = jnp.concatenate([jnp.sin(angle), jnp.sin(angle)], axis=-1)
    return (cosine_table, sine_table)


def rotate(inputs, cosine_table, sine_table):
    halfway = inputs.shape[-1] // 2
    shaped = (inputs.shape[0],) + (1,) * (inputs.ndim - 2) + (inputs.shape[-1],)
    turned = jnp.concatenate([-inputs[..., halfway:], inputs[..., :halfway]], axis=-1)
    return inputs * cosine_table.reshape(shaped) + turned * sine_table.reshape(shaped)


def product(former, latter):
    return jnp.dot(former, latter, preferred_element_type=jnp.float32)


def weight_grad(former, latter):
    return lax.dot_general(
        former, latter, (((0,), (0,)), ((), ())), preferred_element_type=jnp.float32
    )


def input_grad(former, latter):
    return lax.dot_general(
        former, latter, (((1,), (1,)), ((), ())), preferred_element_type=jnp.float32
    )


def rms_inverse(inputs):
    return lax.rsqrt(jnp.mean(inputs * inputs, axis=-1, keepdims=True) + EPSILON)


def norm_back(inputs, inverse, gain, upstream):
    inner = upstream * gain
    through = inverse * inner - inputs * inverse**3 * jnp.mean(
        inner * inputs, axis=-1, keepdims=True
    )
    return (through, jnp.sum(upstream * inputs * inverse, axis=0))


def shards(
    tokens,
    block_order,
    attn_gain,
    w_query,
    w_key,
    w_value,
    w_out,
    mlp_gain,
    w_gate,
    w_up,
    w_down,
    cotangent,
):
    device = lax.axis_index("dp")
    member = device % GROUP_DEVS
    group_index = device // GROUP_DEVS
    order_row = lax.dynamic_index_in_dim(block_order, group_index, 0, keepdims=False)
    own_block = lax.dynamic_index_in_dim(order_row, member, 0, keepdims=False)
    offsets = jnp.arange(PB, dtype=jnp.int32)
    prompt_places = order_row[:, None] * PB + offsets[None, :]
    tail_places = GROUP_DEVS * PB + jnp.arange(CL, dtype=jnp.int32)
    places = jnp.concatenate([own_block * PB + offsets, tail_places])
    cosine_table, sine_table = rotary_tables(places)
    token_count = tokens.shape[0]
    key_heads = w_key.shape[1] // HEAD_DIM
    repeat = w_query.shape[1] // HEAD_DIM // key_heads
    factor = HEAD_DIM ** (-0.5)
    inputs = tokens.astype(jnp.float32)
    inverse_one = rms_inverse(inputs)
    normed = (inputs * inverse_one * attn_gain).astype(jnp.bfloat16)
    queries = rotate(
        product(normed, w_query).reshape(token_count, key_heads, repeat, HEAD_DIM),
        cosine_table,
        sine_table,
    ).astype(jnp.bfloat16)
    key_set = rotate(
        product(normed, w_key).reshape(token_count, key_heads, HEAD_DIM), cosine_table, sine_table
    ).astype(jnp.bfloat16)
    value_set = (
        product(normed, w_value).reshape(token_count, key_heads, HEAD_DIM).astype(jnp.bfloat16)
    )
    levels = GROUP_DEVS.bit_length() - 1
    stacked = jnp.stack([key_set[:PB], value_set[:PB]])[:, None]
    for level in range(levels):
        partner = from_partner(stacked, "dp", level)
        upper = member // 2**level % 2 == 1
        stacked = jnp.where(
            upper,
            jnp.concatenate([partner, stacked], axis=1),
            jnp.concatenate([stacked, partner], axis=1),
        )
    prompt_keys = stacked[0]
    prompt_values = stacked[1]
    tail_keys = key_set[PB:]
    tail_values = value_set[PB:]

    def scores(key_block, key_places):
        products = (
            jnp.einsum("qkrd,nkd->krqn", queries, key_block, preferred_element_type=jnp.float32)
            * factor
        )
        visible = key_places[None, None, None, :] <= places[None, None, :, None]
        return (products, visible)

    def total_step(running, block):
        summit, totals = running
        products, visible = scores(block[0], block[1])
        masked = jnp.where(visible, products, -1e30)
        higher = jnp.maximum(summit, jnp.max(masked, axis=-1))
        totals = totals * jnp.exp(summit - higher) + jnp.sum(
            jnp.where(visible, jnp.exp(masked - higher[..., None]), 0.0), axis=-1
        )
        return ((higher, totals), None)

    start = (
        jnp.full((key_heads, repeat, token_count), -1e30, jnp.float32),
        jnp.zeros((key_heads, repeat, token_count), jnp.float32),
    )
    running, _ = lax.scan(total_step, start, (prompt_keys, prompt_places))
    running, _ = total_step(running, (tail_keys, tail_places))
    log_total = running[0] + jnp.log(running[1])

    def chances_of(products, visible):
        return jnp.where(visible, jnp.exp(products - log_total[..., None]), 0.0)

    def output_step(summed, block):
        products, visible = scores(block[0], block[2])
        weights = chances_of(products, visible).astype(jnp.bfloat16)
        return (
            summed
            + jnp.einsum("krqn,nkd->qkrd", weights, block[1], preferred_element_type=jnp.float32),
            None,
        )

    empty_heads = jnp.zeros((token_count, key_heads, repeat, HEAD_DIM), jnp.float32)
    attended, _ = lax.scan(output_step, empty_heads, (prompt_keys, prompt_values, prompt_places))
    attended, _ = output_step(attended, (tail_keys, tail_values, tail_places))
    attended_low = attended.reshape(token_count, -1).astype(jnp.bfloat16)
    attention = lax.psum(product(attended_low, w_out).astype(jnp.bfloat16), "tensor").astype(
        jnp.float32
    )
    middle = inputs + attention
    inverse_two = rms_inverse(middle)
    normed_two = (middle * inverse_two * mlp_gain).astype(jnp.bfloat16)
    gate_pre = product(normed_two, w_gate)
    up_pre = product(normed_two, w_up)
    sigmoid_gate = jax.nn.sigmoid(gate_pre)
    hidden = (gate_pre * sigmoid_gate * up_pre).astype(jnp.bfloat16)
    feed_out = lax.psum(product(hidden, w_down).astype(jnp.bfloat16), "tensor").astype(jnp.float32)
    activations = (middle + feed_out).astype(jnp.bfloat16)
    upstream = cotangent.astype(jnp.float32)
    grad_hidden = input_grad(cotangent, w_down)
    grad_gate_low = (
        grad_hidden * up_pre * sigmoid_gate * (1.0 + gate_pre * (1.0 - sigmoid_gate))
    ).astype(jnp.bfloat16)
    grad_up_low = (grad_hidden * gate_pre * sigmoid_gate).astype(jnp.bfloat16)
    grad_w_gate = weight_grad(normed_two, grad_gate_low)
    grad_w_up = weight_grad(normed_two, grad_up_low)
    grad_w_down = weight_grad(hidden, cotangent)
    grad_normed_two = lax.psum(
        (input_grad(grad_gate_low, w_gate) + input_grad(grad_up_low, w_up)).astype(jnp.bfloat16),
        "tensor",
    ).astype(jnp.float32)
    through_two, grad_gain_two = norm_back(middle, inverse_two, mlp_gain, grad_normed_two)
    grad_middle = upstream + through_two
    grad_attention = grad_middle.astype(jnp.bfloat16)
    grad_w_out = weight_grad(attended_low, grad_attention)
    grad_attended = (
        input_grad(grad_attention, w_out)
        .reshape(token_count, key_heads, repeat, HEAD_DIM)
        .astype(jnp.bfloat16)
    )
    row_inner = jnp.transpose(
        jnp.sum(grad_attended.astype(jnp.float32) * attended, axis=-1), (1, 2, 0)
    )

    def back_step(grad_queries, block):
        products, visible = scores(block[0], block[2])
        chances = chances_of(products, visible)
        grad_chances = jnp.einsum(
            "qkrd,nkd->krqn", grad_attended, block[1], preferred_element_type=jnp.float32
        )
        grad_scores = (chances * (grad_chances - row_inner[..., None])).astype(jnp.bfloat16)
        grad_queries = (
            grad_queries
            + jnp.einsum(
                "krqn,nkd->qkrd", grad_scores, block[0], preferred_element_type=jnp.float32
            )
            * factor
        )
        grad_keys = (
            jnp.einsum("krqn,qkrd->nkd", grad_scores, queries, preferred_element_type=jnp.float32)
            * factor
        )
        grad_values = jnp.einsum(
            "krqn,qkrd->nkd",
            chances.astype(jnp.bfloat16),
            grad_attended,
            preferred_element_type=jnp.float32,
        )
        return (grad_queries, (grad_keys, grad_values))

    grad_queries, prompt_grads = lax.scan(
        back_step, empty_heads, (prompt_keys, prompt_values, prompt_places)
    )
    grad_queries, tail_grads = back_step(grad_queries, (tail_keys, tail_values, tail_places))
    pending = jnp.stack([prompt_grads[0], prompt_grads[1]])
    for level in reversed(range(levels)):
        halfway = pending.shape[1] // 2
        upper = member // 2**level % 2 == 1
        kept_part = jnp.where(upper, pending[:, halfway:], pending[:, :halfway])
        sent_part = jnp.where(upper, pending[:, :halfway], pending[:, halfway:])
        pending = kept_part + from_partner(sent_part.astype(jnp.bfloat16), "dp", level).astype(
            sent_part.dtype
        )
    grad_key_rot = jnp.concatenate([pending[0, 0], tail_grads[0]])
    grad_value_all = jnp.concatenate([pending[1, 0], tail_grads[1]])
    grad_query_low = (
        rotate(grad_queries, cosine_table, -sine_table)
        .reshape(token_count, -1)
        .astype(jnp.bfloat16)
    )
    grad_key_low = (
        rotate(grad_key_rot, cosine_table, -sine_table)
        .reshape(token_count, -1)
        .astype(jnp.bfloat16)
    )
    grad_value_low = grad_value_all.reshape(token_count, -1).astype(jnp.bfloat16)
    grad_w_query = weight_grad(normed, grad_query_low)
    grad_w_key = weight_grad(normed, grad_key_low)
    grad_w_value = weight_grad(normed, grad_value_low)
    grad_normed = lax.psum(
        (
            input_grad(grad_query_low, w_query)
            + input_grad(grad_key_low, w_key)
            + input_grad(grad_value_low, w_value)
        ).astype(jnp.bfloat16),
        "tensor",
    ).astype(jnp.float32)
    through_one, grad_gain_one = norm_back(inputs, inverse_one, attn_gain, grad_normed)
    grad_tokens = (grad_middle + through_one).astype(jnp.bfloat16)
    shares = (
        lax.psum_scatter(grad_gain_one, "dp", scatter_dimension=0, tiled=True),
        lax.psum_scatter(grad_w_query, "dp", scatter_dimension=0, tiled=True),
        lax.psum_scatter(grad_w_key, "dp", scatter_dimension=0, tiled=True),
        lax.psum_scatter(grad_w_value, "dp", scatter_dimension=0, tiled=True),
        lax.psum_scatter(grad_w_out, "dp", scatter_dimension=1, tiled=True),
        lax.psum_scatter(grad_gain_two, "dp", scatter_dimension=0, tiled=True),
        lax.psum_scatter(grad_w_gate, "dp", scatter_dimension=0, tiled=True),
        lax.psum_scatter(grad_w_up, "dp", scatter_dimension=0, tiled=True),
        lax.psum_scatter(grad_w_down, "dp", scatter_dimension=1, tiled=True),
    )
    summed_grads = (
        lax.all_gather(shares[0].astype(jnp.bfloat16), "dp", axis=0, tiled=True).astype(
            jnp.float32
        ),
        lax.all_gather(shares[1].astype(jnp.bfloat16), "dp", axis=0, tiled=True).astype(
            jnp.float32
        ),
        lax.all_gather(shares[2].astype(jnp.bfloat16), "dp", axis=0, tiled=True).astype(
            jnp.float32
        ),
        lax.all_gather(shares[3].astype(jnp.bfloat16), "dp", axis=0, tiled=True).astype(
            jnp.float32
        ),
        lax.all_gather(shares[4].astype(jnp.bfloat16), "dp", axis=1, tiled=True).astype(
            jnp.float32
        ),
        lax.all_gather(shares[5].astype(jnp.bfloat16), "dp", axis=0, tiled=True).astype(
            jnp.float32
        ),
        lax.all_gather(shares[6].astype(jnp.bfloat16), "dp", axis=0, tiled=True).astype(
            jnp.float32
        ),
        lax.all_gather(shares[7].astype(jnp.bfloat16), "dp", axis=0, tiled=True).astype(
            jnp.float32
        ),
        lax.all_gather(shares[8].astype(jnp.bfloat16), "dp", axis=1, tiled=True).astype(
            jnp.float32
        ),
    )
    return (activations, grad_tokens) + tuple(summed_grads)


def solution(mesh):
    in_specs = (
        P("dp", None),
        P(),
        P(),
        P(None, "tensor"),
        P(None, "tensor"),
        P(None, "tensor"),
        P("tensor", None),
        P(),
        P(None, "tensor"),
        P(None, "tensor"),
        P("tensor", None),
        P("dp", None),
    )
    out_specs = (
        P("dp", None),
        P("dp", None),
        P(),
        P(None, "tensor"),
        P(None, "tensor"),
        P(None, "tensor"),
        P("tensor", None),
        P(),
        P(None, "tensor"),
        P(None, "tensor"),
        P("tensor", None),
    )
    return jax.shard_map(shards, mesh=mesh, in_specs=in_specs, out_specs=out_specs, check_vma=False)
```

profile of v0, /device:TPU:25, one launch (start us, length us, event | category | flops | bytes accessed | tf_op | source)
XLA Modules:
  0.0 1501.3 jit_solution(2448952385256326114)
XLA Ops:
  30.8 14.2 collective-permute-done.1
  59.8 6.5 fusion.59
  66.3 17.0 %collective-permute-done.2 = bf16[2,4,512,2,96]{2,4,3,0,1:T(8,128)(2,1)} collective-permute-done((bf16[2,4,512,2,96]{2,4,3,0,1:T(8,128)(2,1)}, bf16[2,4,512,2,96]{2,4,3,0,1:T(8,128)(2,1)}, u32[]{:S(2)}, u32[]{:S(2)}) %collective-permute-start.2) | collective-permute-done | bytes 1572896 | tf_op jit(solution)/shard_map/ppermute | solution.py:19
  88.5 92.3 %while.39 = (s32[]{:T(128)}, f32[2,2,1024]{2,1,0:T(2,128)S(1)}, f32[2,2,1024]{2,1,0:T(2,128)S(1)}, s32[8,512]{1,0:T(8,128)S(1)}, s32[1024]{0:T(1024)S(1)}, /*ind...) while((s32[]{:T(128)}, f32[2,2,1024]{2,1,0:T(2,128)S(1)}, ...), condition=%wide.region_4.5_spmd.clone, body=%wide.region_1.4_spmd.clone.sunk | while | flops 419975168 | bytes 21654152 | solution.py:145
  88.9 6.4 fusion.203
  100.4 6.4 fusion.203
  111.9 6.4 fusion.203
  123.5 6.4 fusion.203
  135.0 6.4 fusion.203
  146.6 6.4 fusion.203
  158.1 6.4 fusion.203
  169.6 6.4 fusion.203
  186.0 74.3 %while.40 = (s32[]{:T(128)}, f32[1024,2,2,96]{0,3,2,1:T(8,128)}, bf16[8,512,2,96]{1,3,2,0:T(8,128)(2,1)}, s32[8,512]{1,0:T(8,128)S(1)}, s32[1024]{0:T(1024)S(1)}...) while((s32[]{:T(128)}, f32[1024,2,2,96]{0,3,2,1:T(8,128)}, ...), condition=%wide.region_8.9_spmd.clone, body=%wide.region_7.8_spmd.clone.sunk | while | flops 815005696 | bytes 6646447 | solution.py:162
  197.8 6.3 bitcast_add_fusion.6
  207.1 6.3 bitcast_add_fusion.6
  216.5 6.3 bitcast_add_fusion.6
  225.8 6.3 bitcast_add_fusion.6
  235.1 6.3 bitcast_add_fusion.6
  244.4 6.3 bitcast_add_fusion.6
  253.7 6.3 bitcast_add_fusion.6
  260.3 7.2 fusion.99
  272.0 121.6 %all-reduce.11.cloned.1.call-done = bf16[1024,1536]{1,0:T(8,128)(2,1)} async-done(((bf16[1024,1536]{1,0:T(8,128)(2,1)}), bf16[1024,1536]{1,0:T(8,128)(2,1)}) %all-reduce.11.cloned.1.call-update) | async-done | bytes 3145744 | tf_op jit(solution)/shard_map/psum | solution.py:165
  409.0 8.3 multiply_convert_fusion.1
  428.1 120.2 %all-reduce.13.cloned.1.call-done = bf16[1024,1536]{1,0:T(8,128)(2,1)} async-done(((bf16[1024,1536]{1,0:T(8,128)(2,1)}), bf16[1024,1536]{1,0:T(8,128)(2,1)}) %all-reduce.13.cloned.1.call-update) | async-done | bytes 3145744 | tf_op jit(solution)/shard_map/psum | solution.py:186
  548.3 6.9 fusion.71
  568.2 181.3 %while.41 = (s32[]{:T(128)}, f32[1024,2,2,96]{0,3,2,1:T(8,128)}, f32[8,512,2,96]{1,3,2,0:T(8,128)}, f32[8,512,2,96]{1,3,2,0:T(8,128)}, bf16[8,512,2,96]{1,3,2,0:...) while((s32[]{:T(128)}, f32[1024,2,2,96]{0,3,2,1:T(8,128)}, ...), condition=%wide.region_16.17_spmd.clone, body=%wide.region_15.16_spmd.clone.sunk | while | flops 2036039680 | bytes 111014752 | solution.py:229
  607.5 6.1 fusion.223
  630.2 6.0 fusion.223
  763.5 8.7 fusion.124
  772.3 9.0 fusion.125
  781.4 8.6 fusion.126
  795.4 37.3 %collective-permute-done.3 = bf16[2,4,512,2,96]{2,4,3,1,0:T(8,128)(2,1)S(1)} collective-permute-done((bf16[2,4,512,2,96]{2,4,3,1,0:T(8,128)(2,1)S(1)}, bf16[2,4,512,2,96]{2,4,3,1,0:T(8,128)(2,1)S(1)}, u32[]{:S(2)}, u32[]{:S(2)}) %collective-permute-start.3) | collective-permute-done | bytes 1572896 | tf_op jit(solution)/shard_map/ppermute | solution.py:19
  838.1 33.1 %collective-permute-done.4 = bf16[2,2,512,2,96]{2,4,3,1,0:T(8,128)(2,1)S(1)} collective-permute-done((bf16[2,2,512,2,96]{2,4,3,1,0:T(8,128)(2,1)S(1)}, bf16[2,2,512,2,96]{2,4,3,1,0:T(8,128)(2,1)S(1)}, u32[]{:S(2)}, u32[]{:S(2)}) %collective-permute-start.4) | collective-permute-done | bytes 786464 | tf_op jit(solution)/shard_map/ppermute | solution.py:19
  893.0 6.5 convolution_convert_fusion.1
  907.9 49.9 %reduce-scatter.18.cloned.1.call-done = f32[192,1024]{1,0:T(8,128)} async-done(((f32[1536,1024]{1,0:T(8,128)}), f32[192,1024]{1,0:T(8,128)}) %reduce-scatter.18.cloned.1.call-update) | async-done | bytes 786448 | tf_op jit(solution)/shard_map/reduce_scatter | solution.py:276
  959.8 63.1 %reduce-scatter.20.cloned.1.call-done = f32[1024,192]{0,1:T(8,128)} async-done(((f32[1024,1536]{0,1:T(8,128)}), f32[1024,192]{0,1:T(8,128)}) %reduce-scatter.20.cloned.1.call-update) | async-done | bytes 786448 | tf_op jit(solution)/shard_map/reduce_scatter | solution.py:277
  1026.8 38.3 %reduce-scatter.12.cloned.1.call-done = f32[192,192]{1,0:T(8,128)} async-done(((f32[1536,192]{1,0:T(8,128)}), f32[192,192]{1,0:T(8,128)}) %reduce-scatter.12.cloned.1.call-update) | async-done | bytes 147472 | tf_op jit(solution)/shard_map/reduce_scatter | solution.py:272
  1066.0 11.8 all_gather.30
  1080.2 26.9 %reduce-scatter.10.cloned.1.call-done = f32[192,192]{1,0:T(8,128)} async-done(((f32[1536,192]{1,0:T(8,128)}), f32[192,192]{1,0:T(8,128)}) %reduce-scatter.10.cloned.1.call-update) | async-done | bytes 147472 | tf_op jit(solution)/shard_map/reduce_scatter | solution.py:271
  1108.1 11.8 all_gather.29
  1122.3 11.2 all-gather.8.cloned.1.call-done
  1136.3 24.0 %all-gather.6.cloned.1.call-done = bf16[1536,384]{1,0:T(8,128)(2,1)} async-done(((bf16[192,384]{1,0:T(8,128)(2,1)}), bf16[1536,384]{1,0:T(8,128)(2,1)}) %all-gather.6.cloned.1.call-update) | async-done | bytes 1179664 | tf_op jit(solution)/shard_map/all_gather | solution.py:283
  1163.1 220.9 %all-reduce.15.cloned.1.call-done = (bf16[1024,1536]{1,0:T(8,128)(2,1)}, bf16[1024,1536]{1,0:T(8,128)(2,1)}) async-done(((bf16[1024,1536]{1,0:T(8,128)(2,1)}, bf16[1024,1536]{1,0:T(8,128)(2,1)}), (bf16[1024,1536]{1,0:T(8,128)(2,1)}, bf16[1024,1536]{1,0:T(8,128)(2,1)})) %all-reduce.15.cloned.1.call-update) | async-done | bytes 6291472 | tf_op jit(solution)/shard_map/psum | solution.py:175
  1388.5 21.8 %all-reduce.4 = (bf16[1536]{0:T(1024)(128)(2,1)S(1)}, bf16[1536]{0:T(1024)(128)(2,1)S(1)}) all-reduce(f32[1536]{0:T(1024)S(1)} %get-tuple-element.291, f32[1536]{0:T(1024)S(1)} %copy-done.62), channel_id=2, replica_groups=mesh['dp'=8,'tensor'=4] {'dp'}, use_global_device_ids=true, to_apply=%region_20.21.clone | all-reduce | flops 3072 | bytes 18432
  1410.9 15.1 %all-reduce.5 = (bf16[1536]{0:T(1024)(128)(2,1)S(1)}, bf16[1536]{0:T(1024)(128)(2,1)S(1)}) all-reduce(bf16[1536]{0:T(1024)(128)(2,1)S(1)} %dynamic-update-slice, bf16[1536]{0:T(1024)(128)(2,1)S(1)} %dynamic-update-slice.1), channel_id=1, replica_groups=mesh['dp'=8,'tensor'=4] {'dp'}, use_global_device_ids=true, to_apply=%add | all-reduce | flops 3072 | bytes 12288
  1427.3 10.9 fusion.66
  1443.5 11.3 all-gather.12.cloned.1.call-done
  1460.2 28.9 %all-gather.14.cloned.1.call-done = bf16[1024,1536]{0,1:T(8,128)(2,1)} async-done(((bf16[1024,192]{0,1:T(8,128)(2,1)}), bf16[1024,1536]{0,1:T(8,128)(2,1)}) %all-gather.14.cloned.1.call-update) | async-done | bytes 3145744 | tf_op jit(solution)/shard_map/all_gather | solution.py:304
  (566 shorter events, 424.0 us)
Async XLA Ops:
  7.2 401.8 %copy-start = (bf16[1024,1536]{1,0:T(8,128)(2,1)S(1)}, bf16[1024,1536]{1,0:T(8,128)(2,1)}, u32[]{:S(2)}) copy-start(bf16[1024,1536]{1,0:T(8,128)(2,1)} %param.28) | copy-start | bytes 9437188
  7.2 8.0 copy-start.57
  7.2 386.3 %all-reduce.11.cloned.1.call-start = ((), (), s32[]{:S(2)}) async-start(), calls=%async_computation.7 | async-start | bytes 6291456 | tf_op jit(solution)/shard_map/psum | solution.py:165
  7.3 7.9 copy-start.5
  11.7 39.2 %copy-start.16 = (f32[1024,96]{0,1:T(8,128)}, f32[1024,96]{0,1:T(8,128)S(1)}, u32[]{:S(2)}) copy-start(f32[1024,96]{0,1:T(8,128)S(1)} %pad_maximum_fusion.2) | copy-start | bytes 1179652
  21.1 2.4 collective-permute-start
  25.9 19.1 %collective-permute-start.1 = (bf16[2,2,512,2,96]{2,4,3,0,1:T(8,128)(2,1)}, bf16[2,2,512,2,96]{2,4,3,0,1:T(8,128)(2,1)}, u32[]{:S(2)}, u32[]{:S(2)}) collective-permute-start(bf16[2,2,512,2,96]{2,4,3,0,1:T(8,128)(2,1)} %maximum_select_fusion.2), channel_id=1, source_target_pairs={{0,8},{4,12},{8,0},{12,4},{16,24},{20,28},{24,16},{28,20},{1,9},{5... | collective-permute-start | bytes 2359304 | tf_op jit(solution)/shard_map/ppermute | solution.py:19
  30.8 18.8 %copy-start.18 = (f32[1024,384]{0,1:T(8,128)}, f32[1024,384]{0,1:T(8,128)S(1)}, u32[]{:S(2)}) copy-start(f32[1024,384]{0,1:T(8,128)S(1)} %fusion.116) | copy-start | bytes 4718596
  48.4 35.0 %collective-permute-start.2 = (bf16[2,4,512,2,96]{2,4,3,0,1:T(8,128)(2,1)}, bf16[2,4,512,2,96]{2,4,3,0,1:T(8,128)(2,1)}, u32[]{:S(2)}, u32[]{:S(2)}) collective-permute-start(bf16[2,4,512,2,96]{2,4,3,0,1:T(8,128)(2,1)} %maximum_select_fusion.1), channel_id=1, source_target_pairs={{0,16},{4,20},{8,24},{12,28},{16,0},{20,4},{24,8},{28,12},{1,17},{... | collective-permute-start | bytes 4718600 | tf_op jit(solution)/shard_map/ppermute | solution.py:19
  186.0 74.3 %copy-start.54 = (bf16[512,192]{0,1:T(8,128)(2,1)S(1)}, bf16[512,192]{0,1:T(8,128)(2,1)}, u32[]{:S(2)}) copy-start(bf16[512,192]{0,1:T(8,128)(2,1)} %get-tuple-element.370) | copy-start | bytes 589828
  260.3 8.1 copy-start.70
  271.9 125.7 %copy-start.59 = (f32[1536]{0:T(1024)S(1)}, f32[1536]{0:T(1024)}, u32[]{:S(2)}) copy-start(f32[1536]{0:T(1024)} %param.25) | copy-start | bytes 18436
  271.9 276.3 %all-reduce.13.cloned.1.call-start = ((), (), s32[]{:S(2)}) async-start(), calls=%async_computation.8 | async-start | bytes 6291456 | tf_op jit(solution)/shard_map/psum | solution.py:186
  428.0 461.3 %reduce-scatter.14.cloned.1.call-start = ((), (), s32[]{:S(2)}) async-start(), calls=%async_computation.13 | async-start | bytes 2654208 | tf_op jit(solution)/shard_map/reduce_scatter | solution.py:273
  548.3 7.0 copy-start.7
  548.3 7.0 copy-start.9
  548.3 7.0 copy-start.15
  565.6 325.4 %reduce-scatter.8.cloned.1.call-start = ((), (), s32[]{:S(2)}) async-start(), calls=%async_computation.9 | async-start | bytes 2654208 | tf_op jit(solution)/shard_map/reduce_scatter | solution.py:270
  571.5 6.6 copy-start.2
  593.7 6.6 copy-start.2
  616.6 6.5 copy-start.2
  639.3 6.5 copy-start.2
  662.0 6.5 copy-start.2
  684.6 6.5 copy-start.2
  729.9 6.5 copy-start.2
  763.2 142.6 %reduce-scatter.16.cloned.1.call-start = ((), (), s32[]{:S(2)}) async-start(), calls=%async_computation.15 | async-start | bytes 7077888 | tf_op jit(solution)/shard_map/reduce_scatter | solution.py:275
  772.2 185.6 %reduce-scatter.18.cloned.1.call-start = ((), (), s32[]{:S(2)}) async-start(), calls=%async_computation.17 | async-start | bytes 7077888 | tf_op jit(solution)/shard_map/reduce_scatter | solution.py:276
  781.3 241.6 %reduce-scatter.20.cloned.1.call-start = ((), (), s32[]{:S(2)}) async-start(), calls=%async_computation.19 | async-start | bytes 7077888 | tf_op jit(solution)/shard_map/reduce_scatter | solution.py:277
  790.0 275.1 %reduce-scatter.12.cloned.1.call-start = ((), (), s32[]{:S(2)}) async-start(), calls=%async_computation.12 | async-start | bytes 1769472 | tf_op jit(solution)/shard_map/reduce_scatter | solution.py:272
  790.5 83.7 %slice-start = ((s8[8388608]{0:T(1024)(128)(4,1)}), s8[4194304]{0:T(1024)(128)(4,1)S(1)}, s32[]{:S(2)}) async-start(s8[8388608]{0:T(1024)(128)(4,1)} %bitcast.300), calls=%async_computation.22 | async-start | bytes 8388608
  793.9 80.3 %slice-start.1 = ((s8[8388608]{0:T(1024)(128)(4,1)}), s8[4194304]{0:T(1024)(128)(4,1)S(1)}, s32[]{:S(2)}) async-start(s8[8388608]{0:T(1024)(128)(4,1)} %bitcast.300), calls=%async_computation.23 | async-start | bytes 8388608
  793.9 38.8 %collective-permute-start.3 = (bf16[2,4,512,2,96]{2,4,3,1,0:T(8,128)(2,1)S(1)}, bf16[2,4,512,2,96]{2,4,3,1,0:T(8,128)(2,1)S(1)}, u32[]{:S(2)}, u32[]{:S(2)}) collective-permute-start(bf16[2,4,512,2,96]{2,4,3,1,0:T(8,128)(2,1)S(1)} %select_convert_fusion), channel_id=1, source_target_pairs={{0,16},{4,20},{8,24},{12,28},{16,0},{20,4},{24,8},{28,12},{1,17},{... | collective-permute-start | bytes 4718600 | tf_op jit(solution)/shard_map/ppermute | solution.py:19
  836.6 37.5 %copy-start.35 = (pred[1024,512]{0,1:T(8,128)(4,1)S(1)}, pred[1024,512]{0,1:T(8,128)(4,1)}, u32[]{:S(2)}) copy-start(pred[1024,512]{0,1:T(8,128)(4,1)} %copy-done.34) | copy-start | bytes 1572868
  836.7 37.5 %copy-start.46 = (bf16[1024,2,2,96]{0,3,2,1:T(8,128)(2,1)S(1)}, bf16[1024,2,2,96]{0,3,2,1:T(8,128)(2,1)}, u32[]{:S(2)}) copy-start(bf16[1024,2,2,96]{0,3,2,1:T(8,128)(2,1)} %get-tuple-element.726) | copy-start | bytes 2359300
  836.7 37.5 %copy-start.66 = (f32[2,2,1024]{2,1,0:T(2,128)S(1)}, f32[2,2,1024]{2,1,0:T(2,128)}, u32[]{:S(2)}) copy-start(f32[2,2,1024]{2,1,0:T(2,128)} %get-tuple-element.741) | copy-start | bytes 49156
  836.7 34.6 %collective-permute-start.4 = (bf16[2,2,512,2,96]{2,4,3,1,0:T(8,128)(2,1)S(1)}, bf16[2,2,512,2,96]{2,4,3,1,0:T(8,128)(2,1)S(1)}, u32[]{:S(2)}, u32[]{:S(2)}) collective-permute-start(bf16[2,2,512,2,96]{2,4,3,1,0:T(8,128)(2,1)S(1)} %select_convert_fusion.1), channel_id=1, source_target_pairs={{0,8},{4,12},{8,0},{12,4},{16,24},{20,28},{24,16},{28,20},{1,9},{5... | collective-permute-start | bytes 2359304 | tf_op jit(solution)/shard_map/ppermute | solution.py:19
  871.8 4.4 collective-permute-start.5
  880.8 226.4 %reduce-scatter.10.cloned.1.call-start = ((), (), s32[]{:S(2)}) async-start(), calls=%async_computation.11 | async-start | bytes 1769472 | tf_op jit(solution)/shard_map/reduce_scatter | solution.py:271
  889.2 244.3 %all-gather.8.cloned.1.call-start = ((), (), s32[]{:S(2)}) async-start(), calls=%async_computation.14 | async-start | bytes 1327104 | tf_op jit(solution)/shard_map/all_gather | solution.py:292
  891.0 269.3 %all-gather.6.cloned.1.call-start = ((), (), s32[]{:S(2)}) async-start(), calls=%async_computation.10 | async-start | bytes 1327104 | tf_op jit(solution)/shard_map/all_gather | solution.py:283
  892.7 491.2 %all-reduce.15.cloned.1.call-start = ((), (), s32[]{:S(2)}) async-start(), calls=%async_computation.21 | async-start | bytes 12582912 | tf_op jit(solution)/shard_map/psum | solution.py:175
  905.7 119.2 %copy-start.67 = (u32[32]{0:T(128)S(1)}, u32[32]{0:T(128)}, u32[]{:S(2)}) copy-start(u32[32]{0:T(128)} %constant.181) | copy-start | bytes 388
  905.7 532.5 %all-gather.10.cloned.1.call-start = ((), (), s32[]{:S(2)}) async-start(), calls=%async_computation.16 | async-start | bytes 3538944 | tf_op jit(solution)/shard_map/all_gather | solution.py:298
  907.9 547.0 %all-gather.12.cloned.1.call-start = ((), (), s32[]{:S(2)}) async-start(), calls=%async_computation.18 | async-start | bytes 3538944 | tf_op jit(solution)/shard_map/all_gather | solution.py:301
  959.7 529.4 %all-gather.14.cloned.1.call-start = ((), (), s32[]{:S(2)}) async-start(), calls=%async_computation.20 | async-start | bytes 3538944 | tf_op jit(solution)/shard_map/all_gather | solution.py:304
  1122.3 261.6 %copy-start.58 = (f32[1536]{0:T(1024)S(1)}, f32[1536]{0:T(1024)}, u32[]{:S(2)}) copy-start(f32[1536]{0:T(1024)} %param.20) | copy-start | bytes 18436
  1122.3 261.6 %copy-start.61 = (f32[1024]{0:T(1024)S(1)}, f32[1024]{0:T(1024)}, u32[]{:S(2)}) copy-start(f32[1024]{0:T(1024)} %copy-done.60) | copy-start | bytes 12292
  1384.0 43.3 %copy-start.64 = (f32[1024]{0:T(1024)S(1)}, f32[1024]{0:T(1024)}, u32[]{:S(2)}) copy-start(f32[1024]{0:T(1024)} %get-tuple-element.376) | copy-start | bytes 12292
  (118 other events, 438.6 us)
Sparse Core Ops, SparseCore 0:
  272.0 121.4 all-reduce.10
  428.1 120.0 all-reduce.12
  565.7 43.5 reduce-scatter.13
  763.3 47.0 reduce-scatter.7
  814.2 77.5 reduce-scatter.15
  896.0 61.7 reduce-scatter.17
  961.2 61.7 reduce-scatter.19
  1026.5 38.4 reduce-scatter.11
  1068.7 38.4 reduce-scatter.9
  1109.1 24.4 all-gather.7
  1136.2 24.0 all-gather.5
  1163.3 220.6 all-reduce.14
  1386.6 33.8 all-gather.9
  1422.4 32.4 all-gather.11
  1456.8 32.3 all-gather.13
where the time goes:
time: 1510 us; the launch traced here: 1500 us
  waiting for transfers between devices  820 us (54%)
  matrix products  379 us (25%)
  other arithmetic  152 us (10%)
  local copies, waits for them, and re-layouts  62.2 us (4%)
  blocking collectives  60.6 us (4%)
  between operations  16.4 us (1%)
    psum x1, waiting for transfers between devices, shards(): lax.psum(product(hidden, w_down).astype(jnp.bfloat16), 'tensor')  221 us
    psum x1, waiting for transfers between devices, shards(): lax.psum(product(attended_low, w_out).astype(jnp.bfloat16), 'tensor')  122 us
    psum x1, waiting for transfers between devices, shards(): lax.psum((input_grad(grad_gate_low, w_gate) + input_grad(grad_up_low, w_u...  120 us
    ppermute x6, waiting for transfers between devices, from_partner(): return lax.ppermute(value, axis, pairs)  103 us
    dot_general x17, matrix products, scores(): jnp.einsum('qkrd,nkd->krqn', queries, key_block, preferred_element_type=j...  78.6 us
    reduce_scatter x1, waiting for transfers between devices, shards(): lax.psum_scatter(grad_w_down, 'dp', scatter_dimension=1, tiled=True)  63.1 us
    dot_general x9, matrix products, output_step(): jnp.einsum('krqn,nkd->qkrd', weights, block[1], preferred_element_type=jn...  57.3 us
    dot_general x9, matrix products, back_step(): jnp.einsum('krqn,qkrd->nkd', chances.astype(jnp.bfloat16), grad_attended,...  50.1 us
  transfers between devices with their start and end apart: 21, of which 16 were waited for; matrix products, arithmetic and copies ran while one was open for 20% of the time, Pallas kernels for 0%

commit v1 on v0

v1 whole, which is shorter than its diff:
```python
import functools

import jax
import jax.numpy as jnp
from jax import lax
from jax.experimental import pallas as pl
from jax.experimental.pallas import tpu as pltpu
from jax.sharding import PartitionSpec as P

HEAD_DIM = 96
GROUP_DEVS = 8
PB = 512
CL = 512
EPSILON = 1e-05
ROTARY_BASE = 100000.0
LOG2E = 1.4426950408889634
NEG = -1e30
MESH = pl.DeviceIdType.MESH
VM = pltpu.VMEM
F32 = jnp.float32
BF16 = jnp.bfloat16
NT = (((1,), (1,)), ((), ()))


def dot(a, b):
    return jnp.dot(a, b, preferred_element_type=F32)


def dot_nt(a, b):
    return lax.dot_general(a, b, NT, preferred_element_type=F32)


def dot_tn(a, b):
    return lax.dot_general(a, b, (((0,), (0,)), ((), ())), preferred_element_type=F32)


def causal(s):
    key = lax.broadcasted_iota(jnp.int32, s.shape, 0)
    query = lax.broadcasted_iota(jnp.int32, s.shape, 1)
    return jnp.where(key <= query, s, NEG)


def greet(targets):
    barrier = pltpu.get_barrier_semaphore()
    for target in targets:
        pl.semaphore_signal(barrier, inc=1, device_id=target, device_id_type=MESH)
    pl.semaphore_wait(barrier, len(targets))


def remote(src, dst, send, recv, target):
    return pltpu.make_async_remote_copy(
        src_ref=src, dst_ref=dst, send_sem=send, recv_sem=recv, device_id=target, device_id_type=MESH
    )


def forward_kernel(
    nz, q_ref, kv_ref, bias_ref, att, kv_all, lse_ref, acc, top, total, ktok, gs, gr, zs, zr
):
    heads = q_ref.shape[0]
    kvh = heads // 2
    d, z = lax.axis_index("dp"), lax.axis_index("tensor")
    peer = lambda m: (jnp.bitwise_xor(d, m), z)
    greet(
        [peer(1), peer(2), peer(4), peer(6)]
        + [(d, lax.rem(z + 1, nz)), (d, lax.rem(z + nz - 1, nz))]
    )
    own = kv_ref.at[:, :, pl.ds(0, PB)]
    firsts = [remote(own, kv_all.at[m], gs.at[m], gr.at[m], peer(m)) for m in (1, 2, 4, 6)]
    for copy in firsts:
        copy.start()
    kv_all[0] = kv_ref[:, :, 0:PB]
    for h in range(kvh):
        ktok[8, h] = kv_ref[h, :, PB : PB + CL].T
        ktok[0, h] = kv_ref[h, :, 0:PB].T
    acc[...] = jnp.zeros_like(acc)
    top[...] = jnp.full_like(top, NEG)
    total[...] = jnp.zeros_like(total)

    def block(head, half, key, value, mask, bias):
        cols = pl.ds(half * PB, PB)
        s = dot(key, q_ref[head, :, cols])
        if mask:
            s = causal(s)
        if bias is not None:
            s = s + bias
        old = top[head, :, cols]
        new = jnp.maximum(old, jnp.max(s, axis=0, keepdims=True))
        p = jnp.exp2(s - new)
        shrink = jnp.exp2(old - new)
        total[head, :, cols] = total[head, :, cols] * shrink + jnp.sum(p, axis=0, keepdims=True)
        acc[head, :, cols] = acc[head, :, cols] * shrink + dot(value, p.astype(BF16))
        top[head, :, cols] = new

    def slot_step(slot, half, mask=False, bias=None):
        for head in range(heads):
            block(head, half, ktok[slot, head // 2], kv_all[slot, kvh + head // 2], mask, bias)

    slot_step(0, 1)
    for head in range(heads):
        block(head, 1, ktok[8, head // 2], kv_ref[kvh + head // 2, :, PB : PB + CL], True, None)

    def arrive(m):
        remote(kv_all.at[m], kv_all.at[m], gs.at[m], gr.at[m], peer(1)).wait_recv()

    def hand_on(m):
        return remote(kv_all.at[m], kv_all.at[m + 1], gs.at[m + 1], gr.at[m + 1], peer(1))

    def tail_slot(m, carry):
        arrive(m)

        @pl.when(lax.rem(m, 2) == 0)
        def _():
            hand_on(m).start()

        for h in range(kvh):
            ktok[m, h] = kv_all[m, h].T
        slot_step(m, 1)
        return carry

    tail_slot(1, 0)
    slot_step(0, 0, mask=True)
    slot_step(1, 0, bias=bias_ref[1])
    lax.fori_loop(2, GROUP_DEVS, tail_slot, 0)

    rows = heads * HEAD_DIM

    def finish(half):
        cols = pl.ds(half * PB, PB)
        for head in range(heads):
            att[z, pl.ds(head * HEAD_DIM, HEAD_DIM), cols] = (
                acc[head, :, cols] / total[head, :, cols]
            ).astype(BF16)
            lse_ref[head, :, cols] = top[head, :, cols] + jnp.log2(total[head, :, cols])

    def piece(index, half):
        return att.at[index, :, pl.ds(half * PB, PB)]

    def z_send(right, half, s):
        index, target = (z - s, z + 1) if right else (z + s, z - 1)
        there = (z - s >= 0) & (z < nz - 1) if right else (z + s < nz) & (z > 0)
        where = piece(index, half)
        return there, remote(
            where, where, zs.at[half, int(right), s], zr.at[half, int(right), s], (d, target)
        )

    def z_arrive(right, half, s):
        index = z - 1 - s if right else z + 1 + s
        there = index >= 0 if right else index < nz
        where = piece(index, half)

        @pl.when(there)
        def _():
            remote(
                where, where, zs.at[half, int(right), s], zr.at[half, int(right), s], (d, z)
            ).wait_recv()

    def z_start(half, s):
        for right in (True, False):
            if s > 0:
                z_arrive(right, half, s - 1)
            there, copy = z_send(right, half, s)
            pl.when(there)(copy.start)

    def z_finish(half):
        for right in (True, False):
            z_arrive(right, half, nz - 2)
            for s in range(nz - 1):
                there, copy = z_send(right, half, s)
                pl.when(there)(copy.wait_send)

    def prompt_slot(m, carry):
        slot_step(m, 0, bias=bias_ref[m])
        return carry

    finish(1)
    z_start(1, 0)
    lax.fori_loop(2, 6, prompt_slot, 0)
    z_start(1, 1)
    lax.fori_loop(6, GROUP_DEVS, prompt_slot, 0)
    finish(0)
    z_start(0, 0)
    for s in range(2, nz - 1):
        z_start(1, s)
    for s in range(1, nz - 1):
        z_start(0, s)
    z_finish(1)
    z_finish(0)
    for copy in firsts:
        copy.wait_send()
    for m in (2, 4, 6):
        hand_on(m).wait_send()


def forward_attention(nz, q, kv, bias):
    heads, tokens = q.shape[0], q.shape[2]
    kvh = heads // 2
    return pl.pallas_call(
        functools.partial(forward_kernel, nz),
        out_shape=(
            jax.ShapeDtypeStruct((nz, heads * HEAD_DIM, tokens), BF16),
            jax.ShapeDtypeStruct((GROUP_DEVS, 2 * kvh, HEAD_DIM, PB), BF16),
            jax.ShapeDtypeStruct((heads, 1, tokens), F32),
        ),
        in_specs=[
            pl.BlockSpec(memory_space=VM),
            pl.BlockSpec(memory_space=VM),
            pl.BlockSpec(memory_space=pltpu.SMEM),
        ],
        out_specs=(pl.BlockSpec(memory_space=VM),) * 3,
        scratch_shapes=[
            VM((heads, HEAD_DIM, tokens), F32),
            VM((heads, 1, tokens), F32),
            VM((heads, 1, tokens), F32),
            VM((GROUP_DEVS + 1, kvh, PB, HEAD_DIM), BF16),
            pltpu.SemaphoreType.DMA((GROUP_DEVS,)),
            pltpu.SemaphoreType.DMA((GROUP_DEVS,)),
            pltpu.SemaphoreType.DMA((2, 2, nz - 1)),
            pltpu.SemaphoreType.DMA((2, 2, nz - 1)),
        ],
        compiler_params=pltpu.CompilerParams(
            collective_id=0, has_side_effects=True, vmem_limit_bytes=48 << 20
        ),
        cost_estimate=pl.CostEstimate(
            flops=40_000_000_000, bytes_accessed=12_000_000, transcendentals=19_000_000
        ),
        name="forward_attention",
    )(q, kv, bias)


def backward_kernel(
    q_ref, kv_ref, kv_all, do_ref, bias_ref, lse_ref, inner_ref, dq, dkv, dkv_tail, ktok, vtok
):
    heads = q_ref.shape[0]
    kvh = heads // 2
    dq[...] = jnp.zeros_like(dq)

    def block(head, half, keyt, slot, mask, bias):
        h = head // 2
        cols = pl.ds(half * PB, PB)
        s = dot(ktok[slot, h], q_ref[head, :, cols])
        if mask:
            s = causal(s)
        shift = lse_ref[head, :, cols]
        if bias is not None:
            shift = shift - bias
        p = jnp.exp2(s - shift)
        dp = dot(vtok[slot, h], do_ref[head, :, cols])
        ds = (p * (dp - inner_ref[head, :, cols])).astype(BF16)
        dq[head, :, cols] += dot(keyt, ds)
        dv = dot_nt(do_ref[head, :, cols], p.astype(BF16))
        dk = dot_nt(q_ref[head, :, cols], ds)
        return dk, dv

    def total(parts):
        out = parts[0]
        for part in parts[1:]:
            out = out + part
        return out

    for h in range(kvh):
        ktok[1, h] = kv_ref[h, :, PB : PB + CL].T
        vtok[1, h] = kv_ref[kvh + h, :, PB : PB + CL].T
    for h in range(kvh):
        pairs = [
            block(2 * h + r, 1, kv_ref[h, :, PB : PB + CL], 1, True, None) for r in range(2)
        ]
        dkv_tail[h] = total([p[0] for p in pairs]) * (1.0 / LOG2E)
        dkv_tail[kvh + h] = total([p[1] for p in pairs])

    def slot_step(m, first):
        for h in range(kvh):
            ktok[0, h] = kv_all[m, h].T
            vtok[0, h] = kv_all[m, kvh + h].T
        for h in range(kvh):
            pairs = []
            for r in range(2):
                pairs.append(block(2 * h + r, 1, kv_all[m, h], 0, False, None))
                pairs.append(
                    block(2 * h + r, 0, kv_all[m, h], 0, first, None if first else bias_ref[m])
                )
            dkv[m, h] = (total([p[0] for p in pairs]) * (1.0 / LOG2E)).astype(BF16)
            dkv[m, kvh + h] = total([p[1] for p in pairs]).astype(BF16)

    slot_step(0, True)

    def step(m, carry):
        slot_step(m, False)
        return carry

    lax.fori_loop(1, GROUP_DEVS, step, 0)


def backward_attention(q, kv, kv_all, do, bias, lse, inner):
    heads, tokens = q.shape[0], q.shape[2]
    kvh = heads // 2
    return pl.pallas_call(
        backward_kernel,
        out_shape=(
            jax.ShapeDtypeStruct((heads, HEAD_DIM, tokens), F32),
            jax.ShapeDtypeStruct((GROUP_DEVS, 2 * kvh, HEAD_DIM, PB), BF16),
            jax.ShapeDtypeStruct((2 * kvh, HEAD_DIM, CL), F32),
        ),
        in_specs=[pl.BlockSpec(memory_space=VM)] * 4
        + [pl.BlockSpec(memory_space=pltpu.SMEM)]
        + [pl.BlockSpec(memory_space=VM)] * 2,
        out_specs=(pl.BlockSpec(memory_space=VM),) * 3,
        scratch_shapes=[VM((2, kvh, PB, HEAD_DIM), BF16), VM((2, kvh, PB, HEAD_DIM), BF16)],
        compiler_params=pltpu.CompilerParams(vmem_limit_bytes=48 << 20),
        cost_estimate=pl.CostEstimate(
            flops=60_000_000_000, bytes_accessed=12_000_000, transcendentals=19_000_000
        ),
        name="backward_attention",
    )(q, kv, kv_all, do, bias, lse, inner)


def keys_home_kernel(part, out, near, far, ns, nr, fs, fr):
    d, z = lax.axis_index("dp"), lax.axis_index("tensor")
    peer = lambda m: (jnp.bitwise_xor(d, m), z)
    greet([peer(1), peer(2), peer(4), peer(6)])
    order = (2, 4, 6, 0)
    nears = [
        remote(part.at[m + 1], near.at[m // 2], ns.at[m // 2], nr.at[m // 2], peer(1))
        for m in order
    ]
    for copy in nears:
        copy.start()
    fars = []
    for i, m in enumerate(order):
        nears[i].wait_recv()
        merged = part[m].astype(F32) + near[m // 2].astype(F32)
        if m == 0:
            out[...] = merged
        else:
            near[m // 2] = merged.astype(BF16)
            copy = remote(near.at[m // 2], far.at[m // 2], fs.at[m // 2], fr.at[m // 2], peer(m))
            copy.start()
            fars.append((copy, m))
    for copy, m in fars:
        copy.wait_recv()
        out[...] += far[m // 2].astype(F32)
    for copy in nears:
        copy.wait_send()
    for copy, _ in fars:
        copy.wait_send()


def keys_home(part):
    shape = part.shape[1:]
    return pl.pallas_call(
        keys_home_kernel,
        out_shape=jax.ShapeDtypeStruct(shape, F32),
        in_specs=[pl.BlockSpec(memory_space=VM)],
        out_specs=pl.BlockSpec(memory_space=VM),
        scratch_shapes=[VM((4,) + shape, BF16), VM((4,) + shape, BF16)]
        + [pltpu.SemaphoreType.DMA((4,))] * 4,
        compiler_params=pltpu.CompilerParams(
            collective_id=1, has_side_effects=True, vmem_limit_bytes=24 << 20
        ),
        name="keys_home",
    )(part)


def line_sum_kernel(nz, chunk, part, out, held, rs, rr, bs, br):
    d, z = lax.axis_index("dp"), lax.axis_index("tensor")
    greet([(d, lax.rem(z + 1, nz)), (d, lax.rem(z + nz - 1, nz))])
    half = part.shape[0] // 2
    count = half // chunk
    last = nz - 1

    def step(s, carry):
        for way in range(2):
            place = z if way == 0 else last - z
            onward = z + 1 if way == 0 else z - 1
            back = z - 1 if way == 0 else z + 1

            def rows(c):
                return pl.ds(pl.multiple_of(way * half + c * chunk, chunk), chunk)

            def forth(c):
                return remote(
                    held.at[rows(c)], held.at[rows(c)], rs.at[way, c], rr.at[way, c], (d, onward)
                )

            def home(c):
                return remote(
                    out.at[rows(c)], out.at[rows(c)], bs.at[way, c], br.at[way, c], (d, back)
                )

            c = s - place
            live = (c >= 0) & (c < count)

            @pl.when(live & (place == 0))
            def _():
                remote(
                    part.at[rows(c)], held.at[rows(c)], rs.at[way, c], rr.at[way, c], (d, onward)
                ).start()

            @pl.when(live & (place > 0) & (place < last))
            def _():
                forth(c).wait_recv()
                held[rows(c)] = (held[rows(c)].astype(F32) + part[rows(c)].astype(F32)).astype(BF16)
                forth(c).start()

            @pl.when(live & (place == last))
            def _():
                forth(c).wait_recv()
                out[rows(c)] = (held[rows(c)].astype(F32) + part[rows(c)].astype(F32)).astype(BF16)
                home(c).start()

            b = s - (2 * last - place)
            back_live = (b >= 0) & (b < count) & (place < last)

            @pl.when(back_live)
            def _():
                home(b).wait_recv()

            @pl.when(back_live & (place > 0))
            def _():
                home(b).start()

        return carry

    lax.fori_loop(0, count + 2 * last, step, 0)

    def drain(c, carry):
        for way in range(2):
            place = z if way == 0 else last - z
            where = pl.ds(pl.multiple_of(way * half + c * chunk, chunk), chunk)

            @pl.when(place < last)
            def _():
                remote(
                    held.at[where], held.at[where], rs.at[way, c], rr.at[way, c], (d, z)
                ).wait_send()

            @pl.when(place > 0)
            def _():
                remote(out.at[where], out.at[where], bs.at[way, c], br.at[way, c], (d, z)).wait_send()

        return carry

    lax.fori_loop(0, count, drain, 0)


def line_sum(nz, part, ident, chunk=16):
    count = part.shape[0] // 2 // chunk
    return pl.pallas_call(
        functools.partial(line_sum_kernel, nz, chunk),
        out_shape=jax.ShapeDtypeStruct(part.shape, BF16),
        in_specs=[pl.BlockSpec(memory_space=VM)],
        out_specs=pl.BlockSpec(memory_space=VM),
        scratch_shapes=[VM(part.shape, BF16)] + [pltpu.SemaphoreType.DMA((2, count))] * 4,
        compiler_params=pltpu.CompilerParams(
            collective_id=ident, has_side_effects=True, vmem_limit_bytes=24 << 20
        ),
        name="line_sum",
    )(part)


def rms_inverse(inputs):
    return lax.rsqrt(jnp.mean(inputs * inputs, axis=-1, keepdims=True) + EPSILON)


def norm_back(inputs, inverse, gain, upstream):
    inner = upstream * gain
    through = inverse * inner - inputs * inverse**3 * jnp.mean(
        inner * inputs, axis=-1, keepdims=True
    )
    return (through, jnp.sum(upstream * inputs * inverse, axis=0))


def rotate(u, cosine, sine):
    half = HEAD_DIM // 2
    lower, upper = u[:, :half], u[:, half:]
    return jnp.concatenate(
        [lower * cosine - upper * sine, upper * cosine + lower * sine], axis=1
    )


def everywhere(share, axis_size, dimension):
    summed = lax.psum_scatter(share.astype(BF16), "dp", scatter_dimension=dimension, tiled=True)
    return lax.all_gather(summed, "dp", axis=dimension, tiled=True).astype(F32)


def shards(
    nz,
    tokens,
    block_order,
    attn_gain,
    w_query,
    w_key,
    w_value,
    w_out,
    mlp_gain,
    w_gate,
    w_up,
    w_down,
    cotangent,
):
    device = lax.axis_index("dp")
    n_dp = lax.axis_size("dp")
    member = device % GROUP_DEVS
    order_row = lax.dynamic_index_in_dim(block_order, device // GROUP_DEVS, 0, keepdims=False)
    by_slot = order_row[jnp.bitwise_xor(jnp.arange(GROUP_DEVS), member)]
    own_block = by_slot[0]
    bias = jnp.where(by_slot <= own_block, 0.0, NEG).astype(F32)
    offsets = jnp.arange(PB, dtype=jnp.int32)
    places = jnp.concatenate([own_block * PB + offsets, GROUP_DEVS * PB + offsets])
    halfway = HEAD_DIM // 2
    frequency = ROTARY_BASE ** (-(jnp.arange(halfway, dtype=F32) * 2.0) / HEAD_DIM)
    angle = frequency[:, None] * places.astype(F32)[None, :]
    cosine, sine = jnp.cos(angle)[None], jnp.sin(angle)[None]

    rows = w_out.shape[0] // n_dp
    w_piece = lax.dynamic_slice_in_dim(w_out, device * rows, rows, 0)
    w_out_all = lax.all_gather(w_piece, ("tensor", "dp"), axis=0, tiled=True)

    count = tokens.shape[0]
    factor = HEAD_DIM ** (-0.5)
    inputs = tokens.astype(F32)
    inverse_one = rms_inverse(inputs)
    normed = (inputs * inverse_one * attn_gain).astype(BF16)

    def project(weight):
        out = lax.dot_general(
            weight, normed, (((0,), (1,)), ((), ())), preferred_element_type=F32
        )
        return out.reshape(-1, HEAD_DIM, count)

    queries = (rotate(project(w_query), cosine, sine) * (factor * LOG2E)).astype(BF16)
    keys = rotate(project(w_key), cosine, sine).astype(BF16)
    values = project(w_value).astype(BF16)
    kv = jnp.concatenate([keys, values], axis=0)
    heads, kvh = queries.shape[0], keys.shape[0]

    att_all, kv_all, lse = forward_attention(nz, queries, kv, bias)
    attended = lax.dynamic_index_in_dim(att_all, lax.axis_index("tensor"), 0, keepdims=False)
    attention = dot_tn(att_all.reshape(-1, count), w_out_all)
    middle = inputs + attention
    inverse_two = rms_inverse(middle)
    normed_two = (middle * inverse_two * mlp_gain).astype(BF16)
    gate_pre = dot(normed_two, w_gate)
    up_pre = dot(normed_two, w_up)
    sigmoid_gate = jax.nn.sigmoid(gate_pre)
    hidden = (gate_pre * sigmoid_gate * up_pre).astype(BF16)
    grad_hidden = dot_nt(cotangent, w_down)
    grad_gate_low = (
        grad_hidden * up_pre * sigmoid_gate * (1.0 + gate_pre * (1.0 - sigmoid_gate))
    ).astype(BF16)
    grad_up_low = (grad_hidden * gate_pre * sigmoid_gate).astype(BF16)
    partial_two = (dot_nt(grad_gate_low, w_gate) + dot_nt(grad_up_low, w_up)).astype(BF16)
    grad_normed_two = line_sum(nz, partial_two, 2).astype(F32)
    feed_out = lax.psum(dot(hidden, w_down).astype(BF16), "tensor").astype(F32)
    activations = (middle + feed_out).astype(BF16)
    grad_w_gate_up = jnp.concatenate(
        [dot_tn(normed_two, grad_gate_low), dot_tn(normed_two, grad_up_low)], axis=1
    )
    grad_w_down = dot_tn(hidden, cotangent)
    upstream = cotangent.astype(F32)
    through_two, grad_gain_two = norm_back(middle, inverse_two, mlp_gain, grad_normed_two)
    grad_middle = upstream + through_two
    grad_attention = grad_middle.astype(BF16)
    grad_w_out = dot(attended, grad_attention)
    grad_attended = dot_nt(w_out, grad_attention).astype(BF16)
    row_inner = jnp.sum(
        (grad_attended.astype(F32) * attended.astype(F32)).reshape(heads, HEAD_DIM, count),
        axis=1,
        keepdims=True,
    )
    grad_queries, grad_kv_part, grad_kv_tail = backward_attention(
        queries,
        kv,
        kv_all,
        grad_attended.reshape(heads, HEAD_DIM, count),
        bias,
        lse,
        row_inner,
    )
    grad_kv_prompt = keys_home(grad_kv_part)
    grad_kv = jnp.concatenate([grad_kv_prompt, grad_kv_tail], axis=2)
    grad_query_low = rotate(grad_queries * factor, cosine, -sine).astype(BF16).reshape(-1, count)
    grad_key_low = rotate(grad_kv[:kvh], cosine, -sine).astype(BF16).reshape(-1, count)
    grad_value_low = grad_kv[kvh:].astype(BF16).reshape(-1, count)

    def back(grad, weight):
        return lax.dot_general(grad, weight, (((0,), (1,)), ((), ())), preferred_element_type=F32)

    partial_one = (
        back(grad_query_low, w_query) + back(grad_key_low, w_key) + back(grad_value_low, w_value)
    ).astype(BF16)
    grad_normed = line_sum(nz, partial_one, 3).astype(F32)
    grads_low = jnp.concatenate([grad_query_low, grad_key_low, grad_value_low], axis=0)
    grad_w_qkv = dot_tn(normed, grads_low.T)
    through_one, grad_gain_one = norm_back(inputs, inverse_one, attn_gain, grad_normed)
    grad_tokens = (grad_middle + through_one).astype(BF16)
    gains = lax.psum(jnp.stack([grad_gain_one, grad_gain_two]), "dp")
    gate_up = everywhere(grad_w_gate_up, n_dp, 0)
    down = everywhere(grad_w_down, n_dp, 0)
    out = everywhere(grad_w_out, n_dp, 0)
    qkv = everywhere(grad_w_qkv, n_dp, 0)
    nq, nk = w_query.shape[1], w_key.shape[1]
    nf = w_gate.shape[1]
    return (
        activations,
        grad_tokens,
        gains[0],
        qkv[:, :nq],
        qkv[:, nq : nq + nk],
        qkv[:, nq + nk :],
        out,
        gains[1],
        gate_up[:, :nf],
        gate_up[:, nf:],
        down,
    )


def solution(mesh):
    in_specs = (
        P("dp", None),
        P(),
        P(),
        P(None, "tensor"),
        P(None, "tensor"),
        P(None, "tensor"),
        P("tensor", None),
        P(),
        P(None, "tensor"),
        P(None, "tensor"),
        P("tensor", None),
        P("dp", None),
    )
    out_specs = (
        P("dp", None),
        P("dp", None),
        P(),
        P(None, "tensor"),
        P(None, "tensor"),
        P(None, "tensor"),
        P("tensor", None),
        P(),
        P(None, "tensor"),
        P(None, "tensor"),
        P("tensor", None),
    )
    return jax.shard_map(
        functools.partial(shards, mesh.shape["tensor"]),
        mesh=mesh,
        in_specs=in_specs,
        out_specs=out_specs,
        check_vma=False,
    )
```

time: 1510 us -> 789 us (0.52)
  waiting for transfers between devices: 820 us -> 85.8 us
  Pallas kernels: 0 us -> 470 us
  matrix products: 379 us -> 78.9 us
  other arithmetic: 152 us -> 38.7 us
  blocking collectives: 60.6 us -> 39.6 us
  local copies, waits for them, and re-layouts: 62.2 us -> 46.1 us
    pallas_call x0 -> x5, Pallas kernels: none -> 470 us  [the longest x2 279 us: line_sum(): pl.pallas_call(functools.partial(line_sum_kernel, nz, chunk), out_shape=j...]
    psum x3 -> x1, waiting for transfers between devices: 463 us -> 0.02 us  [shards(): feed_out = lax.psum(dot(hidden, w_down).astype(BF16), 'tensor').astype(F32)]
    dot_general x83 -> x19, matrix products: 379 us -> 78.9 us  [the longest x5 30.6 us: dot_tn(): lax.dot_general(a, b, (((0,), (0,)), ((), ())), preferred_element_type=F32)]
    ppermute x6 -> x0, waiting for transfers between devices: 103 us -> none  [from_partner(): return lax.ppermute(value, axis, pairs)]
    reduce_scatter x7 -> x4, waiting for transfers between devices: 178 us -> 84.3 us  [everywhere(): lax.psum_scatter(share.astype(BF16), 'dp', scatter_dimension=dimension, t...]
    all_gather x5, waiting for transfers between devices: 75.5 us -> 0.01 us  [the longest x4 0.01 us: everywhere(): return lax.all_gather(summed, 'dp', axis=dimension, tiled=True).astype(F32)]
    reduce_sum x10 -> x1, other arithmetic: 44 us -> 1.53 us  [shards(): jnp.sum((grad_attended.astype(F32) * attended.astype(F32)).reshape(heads,...]
    psum x0 -> x1, blocking collectives: none -> 39.6 us  [shards(): gains = lax.psum(jnp.stack([grad_gain_one, grad_gain_two]), 'dp')]
  transfers between devices with their start and end apart: 21 -> 10, of which waited for: 16 -> 2; matrix products, arithmetic and copies ran while one was open for 20% -> 13% of each run, Pallas kernels for 0% -> 61%
where the time goes in v1:
time: 789 us; the launch traced here: 775 us
  Pallas kernels  470 us (60%)
  waiting for transfers between devices  85.8 us (11%)
  matrix products  78.9 us (10%)
  local copies, waits for them, and re-layouts  46.1 us (6%)
  blocking collectives  39.6 us (5%)
  other arithmetic  38.7 us (5%)
  between operations  15.2 us (2%)
    pallas_call x2, Pallas kernels, line_sum(): pl.pallas_call(functools.partial(line_sum_kernel, nz, chunk), out_shape=j...  279 us
    pallas_call x1, Pallas kernels, forward_attention(): pl.pallas_call(functools.partial(forward_kernel, nz), out_shape=(jax.Shap...  95.7 us
    reduce_scatter x4, waiting for transfers between devices, everywhere(): lax.psum_scatter(share.astype(BF16), 'dp', scatter_dimension=dimension, t...  84.3 us
    pallas_call x1, Pallas kernels, backward_attention(): pl.pallas_call(backward_kernel, out_shape=(jax.ShapeDtypeStruct((heads, H...  58.4 us
    psum x1, blocking collectives, shards(): gains = lax.psum(jnp.stack([grad_gain_one, grad_gain_two]), 'dp')  39.6 us
    pallas_call x1, Pallas kernels, keys_home(): pl.pallas_call(keys_home_kernel, out_shape=jax.ShapeDtypeStruct(shape, F3...  36.3 us
    dot_general x5, matrix products, dot_tn(): lax.dot_general(a, b, (((0,), (0,)), ((), ())), preferred_element_type=F32)  30.6 us
    unnamed x83, local copies, waits for them, and re-layouts  28.1 us
  transfers between devices with their start and end apart: 10, of which 2 were waited for; matrix products, arithmetic and copies ran while one was open for 13% of the time, Pallas kernels for 61%

profile of v1, /device:TPU:25, one launch (start us, length us, event | category | flops | bytes accessed | tf_op | source)
XLA Modules:
  0.0 774.6 jit_solution(17221250589255975044)
XLA Ops:
  7.3 1.7 constant_dynamic-slice_fusion
  9.1 1.3 gather_fusion
  10.5 2.7 fusion.11
  13.8 1.4 fusion.35
  15.3 2.9 fusion.43
  20.7 1.3 convolution_convert_fusion.6
  22.1 95.7 %forward_attention.1 = (bf16[4,384,1024]{2,1,0:T(8,128)(2,1)S(1)}, bf16[8,4,96,512]{3,2,1,0:T(8,128)(2,1)}, f32[4,1,1024]{2,1,0:T(1,128)S(1)}) custom-call(bf16[4,96,1024]{2,1,0:T(8,128)(2,1)S(1)} %fusion.18.q_ref, bf16[4,96,1024]{2,1,0:T(8,128)(2,1)S(1)} %pad_maximum_fusion.2.kv_ref, f32[8]{0:T(128)S(1)} %compare_select_fusion.1.bias_ref), custom_call_target="tpu_custom_call" | custom-call | flops 40000000000 | bytes 12000000 | tf_op jit(solution)/shard_map/forward_attention/pallas_call | solution.py:197
  118.8 1.7 copy-done.7
  120.4 9.3 %multiply_reduce_fusion = (f32[1024]{0:T(1024)S(1)}, f32[1024,1536]{1,0:T(8,128)S(1)}) fusion(bf16[1536,1024]{1,0:T(8,128)(2,1)} %bitcast.59, bf16[1536,1536]{1,0:T(8,128)(2,1)} %all-gather.6.cloned.1.call-done, bf16[1024,1536]{1,0:T(8,128)(2,1)} %param.12), kind=kOutput, calls=%fused_computation.33 | convolution fusion | flops 4838128640 | bytes 17305600 | tf_op jit(solution)/shard_map/dot_general | solution.py:34
  130.4 3.5 copy-done.31
  134.0 3.4 fusion.47
  137.4 3.4 fusion.48
  140.9 6.8 multiply_convert_fusion.1
  147.7 1.3 copy-done.37
  149.0 4.8 convolution_convert_fusion.3
  153.8 1.8 copy-done.32
  155.7 5.2 fusion.49
  160.9 3.8 add_convert_fusion.1.part
  164.7 179.1 %line_sum.2 = bf16[1024,1536]{1,0:T(8,128)(2,1)S(1)} custom-call(bf16[1024,1536]{1,0:T(8,128)(2,1)S(1)} %add_convert_fusion.1.part), custom_call_target="tpu_custom_call" | custom-call | tf_op jit(solution)/shard_map/line_sum/pallas_call | solution.py:447
  343.7 2.4 fusion.10
  346.2 8.0 %fusion.7 = (f32[1024,1536]{1,0:T(8,128)}, bf16[1024,1536]{1,0:T(8,128)(2,1)}) fusion(bf16[1024,1536]{1,0:T(8,128)(2,1)S(1)} %line_sum.2, f32[1024,1536]{1,0:T(8,128)} %copy-done.8, bf16[1024,1536]{1,0:T(8,128)(2,1)} %param.23, f32[1024]{0:T(1024)S(1)} %broadcast_multiply_fusion.2, f32[1024]{0:T(1024)S(1)} %get-tuple-element.84, f32[1536]{0:T(1024)S(1)} %copy-done.25, ...), kind=kLoop, calls=%fused_computation.17 | loop fusion | flops 17301504 | bytes 25184256 | tf_op jit(solution)/shard_map/add | solution.py:561
  354.2 5.6 convolution_convert_fusion.5
  359.8 6.8 convolution_convert_fusion
  366.7 6.0 convert_multiply_fusion.8
  372.7 1.5 reduce_sum.66
  374.2 58.4 %backward_attention.1 = (f32[4,96,1024]{2,1,0:T(8,128)S(1)}, bf16[8,4,96,512]{3,2,1,0:T(8,128)(2,1)}, f32[4,96,512]{2,1,0:T(8,128)S(1)}) custom-call(bf16[4,96,1024]{2,1,0:T(8,128)(2,1)S(1)} %copy-done.6, bf16[4,96,1024]{2,1,0:T(8,128)(2,1)S(1)} %copy-done.4, bf16[8,4,96,512]{3,2,1,0:T(8,128)(2,1)} %get-tuple-element.18.kv_all, ...), custom_call_target="tpu_custom_call" | custom-call | flops 60000002048 | bytes 12000000 | tf_op jit(solution)/shard_map/backward_attention/pallas_call | solution.py:296
  432.7 1.9 copy-done.2
  434.6 36.3 %keys_home.1 = f32[4,96,512]{2,1,0:T(8,128)S(1)} custom-call(bf16[8,4,96,512]{3,2,1,0:T(8,128)(2,1)S(1)} %copy-done.2), custom_call_target="tpu_custom_call" | custom-call | tf_op jit(solution)/shard_map/keys_home/pallas_call | solution.py:349
  471.6 1.4 copy-done.10
  473.0 4.5 convolution_convert_fusion.4
  477.7 6.2 convolution_convert_fusion.1
  483.9 3.9 convolution_convert_fusion.2
  487.8 3.1 pad_maximum_fusion
  490.9 8.6 %copy.34 = bf16[1536,2048]{1,0:T(8,128)(2,1)} copy(bf16[1536,2048]{0,1:T(8,128)(2,1)} %pad_maximum_fusion) | data formatting | bytes 12582912
  501.1 18.4 %reduce-scatter.7.cloned.1.call-done = bf16[192,768]{1,0:T(8,128)(2,1)} async-done(((bf16[1536,768]{1,0:T(8,128)(2,1)}), bf16[192,768]{1,0:T(8,128)(2,1)}) %reduce-scatter.7.cloned.1.call-update) | async-done | bytes 294928 | tf_op jit(solution)/shard_map/reduce_scatter | solution.py:481
  519.6 65.9 %reduce-scatter.13.cloned.1.call-done = bf16[192,2048]{1,0:T(8,128)(2,1)} async-done(((bf16[1536,2048]{1,0:T(8,128)(2,1)}), bf16[192,2048]{1,0:T(8,128)(2,1)}) %reduce-scatter.13.cloned.1.call-update) | async-done | bytes 786448 | tf_op jit(solution)/shard_map/reduce_scatter | solution.py:481
  586.8 1.9 fusion.50
  589.8 100.4 %line_sum.3 = bf16[1024,1536]{1,0:T(8,128)(2,1)S(1)} custom-call(bf16[1024,1536]{1,0:T(8,128)(2,1)S(1)} %add_convert_fusion.part), custom_call_target="tpu_custom_call" | custom-call | tf_op jit(solution)/shard_map/line_sum/pallas_call | solution.py:447
  690.2 2.6 fusion.17
  692.8 39.6 %psum.15 = f32[2,1536]{1,0:T(2,128)S(1)} all-reduce(f32[2,1536]{1,0:T(2,128)S(1)} %pad_maximum_fusion.5), channel_id=1, replica_groups=mesh['dp'=8,'tensor'=4] {'dp'}, use_global_device_ids=true, to_apply=%region_8.9 | all-reduce | flops 3072 | bytes 24576 | tf_op jit(solution)/shard_map/psum | solution.py:596
  733.1 5.8 fusion.5
  738.9 3.0 convert_element_type.143
  741.9 5.5 convert_element_type.146
  747.4 3.4 fusion.46
  750.8 3.0 copy.32
  753.8 2.9 copy.33
  756.7 1.6 slice.85
  758.2 9.3 %fusion.45 = (f32[1536,1024]{1,0:T(8,128)}, f32[1536,1024]{1,0:T(8,128)}) fusion(bf16[1536,2048]{1,0:T(8,128)(2,1)} %all-gather.12.cloned.1.call-done), kind=kLoop, calls=%fused_computation.104 | loop fusion | bytes 25165824 | tf_op jit(solution)/shard_map/slice | solution.py:613
  (132 shorter events, 10.7 us)
Async XLA Ops:
  7.2 133.7 %copy-start = (bf16[1024,1536]{1,0:T(8,128)(2,1)S(1)}, bf16[1024,1536]{1,0:T(8,128)(2,1)}, u32[]{:S(2)}) copy-start(bf16[1024,1536]{1,0:T(8,128)(2,1)} %param.22) | copy-start | bytes 9437188
  7.2 8.1 %copy-start.28 = (f32[1536]{0:T(1024)S(1)}, f32[1536]{0:T(1024)}, u32[]{:S(2)}) copy-start(f32[1536]{0:T(1024)} %param.14) | copy-start | bytes 18436
  7.2 113.2 %all-gather.6.cloned.1.call-start = ((), (), s32[]{:S(2)}) async-start(), calls=%async_computation.4 | async-start | bytes 4866048 | tf_op jit(solution)/shard_map/all_gather | solution.py:516
  9.0 337.1 %all-reduce.2.cloned.1.call-start = ((), (), s32[]{:S(2)}) async-start(), calls=%async_computation.5 | async-start | bytes 6291456 | tf_op jit(solution)/shard_map/psum | solution.py:553
  10.5 4.8 copy-start.9
  13.8 6.8 copy-start.26
  15.3 5.3 copy-start.13
  19.3 2.8 copy-start.5
  19.3 1.4 copy-start.21
  118.8 1.7 copy-start.7
  120.4 9.4 %copy-start.25 = (f32[1536]{0:T(1024)S(1)}, f32[1536]{0:T(1024)}, u32[]{:S(2)}) copy-start(f32[1536]{0:T(1024)} %param.19) | copy-start | bytes 18436
  129.8 7.6 copy-start.8
  129.8 4.1 copy-start.31
  134.0 3.4 copy-start.17
  134.0 3.4 copy-start.33
  137.4 3.5 copy-start.15
  147.7 1.3 copy-start.37
  153.8 1.9 copy-start.32
  153.8 345.8 %reduce-scatter.9.cloned.1.call-start = ((), (), s32[]{:S(2)}) async-start(), calls=%async_computation.8 | async-start | bytes 1327104 | tf_op jit(solution)/shard_map/reduce_scatter | solution.py:481
  155.7 5.2 copy-start.34
  155.7 5.2 copy-start.36
  155.7 188.1 %slice-start = ((s8[6291456]{0:T(1024)(128)(4,1)}), s8[4194304]{0:T(1024)(128)(4,1)S(1)}, s32[]{:S(2)}) async-start(s8[6291456]{0:T(1024)(128)(4,1)} %bitcast.61), calls=%async_computation.14 | async-start | bytes 8388608
  160.9 182.9 %slice-start.1 = ((s8[6291456]{0:T(1024)(128)(4,1)}), s8[2097152]{0:T(1024)(128)(4,1)S(1)}, s32[]{:S(2)}) async-start(s8[6291456]{0:T(1024)(128)(4,1)} %bitcast.61), calls=%async_computation.15 | async-start | bytes 4194304
  354.2 5.6 copy-start.16
  359.8 140.6 %reduce-scatter.11.cloned.1.call-start = ((), (), s32[]{:S(2)}) async-start(), calls=%async_computation.11 | async-start | bytes 3538944 | tf_op jit(solution)/shard_map/reduce_scatter | solution.py:481
  366.6 7.6 copy-start.4
  366.6 7.6 copy-start.6
  366.7 152.9 %reduce-scatter.7.cloned.1.call-start = ((), (), s32[]{:S(2)}) async-start(), calls=%async_computation.6 | async-start | bytes 2654208 | tf_op jit(solution)/shard_map/reduce_scatter | solution.py:481
  432.7 1.9 copy-start.2
  434.6 36.3 %copy-start.14 = (f32[48,1024]{1,0:T(8,128)S(1)}, f32[48,1024]{1,0:T(8,128)}, u32[]{:S(2)}) copy-start(f32[48,1024]{1,0:T(8,128)} %copy-done.13) | copy-start | bytes 589828
  434.6 36.3 %copy-start.19 = (f32[48,1024]{1,0:T(8,128)S(1)}, f32[48,1024]{1,0:T(8,128)}, u32[]{:S(2)}) copy-start(f32[48,1024]{1,0:T(8,128)} %get-tuple-element.79) | copy-start | bytes 589828
  471.1 1.9 copy-start.10
  471.1 1.9 copy-start.27
  471.1 1.9 copy-start.29
  477.5 108.0 %reduce-scatter.13.cloned.1.call-start = ((), (), s32[]{:S(2)}) async-start(), calls=%async_computation.13 | async-start | bytes 7077888 | tf_op jit(solution)/shard_map/reduce_scatter | solution.py:481
  477.7 6.2 copy-start.18
  477.7 6.2 copy-start.35
  499.5 86.0 %copy-start.24 = (bf16[1536,192]{0,1:T(8,128)(2,1)S(1)}, bf16[1536,192]{0,1:T(8,128)(2,1)}, u32[]{:S(2)}) copy-start(bf16[1536,192]{0,1:T(8,128)(2,1)} %param.16) | copy-start | bytes 1769476
  499.5 239.4 %all-gather.10.cloned.1.call-start = ((), (), s32[]{:S(2)}) async-start(), calls=%async_computation.9 | async-start | bytes 1327104 | tf_op jit(solution)/shard_map/all_gather | solution.py:482
  500.3 241.6 %all-gather.14.cloned.1.call-start = ((), (), s32[]{:S(2)}) async-start(), calls=%async_computation.12 | async-start | bytes 3538944 | tf_op jit(solution)/shard_map/all_gather | solution.py:482
  501.0 246.3 %all-gather.8.cloned.1.call-start = ((), (), s32[]{:S(2)}) async-start(), calls=%async_computation.7 | async-start | bytes 2654208 | tf_op jit(solution)/shard_map/all_gather | solution.py:482
  519.6 238.7 %all-gather.12.cloned.1.call-start = ((), (), s32[]{:S(2)}) async-start(), calls=%async_computation.10 | async-start | bytes 7077888 | tf_op jit(solution)/shard_map/all_gather | solution.py:482
  585.5 1.3 copy-start.20
  586.8 1.9 copy-start.22
  589.7 100.4 %copy-start.11 = (bf16[1024,1536]{1,0:T(8,128)(2,1)S(1)}, bf16[1024,1536]{1,0:T(8,128)(2,1)}, u32[]{:S(2)}) copy-start(bf16[1024,1536]{1,0:T(8,128)(2,1)} %param.12) | copy-start | bytes 9437188
  690.2 42.9 %copy-start.30 = (f32[1024]{0:T(1024)S(1)}, f32[1024]{0:T(1024)}, u32[]{:S(2)}) copy-start(f32[1024]{0:T(1024)} %get-tuple-element.82) | copy-start | bytes 12292
  750.8 5.9 copy-start.12
  758.2 9.3 %copy-start.1 = (bf16[1024,1536]{1,0:T(8,128)(2,1)S(1)}, bf16[1024,1536]{1,0:T(8,128)(2,1)}, u32[]{:S(2)}) copy-start(bf16[1024,1536]{1,0:T(8,128)(2,1)} %param.22) | copy-start | bytes 9437188
  (2 other events, 2.0 us)
Sparse Core Ops, SparseCore 0:
  11.5 69.4 all-gather.5
  153.9 169.4 all-reduce.1
  359.9 46.5 reduce-scatter.8
  410.1 50.9 reduce-scatter.10
  477.6 41.8 reduce-scatter.6
  523.7 61.7 reduce-scatter.12
  587.4 24.4 all-gather.9
  613.7 32.2 all-gather.13
  648.0 29.0 all-gather.7
  678.8 45.6 all-gather.11

commit v2 on v1

--- a/solution.py
+++ b/solution.py
@@ -227,11 +227,318 @@
     )(q, kv, bias)
 
 
+class Line:
+    def __init__(self, nz, chunk, part, out, held, sems):
+        self.d, self.z = lax.axis_index("dp"), lax.axis_index("tensor")
+        self.chunk, self.part, self.out, self.held = chunk, part, out, held
+        self.ss, self.rr, self.fs, self.fr = sems
+        self.count = part.shape[0] // chunk
+        self.root, self.last = nz // 2 - 1, nz - 1
+
+    def rows(self, c):
+        return pl.ds(pl.multiple_of(c * self.chunk, self.chunk), self.chunk)
+
+    def toward(self, c, side, src):
+        rows = self.rows(c)
+        target = self.z + 1 if side == 0 else self.z - 1
+        return remote(
+            src.at[rows],
+            (self.out if side == 0 else self.held).at[rows],
+            self.ss.at[side, c],
+            self.rr.at[side, c],
+            (self.d, target),
+        )
+
+    def final(self, c, side):
+        rows = self.rows(c)
+        target = self.z - 1 if side == 0 else self.z + 1
+        return remote(
+            self.out.at[rows], self.out.at[rows], self.fs.at[side, c], self.fr.at[c], (self.d, target)
+        )
+
+    def mine(self, c, side):
+        rows = self.rows(c)
+        arrived = (self.out if side == 0 else self.held)[rows]
+        return arrived.astype(F32) + self.part[rows].astype(F32)
+
+    def issue(self, c):
+        @pl.when(self.z == 0)
+        def _():
+            self.toward(c, 0, self.part).start()
+
+        @pl.when(self.z == self.last)
+        def _():
+            self.toward(c, 1, self.part).start()
+
+    def service(self, c):
+        @pl.when((self.z > self.root) & (self.z < self.last))
+        def _():
+            rows = self.rows(c)
+            self.toward(c, 1, self.held).wait_recv()
+            self.held[rows] = self.mine(c, 1).astype(BF16)
+            self.toward(c, 1, self.held).start()
+
+    def ready(self, c):
+        @pl.when(self.z != self.root)
+        def _():
+            self.final(c, 1).wait_recv()
+
+        @pl.when((self.z > self.root) & (self.z < self.last))
+        def _():
+            self.final(c, 1).start()
+
+        @pl.when(self.z == self.root)
+        def _():
+            rows = self.rows(c)
+            self.toward(c, 0, self.out).wait_recv()
+            self.toward(c, 1, self.held).wait_recv()
+            self.out[rows] = (self.mine(c, 0) + self.held[rows].astype(F32)).astype(BF16)
+            self.final(c, 0).start()
+            self.final(c, 1).start()
+
+    def drain(self):
+        def body(c, carry):
+            @pl.when(self.z < self.root + 1)
+            def _():
+                @pl.when(self.z == 0)
+                def _():
+                    self.toward(c, 0, self.part).wait_send()
+
+                @pl.when(self.z == self.root)
+                def _():
+                    self.final(c, 0).wait_send()
+                    self.final(c, 1).wait_send()
+
+            @pl.when(self.z > self.root)
+            def _():
+                self.toward(c, 1, self.part).wait_send()
+
+                @pl.when(self.z < self.last)
+                def _():
+                    self.final(c, 1).wait_send()
+
+            return carry
+
+        lax.fori_loop(0, self.count, body, 0)
+
+
+def line_scratch(shape, chunk):
+    count = shape[0] // chunk
+    return [VM(shape, BF16)] + [pltpu.SemaphoreType.DMA((2, count))] * 3 + [
+        pltpu.SemaphoreType.DMA((count,))
+    ]
+
+
+def neighbours(nz):
+    d, z = lax.axis_index("dp"), lax.axis_index("tensor")
+    return [(d, lax.rem(z + 1, nz)), (d, lax.rem(z + nz - 1, nz))]
+
+
+def plane(masks):
+    d, z = lax.axis_index("dp"), lax.axis_index("tensor")
+    return [(jnp.bitwise_xor(d, m), z) for m in masks]
+
+
+def loop(start, stop, body):
+    def step(i, carry):
+        body(i)
+        return carry
+
+    lax.fori_loop(start, stop, step, 0)
+
+
+def fold_rows(values):
+    return jnp.sum(values.reshape(values.shape[0] // 8, 8, values.shape[1]), axis=0)
+
+
+class PlaneSum:
+    def __init__(self, part, out, near, far, sems):
+        self.d, self.z = lax.axis_index("dp"), lax.axis_index("tensor")
+        member = lax.rem(self.d, GROUP_DEVS)
+        self.chip, self.core = member // 2, lax.rem(member, 2)
+        self.part, self.out, self.near, self.far, self.sems = part, out, near, far, sems
+        self.height = part.shape[0] // GROUP_DEVS
+
+    def rows(self, chip, core):
+        return pl.ds(pl.multiple_of((chip * 2 + core) * self.height, self.height), self.height)
+
+    def target(self, mask):
+        return (jnp.bitwise_xor(self.d, mask), self.z)
+
+    def copy(self, kind, i, src, dst, mask):
+        return remote(
+            src, dst, self.sems.at[2 * kind, i], self.sems.at[2 * kind + 1, i], self.target(mask)
+        )
+
+    def to_core(self, i):
+        return self.copy(0, i, self.part.at[self.rows(i, 1 - self.core)], self.near.at[i], 1)
+
+    def to_chip(self, k):
+        return self.copy(1, k, self.near.at[jnp.bitwise_xor(self.chip, k)], self.far.at[k], 2 * k)
+
+    def home(self, k):
+        mine = self.out.at[self.rows(self.chip, self.core)]
+        return self.copy(2, k, mine, mine, 2 * k)
+
+    def share(self, k):
+        piece = self.out.at[self.rows(jnp.bitwise_xor(self.chip, k), self.core)]
+        return self.copy(3, k, piece, piece, 1)
+
+    def start(self):
+        for i in range(4):
+            self.to_core(i).start()
+
+    def between(self):
+        for i in range(4):
+            self.to_core(i).wait_recv()
+            mine = self.part[self.rows(i, self.core)].astype(F32)
+            self.near[i] = (mine + self.near[i].astype(F32)).astype(BF16)
+        for k in (1, 2, 3):
+            self.to_chip(k).start()
+
+    def back(self):
+        result = self.near[self.chip].astype(F32)
+        for k in (1, 2, 3):
+            self.to_chip(k).wait_recv()
+            result = result + self.far[k].astype(F32)
+        self.out[self.rows(self.chip, self.core)] = result.astype(BF16)
+        for k in (1, 2, 3):
+            self.home(k).start()
+        self.share(0).start()
+
+    def spread(self):
+        for k in (1, 2, 3):
+            self.home(k).wait_recv()
+            self.share(k).start()
+
+    def finish(self):
+        for k in range(4):
+            self.share(k).wait()
+            self.to_core(k).wait_send()
+        for k in (1, 2, 3):
+            self.home(k).wait_send()
+            self.to_chip(k).wait_send()
+
+
+def plane_scratch(shape):
+    piece = (4, shape[0] // GROUP_DEVS, shape[1])
+    return [VM(piece, BF16), VM(piece, BF16), pltpu.SemaphoreType.DMA((8, 4))]
+
+
+def last_kernel(
+    nz, chunk, part, weights, x_ref, ga_ref, gain_ref, gain_two, gt, gains, summed,
+    total, accum, box, held, ss, rr, fs, fr, bs, br, near, far, sems,
+):
+    d = lax.axis_index("dp")
+    member = lax.rem(d, GROUP_DEVS)
+    masks = range(1, GROUP_DEVS)
+    greet(neighbours(nz) + plane(masks))
+    line = Line(nz, chunk, part, total, held, (ss, rr, fs, fr))
+    plane_sum = PlaneSum(weights, summed, near, far, sems)
+    loop(0, line.count, line.issue)
+    plane_sum.start()
+    accum[...] = jnp.zeros_like(accum)
+    gain = gain_ref[...]
+    lag = 2
+
+    def body(s):
+        @pl.when(s < line.count)
+        def _():
+            line.service(s)
+
+        @pl.when(s >= lag)
+        def _():
+            c = s - lag
+            line.ready(c)
+            rows = line.rows(c)
+            x = x_ref[rows].astype(F32)
+            inverse = lax.rsqrt(jnp.mean(x * x, axis=-1, keepdims=True) + EPSILON)
+            upstream = total[rows].astype(F32)
+            inner = upstream * gain
+            through = inverse * inner - x * inverse**3 * jnp.mean(
+                inner * x, axis=-1, keepdims=True
+            )
+            gt[rows] = (ga_ref[rows].astype(F32) + through).astype(BF16)
+            accum[...] += fold_rows(upstream * x * inverse)
+
+    marks = [0, line.count // 8, line.count // 2, line.count - line.count // 8, line.count + lag]
+    loop(marks[0], marks[1], body)
+    plane_sum.between()
+    loop(marks[1], marks[2], body)
+    plane_sum.back()
+    loop(marks[2], marks[3], body)
+    plane_sum.spread()
+    loop(marks[3], marks[4], body)
+    box[member, 0:1] = jnp.sum(accum[...], axis=0, keepdims=True)
+    box[member, 1:2] = gain_two[...]
+    copies = [
+        remote(box.at[member], box.at[member], bs.at[m], br.at[m], target)
+        for m, target in zip(masks, plane(masks))
+    ]
+    for copy in copies:
+        copy.start()
+    line.drain()
+    plane_sum.finish()
+    for copy in copies:
+        copy.wait()
+    result = box[0]
+    for m in masks:
+        result = result + box[m]
+    gains[...] = result
+
+
+def last_stage(nz, part, weights, x, ga, gain, gain_two, chunk=64):
+    width = part.shape[1]
+    return pl.pallas_call(
+        functools.partial(last_kernel, nz, chunk),
+        out_shape=(
+            jax.ShapeDtypeStruct(part.shape, BF16),
+            jax.ShapeDtypeStruct((2, width), F32),
+            jax.ShapeDtypeStruct(weights.shape, BF16),
+        ),
+        in_specs=[pl.BlockSpec(memory_space=VM)] * 6,
+        out_specs=(pl.BlockSpec(memory_space=VM),) * 3,
+        scratch_shapes=[
+            VM(part.shape, BF16),
+            VM((8, width), F32),
+            VM((GROUP_DEVS, 2, width), F32),
+        ]
+        + line_scratch(part.shape, chunk)
+        + [pltpu.SemaphoreType.DMA((GROUP_DEVS,))] * 2
+        + plane_scratch(weights.shape),
+        compiler_params=pltpu.CompilerParams(
+            collective_id=3, has_side_effects=True, vmem_limit_bytes=48 << 20
+        ),
+        cost_estimate=pl.CostEstimate(
+            flops=100_000_000_000, bytes_accessed=24_000_000, transcendentals=0
+        ),
+        name="last_stage",
+    )(part, weights, x, ga, gain, gain_two)
+
+
 def backward_kernel(
-    q_ref, kv_ref, kv_all, do_ref, bias_ref, lse_ref, inner_ref, dq, dkv, dkv_tail, ktok, vtok
+    nz, chunk, q_ref, kv_ref, kv_all, do_ref, bias_ref, lse_ref, inner_ref, feed, mid_ref,
+    dq, dkv_home, dkv_tail, act,
+    dkv, near, far, ktok, vtok, total, held, ss, rr, fs, fr, ns, nr, ps, pr,
 ):
     heads = q_ref.shape[0]
     kvh = heads // 2
+    greet(neighbours(nz) + plane((1, 2, 4, 6)))
+    line = Line(nz, chunk, feed, total, held, (ss, rr, fs, fr))
+    loop(0, line.count, line.issue)
+    lag = 3
+
+    def background(s):
+        @pl.when(s < line.count)
+        def _():
+            line.service(s)
+
+        @pl.when((s >= lag) & (s < line.count + lag))
+        def _():
+            line.ready(s - lag)
+            rows = line.rows(s - lag)
+            act[rows] = (mid_ref[rows].astype(F32) + total[rows].astype(F32)).astype(BF16)
+
     dq[...] = jnp.zeros_like(dq)
 
     def block(head, half, keyt, slot, mask, bias):
@@ -251,7 +558,7 @@
         dk = dot_nt(q_ref[head, :, cols], ds)
         return dk, dv
 
-    def total(parts):
+    def total_of(parts):
         out = parts[0]
         for part in parts[1:]:
             out = out + part
@@ -264,209 +571,282 @@
         pairs = [
             block(2 * h + r, 1, kv_ref[h, :, PB : PB + CL], 1, True, None) for r in range(2)
         ]
-        dkv_tail[h] = total([p[0] for p in pairs]) * (1.0 / LOG2E)
-        dkv_tail[kvh + h] = total([p[1] for p in pairs])
-
-    def slot_step(m, first):
+        dkv_tail[h] = total_of([p[0] for p in pairs]) * (1.0 / LOG2E)
+        dkv_tail[kvh + h] = total_of([p[1] for p in pairs])
+
+    def slot_step(m, first, tick):
         for h in range(kvh):
             ktok[0, h] = kv_all[m, h].T
             vtok[0, h] = kv_all[m, kvh + h].T
         for h in range(kvh):
+            background(tick * 2 + h)
             pairs = []
             for r in range(2):
                 pairs.append(block(2 * h + r, 1, kv_all[m, h], 0, False, None))
                 pairs.append(
                     block(2 * h + r, 0, kv_all[m, h], 0, first, None if first else bias_ref[m])
                 )
-            dkv[m, h] = (total([p[0] for p in pairs]) * (1.0 / LOG2E)).astype(BF16)
-            dkv[m, kvh + h] = total([p[1] for p in pairs]).astype(BF16)
-
-    slot_step(0, True)
-
-    def step(m, carry):
-        slot_step(m, False)
-        return carry
-
-    lax.fori_loop(1, GROUP_DEVS, step, 0)
-
-
-def backward_attention(q, kv, kv_all, do, bias, lse, inner):
+            dkv[m, h] = (total_of([p[0] for p in pairs]) * (1.0 / LOG2E)).astype(BF16)
+            dkv[m, kvh + h] = total_of([p[1] for p in pairs]).astype(BF16)
+
+    def to_near(i):
+        return remote(dkv.at[2 * i + 1], near.at[i], ns.at[i], nr.at[i], plane((1,))[0])
+
+    def to_far(i):
+        return remote(near.at[i], far.at[i], ps.at[i], pr.at[i], plane((2 * i,))[0])
+
+    def odd(i):
+        slot_step(2 * i + 1, False, i)
+        to_near(i).start()
+
+    def even(i):
+        slot_step(2 * i, False, i + 3)
+        to_near(i).wait_recv()
+        near[i] = (dkv[2 * i].astype(F32) + near[i].astype(F32)).astype(BF16)
+        to_far(i).start()
+
+    quarter = GROUP_DEVS // 2
+    loop(0, quarter, odd)
+    loop(1, quarter, even)
+    slot_step(0, True, GROUP_DEVS - 1)
+    to_near(0).wait_recv()
+    dkv_home[...] = dkv[0].astype(F32) + near[0].astype(F32)
+    loop(2 * GROUP_DEVS, line.count + lag, background)
+    for i in range(1, quarter):
+        to_far(i).wait_recv()
+        dkv_home[...] += far[i].astype(F32)
+    for i in range(quarter):
+        to_near(i).wait_send()
+    for i in range(1, quarter):
+        to_far(i).wait_send()
+    line.drain()
+
+
+def backward_attention(nz, q, kv, kv_all, do, bias, lse, inner, feed, middle, chunk=64):
     heads, tokens = q.shape[0], q.shape[2]
     kvh = heads // 2
+    slot = (2 * kvh, HEAD_DIM, PB)
     return pl.pallas_call(
-        backward_kernel,
+        functools.partial(backward_kernel, nz, chunk),
         out_shape=(
             jax.ShapeDtypeStruct((heads, HEAD_DIM, tokens), F32),
-            jax.ShapeDtypeStruct((GROUP_DEVS, 2 * kvh, HEAD_DIM, PB), BF16),
+            jax.ShapeDtypeStruct(slot, F32),
             jax.ShapeDtypeStruct((2 * kvh, HEAD_DIM, CL), F32),
+            jax.ShapeDtypeStruct(feed.shape, BF16),
         ),
         in_specs=[pl.BlockSpec(memory_space=VM)] * 4
         + [pl.BlockSpec(memory_space=pltpu.SMEM)]
-        + [pl.BlockSpec(memory_space=VM)] * 2,
-        out_specs=(pl.BlockSpec(memory_space=VM),) * 3,
-        scratch_shapes=[VM((2, kvh, PB, HEAD_DIM), BF16), VM((2, kvh, PB, HEAD_DIM), BF16)],
-        compiler_params=pltpu.CompilerParams(vmem_limit_bytes=48 << 20),
+        + [pl.BlockSpec(memory_space=VM)] * 4,
+        out_specs=(pl.BlockSpec(memory_space=VM),) * 4,
+        scratch_shapes=[
+            VM((GROUP_DEVS,) + slot, BF16),
+            VM((GROUP_DEVS // 2,) + slot, BF16),
+            VM((GROUP_DEVS // 2,) + slot, BF16),
+            VM((2, kvh, PB, HEAD_DIM), BF16),
+            VM((2, kvh, PB, HEAD_DIM), BF16),
+            VM(feed.shape, BF16),
+        ]
+        + line_scratch(feed.shape, chunk)
+        + [pltpu.SemaphoreType.DMA((GROUP_DEVS // 2,))] * 4,
+        compiler_params=pltpu.CompilerParams(
+            collective_id=1, has_side_effects=True, vmem_limit_bytes=50 << 20
+        ),
         cost_estimate=pl.CostEstimate(
-            flops=60_000_000_000, bytes_accessed=12_000_000, transcendentals=19_000_000
+            flops=200_000_000_000, bytes_accessed=24_000_000, transcendentals=19_000_000
         ),
         name="backward_attention",
-    )(q, kv, kv_all, do, bias, lse, inner)
-
-
-def keys_home_kernel(part, out, near, far, ns, nr, fs, fr):
-    d, z = lax.axis_index("dp"), lax.axis_index("tensor")
-    peer = lambda m: (jnp.bitwise_xor(d, m), z)
-    greet([peer(1), peer(2), peer(4), peer(6)])
-    order = (2, 4, 6, 0)
-    nears = [
-        remote(part.at[m + 1], near.at[m // 2], ns.at[m // 2], nr.at[m // 2], peer(1))
-        for m in order
-    ]
-    for copy in nears:
+    )(q, kv, kv_all, do, bias, lse, inner, feed, middle)
+
+
+def middle_kernel(
+    nz, chunk, att_hbm, wo_hbm, x_hbm, wg_hbm, wu_hbm, wd_hbm, cot_hbm, gain_ref,
+    ga, mid, feed, gatt, inner_out, gwo, gain_two, gffn,
+    att, wo, wg, wu, wd, cot, mid32, nt2, hidden, gg, gu, part, total, accum, stage, load, store,
+    held, ss, rr, fs, fr,
+):
+    z = lax.axis_index("tensor")
+    pairs = ((x_hbm, mid), (att_hbm, att), (wo_hbm, wo), (wg_hbm, wg), (wu_hbm, wu), (cot_hbm, cot), (wd_hbm, wd))
+    loads = [pltpu.make_async_copy(src, dst, load.at[i]) for i, (src, dst) in enumerate(pairs)]
+    for copy in loads:
         copy.start()
-    fars = []
-    for i, m in enumerate(order):
-        nears[i].wait_recv()
-        merged = part[m].astype(F32) + near[m // 2].astype(F32)
-        if m == 0:
-            out[...] = merged
-        else:
-            near[m // 2] = merged.astype(BF16)
-            copy = remote(near.at[m // 2], far.at[m // 2], fs.at[m // 2], fr.at[m // 2], peer(m))
-            copy.start()
-            fars.append((copy, m))
-    for copy, m in fars:
-        copy.wait_recv()
-        out[...] += far[m // 2].astype(F32)
-    for copy in nears:
-        copy.wait_send()
-    for copy, _ in fars:
-        copy.wait_send()
-
-
-def keys_home(part):
-    shape = part.shape[1:]
+    greet(neighbours(nz))
+    tokens, width = mid.shape
+    ff = wg.shape[1]
+    own = gatt.shape[0]
+    heads = own // HEAD_DIM
+    group = 256
+    per = group // chunk
+    tile = 512
+    gain = gain_ref[...]
+    accum[...] = jnp.zeros_like(accum)
+    line = Line(nz, chunk, part, total, held, (ss, rr, fs, fr))
+    mine = pl.ds(pl.multiple_of(z * own, own), own)
+    lag = 3
+
+    def settle(c):
+        rows = line.rows(c)
+        m = mid[rows].astype(F32)
+        inverse = lax.rsqrt(jnp.mean(m * m, axis=-1, keepdims=True) + EPSILON)
+        upstream = total[rows].astype(F32)
+        inner = upstream * gain
+        through = inverse * inner - m * inverse**3 * jnp.mean(inner * m, axis=-1, keepdims=True)
+        ga[rows] = (cot[rows].astype(F32) + through).astype(BF16)
+        accum[...] += fold_rows(upstream * m * inverse)
+
+        @pl.when(lax.rem(c, per) == per - 1)
+        def _():
+            block = pl.ds(pl.multiple_of((c // per) * group, group), group)
+            back = dot_nt(wo[mine], ga[block])
+            gatt[:, block] = back.astype(BF16)
+            for head in range(heads):
+                some = pl.ds(head * HEAD_DIM, HEAD_DIM)
+                there = att[pl.ds(pl.multiple_of(z * own + head * HEAD_DIM, 32), HEAD_DIM), block]
+                inner_out[head, :, block] = jnp.sum(
+                    gatt[some, block].astype(F32) * there.astype(F32), axis=0, keepdims=True
+                )
+
+    def tick(s):
+        @pl.when((s >= 0) & (s < line.count))
+        def _():
+            line.service(s)
+
+        @pl.when((s >= lag) & (s < line.count + lag))
+        def _():
+            line.ready(s - lag)
+            settle(s - lag)
+
+    for copy in loads[:3]:
+        copy.wait()
+
+    def forward(j):
+        rows = pl.ds(pl.multiple_of(j * group, group), group)
+        a = att[:, rows].T
+        for t in range(width // tile):
+            cols = pl.ds(t * tile, tile)
+            mid32[:, cols] = mid[rows, cols].astype(F32) + dot(a, wo[:, cols])
+        m = mid32[...]
+        mid[rows] = m.astype(BF16)
+        inverse = lax.rsqrt(jnp.mean(m * m, axis=-1, keepdims=True) + EPSILON)
+        nt2[rows] = (m * inverse * gain).astype(BF16)
+
+        @pl.when(j == 0)
+        def _():
+            for copy in loads[3:]:
+                copy.wait()
+
+        tick(2 * j - 3)
+        for t in range(ff // tile):
+            cols = pl.ds(t * tile, tile)
+            gate = dot(nt2[rows], wg[:, cols])
+            up = dot(nt2[rows], wu[:, cols])
+            back = dot_nt(cot[rows], wd[cols])
+            sig = jax.nn.sigmoid(gate)
+            silu = gate * sig
+            hidden[rows, cols] = (silu * up).astype(BF16)
+            gu[rows, cols] = (back * silu).astype(BF16)
+            gg[rows, cols] = (back * up * (sig * (1.0 + gate * (1.0 - sig)))).astype(BF16)
+        for t in range(width // tile):
+            cols = pl.ds(t * tile, tile)
+            part[rows, cols] = (dot_nt(gg[rows], wg[cols]) + dot_nt(gu[rows], wu[cols])).astype(BF16)
+        loop(j * per, j * per + per, line.issue)
+        for t in range(width // tile):
+            cols = pl.ds(t * tile, tile)
+            feed[rows, cols] = dot(hidden[rows], wd[:, cols]).astype(BF16)
+        tick(2 * j - 2)
+
+    steps = tokens // group
+    loop(0, steps, forward)
+    done = 2 * steps - 3
+    slabs = width // group
+
+    def put(t):
+        return pltpu.make_async_copy(
+            stage.at[lax.rem(t, 2)],
+            gffn.at[pl.ds(pl.multiple_of(t * group, group), group)],
+            store.at[lax.rem(t, 2)],
+        )
+
+    def weights(t):
+        @pl.when(t >= 2)
+        def _():
+            put(t - 2).wait()
+
+        slot = lax.rem(t, 2)
+        cols = pl.ds(pl.multiple_of(t * group, group), group)
+        a = nt2[:, cols].T
+        stage[slot, :, 0:ff] = dot(a, gg[...]).astype(BF16)
+        stage[slot, :, ff : 2 * ff] = dot(a, gu[...]).astype(BF16)
+        stage[slot, :, 2 * ff : 3 * ff] = dot(cot[:, cols].T, hidden[...]).astype(BF16)
+        put(t).start()
+
+        @pl.when(lax.rem(t, 2) == 1)
+        def _():
+            tick(done + t // 2)
+
+    loop(0, slabs, weights)
+    loop(done + slabs // 2, line.count + lag, tick)
+    for t in range(width // tile):
+        cols = pl.ds(t * tile, tile)
+        gwo[:, cols] = dot(att[mine], ga[:, cols]).astype(BF16)
+    gain_two[...] = jnp.sum(accum[...], axis=0, keepdims=True)
+    for t in (slabs - 2, slabs - 1):
+        put(t).wait()
+    line.drain()
+
+
+def middle_stage(nz, att_all, w_out_all, x, w_gate, w_up, w_down, cot, gain, chunk=64):
+    tokens, width = x.shape
+    ff = w_gate.shape[1]
+    own = w_out_all.shape[0] // nz
+    heads = own // HEAD_DIM
+    group = 256
+    wide = jax.ShapeDtypeStruct((tokens, width), BF16)
     return pl.pallas_call(
-        keys_home_kernel,
-        out_shape=jax.ShapeDtypeStruct(shape, F32),
-        in_specs=[pl.BlockSpec(memory_space=VM)],
-        out_specs=pl.BlockSpec(memory_space=VM),
-        scratch_shapes=[VM((4,) + shape, BF16), VM((4,) + shape, BF16)]
-        + [pltpu.SemaphoreType.DMA((4,))] * 4,
+        functools.partial(middle_kernel, nz, chunk),
+        out_shape=(
+            wide,
+            wide,
+            wide,
+            jax.ShapeDtypeStruct((own, tokens), BF16),
+            jax.ShapeDtypeStruct((heads, 1, tokens), F32),
+            jax.ShapeDtypeStruct((own, width), BF16),
+            jax.ShapeDtypeStruct((1, width), F32),
+            jax.ShapeDtypeStruct((width, 3 * ff), BF16),
+        ),
+        in_specs=[pl.BlockSpec(memory_space=pl.ANY)] * 7 + [pl.BlockSpec(memory_space=VM)],
+        out_specs=(pl.BlockSpec(memory_space=VM),) * 7 + (pl.BlockSpec(memory_space=pl.ANY),),
+        scratch_shapes=[
+            VM(w_out_all.shape[:1] + (tokens,), BF16),
+            VM(w_out_all.shape, BF16),
+            VM((width, ff), BF16),
+            VM((width, ff), BF16),
+            VM((ff, width), BF16),
+            VM((tokens, width), BF16),
+            VM((group, width), F32),
+            VM((tokens, width), BF16),
+            VM((tokens, ff), BF16),
+            VM((tokens, ff), BF16),
+            VM((tokens, ff), BF16),
+            VM((tokens, width), BF16),
+            VM((tokens, width), BF16),
+            VM((8, width), F32),
+            VM((2, group, 3 * ff), BF16),
+            pltpu.SemaphoreType.DMA((7,)),
+            pltpu.SemaphoreType.DMA((2,)),
+        ]
+        + line_scratch((tokens, width), chunk),
         compiler_params=pltpu.CompilerParams(
-            collective_id=1, has_side_effects=True, vmem_limit_bytes=24 << 20
-        ),
-        name="keys_home",
-    )(part)
-
-
-def line_sum_kernel(nz, chunk, part, out, held, rs, rr, bs, br):
-    d, z = lax.axis_index("dp"), lax.axis_index("tensor")
-    greet([(d, lax.rem(z + 1, nz)), (d, lax.rem(z + nz - 1, nz))])
-    half = part.shape[0] // 2
-    count = half // chunk
-    last = nz - 1
-
-    def step(s, carry):
-        for way in range(2):
-            place = z if way == 0 else last - z
-            onward = z + 1 if way == 0 else z - 1
-            back = z - 1 if way == 0 else z + 1
-
-            def rows(c):
-                return pl.ds(pl.multiple_of(way * half + c * chunk, chunk), chunk)
-
-            def forth(c):
-                return remote(
-                    held.at[rows(c)], held.at[rows(c)], rs.at[way, c], rr.at[way, c], (d, onward)
-                )
-
-            def home(c):
-                return remote(
-                    out.at[rows(c)], out.at[rows(c)], bs.at[way, c], br.at[way, c], (d, back)
-                )
-
-            c = s - place
-            live = (c >= 0) & (c < count)
-
-            @pl.when(live & (place == 0))
-            def _():
-                remote(
-                    part.at[rows(c)], held.at[rows(c)], rs.at[way, c], rr.at[way, c], (d, onward)
-                ).start()
-
-            @pl.when(live & (place > 0) & (place < last))
-            def _():
-                forth(c).wait_recv()
-                held[rows(c)] = (held[rows(c)].astype(F32) + part[rows(c)].astype(F32)).astype(BF16)
-                forth(c).start()
-
-            @pl.when(live & (place == last))
-            def _():
-                forth(c).wait_recv()
-                out[rows(c)] = (held[rows(c)].astype(F32) + part[rows(c)].astype(F32)).astype(BF16)
-                home(c).start()
-
-            b = s - (2 * last - place)
-            back_live = (b >= 0) & (b < count) & (place < last)
-
-            @pl.when(back_live)
-            def _():
-                home(b).wait_recv()
-
-            @pl.when(back_live & (place > 0))
-            def _():
-                home(b).start()
-
-        return carry
-
-    lax.fori_loop(0, count + 2 * last, step, 0)
-
-    def drain(c, carry):
-        for way in range(2):
-            place = z if way == 0 else last - z
-            where = pl.ds(pl.multiple_of(way * half + c * chunk, chunk), chunk)
-
-            @pl.when(place < last)
-            def _():
-                remote(
-                    held.at[where], held.at[where], rs.at[way, c], rr.at[way, c], (d, z)
-                ).wait_send()
-
-            @pl.when(place > 0)
-            def _():
-                remote(out.at[where], out.at[where], bs.at[way, c], br.at[way, c], (d, z)).wait_send()
-
-        return carry
-
-    lax.fori_loop(0, count, drain, 0)
-
-
-def line_sum(nz, part, ident, chunk=16):
-    count = part.shape[0] // 2 // chunk
-    return pl.pallas_call(
-        functools.partial(line_sum_kernel, nz, chunk),
-        out_shape=jax.ShapeDtypeStruct(part.shape, BF16),
-        in_specs=[pl.BlockSpec(memory_space=VM)],
-        out_specs=pl.BlockSpec(memory_space=VM),
-        scratch_shapes=[VM(part.shape, BF16)] + [pltpu.SemaphoreType.DMA((2, count))] * 4,
-        compiler_params=pltpu.CompilerParams(
-            collective_id=ident, has_side_effects=True, vmem_limit_bytes=24 << 20
-        ),
-        name="line_sum",
-    )(part)
+            collective_id=2, has_side_effects=True, vmem_limit_bytes=60 << 20
+        ),
+        cost_estimate=pl.CostEstimate(
+            flops=100_000_000_000, bytes_accessed=50_000_000, transcendentals=1_000_000
+        ),
+        name="middle_stage",
+    )(att_all, w_out_all, x, w_gate, w_up, w_down, cot, gain)
 
 
 def rms_inverse(inputs):
     return lax.rsqrt(jnp.mean(inputs * inputs, axis=-1, keepdims=True) + EPSILON)
-
-
-def norm_back(inputs, inverse, gain, upstream):
-    inner = upstream * gain
-    through = inverse * inner - inputs * inverse**3 * jnp.mean(
-        inner * inputs, axis=-1, keepdims=True
-    )
-    return (through, jnp.sum(upstream * inputs * inverse, axis=0))
 
 
 def rotate(u, cosine, sine):
@@ -475,11 +855,6 @@
     return jnp.concatenate(
         [lower * cosine - upper * sine, upper * cosine + lower * sine], axis=1
     )
-
-
-def everywhere(share, axis_size, dimension):
-    summed = lax.psum_scatter(share.astype(BF16), "dp", scatter_dimension=dimension, tiled=True)
-    return lax.all_gather(summed, "dp", axis=dimension, tiled=True).astype(F32)
 
 
 def shards(
@@ -534,40 +909,22 @@
     heads, kvh = queries.shape[0], keys.shape[0]
 
     att_all, kv_all, lse = forward_attention(nz, queries, kv, bias)
-    attended = lax.dynamic_index_in_dim(att_all, lax.axis_index("tensor"), 0, keepdims=False)
-    attention = dot_tn(att_all.reshape(-1, count), w_out_all)
-    middle = inputs + attention
-    inverse_two = rms_inverse(middle)
-    normed_two = (middle * inverse_two * mlp_gain).astype(BF16)
-    gate_pre = dot(normed_two, w_gate)
-    up_pre = dot(normed_two, w_up)
-    sigmoid_gate = jax.nn.sigmoid(gate_pre)
-    hidden = (gate_pre * sigmoid_gate * up_pre).astype(BF16)
-    grad_hidden = dot_nt(cotangent, w_down)
-    grad_gate_low = (
-        grad_hidden * up_pre * sigmoid_gate * (1.0 + gate_pre * (1.0 - sigmoid_gate))
-    ).astype(BF16)
-    grad_up_low = (grad_hidden * gate_pre * sigmoid_gate).astype(BF16)
-    partial_two = (dot_nt(grad_gate_low, w_gate) + dot_nt(grad_up_low, w_up)).astype(BF16)
-    grad_normed_two = line_sum(nz, partial_two, 2).astype(F32)
-    feed_out = lax.psum(dot(hidden, w_down).astype(BF16), "tensor").astype(F32)
-    activations = (middle + feed_out).astype(BF16)
-    grad_w_gate_up = jnp.concatenate(
-        [dot_tn(normed_two, grad_gate_low), dot_tn(normed_two, grad_up_low)], axis=1
+    grad_attention, middle, feed_part, grad_attended, row_inner, grad_w_out, grad_gain_two, grad_ffn = (
+        middle_stage(
+            nz,
+            att_all.reshape(-1, count),
+            w_out_all,
+            tokens,
+            w_gate,
+            w_up,
+            w_down,
+            cotangent,
+            mlp_gain[None],
+        )
     )
-    grad_w_down = dot_tn(hidden, cotangent)
-    upstream = cotangent.astype(F32)
-    through_two, grad_gain_two = norm_back(middle, inverse_two, mlp_gain, grad_normed_two)
-    grad_middle = upstream + through_two
-    grad_attention = grad_middle.astype(BF16)
-    grad_w_out = dot(attended, grad_attention)
-    grad_attended = dot_nt(w_out, grad_attention).astype(BF16)
-    row_inner = jnp.sum(
-        (grad_attended.astype(F32) * attended.astype(F32)).reshape(heads, HEAD_DIM, count),
-        axis=1,
-        keepdims=True,
-    )
-    grad_queries, grad_kv_part, grad_kv_tail = backward_attention(
+    grad_ffn = lax.psum_scatter(grad_ffn, "dp", scatter_dimension=0, tiled=True)
+    grad_queries, grad_kv_prompt, grad_kv_tail, activations = backward_attention(
+        nz,
         queries,
         kv,
         kv_all,
@@ -575,8 +932,9 @@
         bias,
         lse,
         row_inner,
+        feed_part,
+        middle,
     )
-    grad_kv_prompt = keys_home(grad_kv_part)
     grad_kv = jnp.concatenate([grad_kv_prompt, grad_kv_tail], axis=2)
     grad_query_low = rotate(grad_queries * factor, cosine, -sine).astype(BF16).reshape(-1, count)
     grad_key_low = rotate(grad_kv[:kvh], cosine, -sine).astype(BF16).reshape(-1, count)
@@ -588,30 +946,35 @@
     partial_one = (
         back(grad_query_low, w_query) + back(grad_key_low, w_key) + back(grad_value_low, w_value)
     ).astype(BF16)
-    grad_normed = line_sum(nz, partial_one, 3).astype(F32)
     grads_low = jnp.concatenate([grad_query_low, grad_key_low, grad_value_low], axis=0)
-    grad_w_qkv = dot_tn(normed, grads_low.T)
-    through_one, grad_gain_one = norm_back(inputs, inverse_one, attn_gain, grad_normed)
-    grad_tokens = (grad_middle + through_one).astype(BF16)
-    gains = lax.psum(jnp.stack([grad_gain_one, grad_gain_two]), "dp")
-    gate_up = everywhere(grad_w_gate_up, n_dp, 0)
-    down = everywhere(grad_w_down, n_dp, 0)
-    out = everywhere(grad_w_out, n_dp, 0)
-    qkv = everywhere(grad_w_qkv, n_dp, 0)
-    nq, nk = w_query.shape[1], w_key.shape[1]
-    nf = w_gate.shape[1]
+    grad_attn = jnp.concatenate(
+        [dot(grads_low, normed).astype(BF16), grad_w_out], axis=0
+    )
+    partial_one, grad_ffn = lax.optimization_barrier((partial_one, grad_ffn))
+    grad_ffn = lax.all_gather(grad_ffn, "dp", axis=0, tiled=True)
+    grad_tokens, gains, grad_attn = last_stage(
+        nz, partial_one, grad_attn, tokens, grad_attention, attn_gain[None], grad_gain_two
+    )
+    if n_dp > GROUP_DEVS:
+        gains = lax.psum(gains, "dp") * (1.0 / GROUP_DEVS)
+        grad_attn = lax.psum(grad_attn.astype(F32), "dp") * (1.0 / GROUP_DEVS)
+    nq, nk, nf = w_query.shape[1], w_key.shape[1], w_gate.shape[1]
+
+    def wide(values):
+        return values.astype(F32)
+
     return (
         activations,
         grad_tokens,
         gains[0],
-        qkv[:, :nq],
-        qkv[:, nq : nq + nk],
-        qkv[:, nq + nk :],
-        out,
+        wide(grad_attn[:nq].T),
+        wide(grad_attn[nq : nq + nk].T),
+        wide(grad_attn[nq + nk : nq + 2 * nk].T),
+        wide(grad_attn[nq + 2 * nk :]),
         gains[1],
-        gate_up[:, :nf],
-        gate_up[:, nf:],
-        down,
+        wide(grad_ffn[:, :nf]),
+        wide(grad_ffn[:, nf : 2 * nf]),
+        wide(grad_ffn[:, 2 * nf :].T),
     )
 
 

time: 789 us -> 505 us (0.64)
  waiting for transfers between devices: 85.8 us -> 0.05 us
  matrix products: 78.9 us -> 14.5 us
  Pallas kernels: 470 us -> 416 us
  blocking collectives: 39.6 us -> 0 us
  local copies, waits for them, and re-layouts: 46.1 us -> 25.9 us
  other arithmetic: 38.7 us -> 24.2 us
    reduce_scatter x4 -> x1, waiting for transfers between devices: 84.3 us -> 0.01 us  [shards(): grad_ffn = lax.psum_scatter(grad_ffn, 'dp', scatter_dimension=0, tiled=True)]
    pallas_call x4 -> x3, Pallas kernels: 374 us -> 321 us  [the longest x1 114 us: last_stage(): pl.pallas_call(functools.partial(last_kernel, nz, chunk), out_shape=(jax....]
    dot_general x9 -> x0, matrix products: 52.3 us -> none  [the longest x5 30.6 us: dot_tn(): lax.dot_general(a, b, (((0,), (0,)), ((), ())), preferred_element_type=F32)]
    psum x1 -> x0, blocking collectives: 39.6 us -> none  [shards(): gains = lax.psum(jnp.stack([grad_gain_one, grad_gain_two]), 'dp')]
    slice x3 -> x1, local copies, waits for them, and re-layouts: 14.3 us -> 0.05 us  [shards(): grad_value_low = grad_kv[kvh:].astype(BF16).reshape(-1, count)]
    dot_general x4 -> x1, matrix products: 17.2 us -> 4.7 us  [dot(): return jnp.dot(a, b, preferred_element_type=F32)]
    add x1 -> x0, other arithmetic: 7.99 us -> none  [shards(): grad_middle = upstream + through_two]
    unnamed x83 -> x51, local copies, waits for them, and re-layouts: 28.1 us -> 20.9 us
  transfers between devices with their start and end apart: 10 -> 3, of which waited for: 2 -> 0; matrix products, arithmetic and copies ran while one was open for 13% -> 7% of each run, Pallas kernels for 61% -> 62%
where the time goes in v2:
time: 505 us; the launch traced here: 496 us
  Pallas kernels  416 us (82%)
  local copies, waits for them, and re-layouts  25.9 us (5%)
  other arithmetic  24.2 us (5%)
  between operations  14.7 us (3%)
  matrix products  14.5 us (3%)
    pallas_call x1, Pallas kernels, last_stage(): pl.pallas_call(functools.partial(last_kernel, nz, chunk), out_shape=(jax....  114 us
    pallas_call x1, Pallas kernels, middle_stage(): pl.pallas_call(functools.partial(middle_kernel, nz, chunk), out_shape=(wi...  110 us
    pallas_call x1, Pallas kernels, backward_attention(): pl.pallas_call(functools.partial(backward_kernel, nz, chunk), out_shape=(...  96.9 us
    pallas_call x1, Pallas kernels, forward_attention(): pl.pallas_call(functools.partial(forward_kernel, nz), out_shape=(jax.Shap...  95.4 us
    unnamed x51, local copies, waits for them, and re-layouts  20.9 us
    convert_element_type x3, other arithmetic, wide(): return values.astype(F32)  16.8 us
  transfers between devices with their start and end apart: 3, of which 0 were waited for; matrix products, arithmetic and copies ran while one was open for 7% of the time, Pallas kernels for 62%

profile of v2, /device:TPU:25, one launch (start us, length us, event | category | flops | bytes accessed | tf_op | source)
XLA Modules:
  0.0 495.6 jit_solution(953212078757516198)
XLA Ops:
  7.2 0.0 all-gather.3.cloned.1.call-start
  7.3 1.7 constant_dynamic-slice_fusion
  8.9 0.0 reduce-scatter.2.cloned.1.call-start
  9.0 1.3 broadcast_in_dim.23.gain_ref
  10.3 1.3 gather_fusion
  11.7 2.7 fusion
  14.5 1.4 fusion.9
  15.9 1.6 fusion.16
  17.6 0.2 multiply_subtract_fusion
  17.8 0.1 fusion.3.q_ref
  17.9 0.7 copy-done.17
  18.6 1.3 fusion.14
  19.9 0.1 subtract_convert_fusion.2
  20.1 1.3 convolution_convert_fusion.1
  21.4 0.1 pad_maximum_fusion.1.kv_ref
  21.5 95.4 %forward_attention.1 = (bf16[4,384,1024]{2,1,0:T(8,128)(2,1)S(1)}, bf16[8,4,96,512]{3,2,1,0:T(8,128)(2,1)}, f32[4,1,1024]{2,1,0:T(1,128)S(1)}) custom-call(bf16[4,96,1024]{2,1,0:T(8,128)(2,1)S(1)} %fusion.3.q_ref, bf16[4,96,1024]{2,1,0:T(8,128)(2,1)S(1)} %pad_maximum_fusion.1.kv_ref, f32[8]{0:T(128)S(1)} %compare_select_fusion.1.bias_ref), custom_call_target="tpu_custom_call" | custom-call | flops 40000000000 | bytes 12000000 | tf_op jit(solution)/shard_map/forward_attention/pallas_call | solution.py:197
  116.9 1.7 copy-done.3
  118.6 110.1 %middle_stage.1 = (bf16[1024,1536]{1,0:T(8,128)(2,1)}, bf16[1024,1536]{1,0:T(8,128)(2,1)}, bf16[1024,1536]{1,0:T(8,128)(2,1)}, bf16[384,1024]{1,0:T(8,128)(2,1)}...) custom-call(bf16[1536,1024]{1,0:T(8,128)(2,1)} %bitcast.36, ...), custom_call_target="tpu_custom_call" | custom-call | flops 99999997952 | bytes 50000000 | tf_op jit(solution)/shard_map/middle_stage/pallas_call | solution.py:804
  228.7 0.0 all-gather.5.cloned.1.call-start
  228.7 1.0 copy-done.4
  229.8 0.7 copy-done.6
  230.5 0.7 copy-done.7
  231.2 96.9 %backward_attention.1 = (f32[4,96,1024]{2,1,0:T(8,128)}, f32[4,96,512]{2,1,0:T(8,128)S(1)}, f32[4,96,512]{2,1,0:T(8,128)S(1)}, bf16[1024,1536]{1,0:T(8,128)(2,1)}) custom-call(bf16[4,96,1024]{2,1,0:T(8,128)(2,1)S(1)} %fusion.3.q_ref, bf16[4,96,1024]{2,1,0:T(8,128)(2,1)S(1)} %pad_maximum_fusion.1.kv_ref, bf16[8,4,96,512]{3,2,1,0:T(8,128)(2,1)} %get-tuple-element.31.kv_all, ...), custom_call_target="tpu_custom_call" | custom-call | flops 199999995904 | bytes 24000000 | tf_op jit(solution)/shard_map/backward_attention/pallas_call | solution.py:629
  328.2 0.1 constant_dynamic-update-slice_fusion.1
  328.2 0.1 constant_dynamic-update-slice_fusion
  328.3 0.1 slice.120
  328.4 0.7 copy-done.10
  329.1 0.1 copy-done.12
  329.2 0.1 subtract_convert_fusion.1
  329.3 0.4 copy-done.13
  329.8 0.1 broadcast_multiply_fusion
  329.9 0.3 subtract_convert_fusion
  330.2 0.1 pad_maximum_fusion.2
  330.2 0.6 copy-done.18
  330.8 1.0 fusion.19
  331.9 1.8 fusion.18
  333.7 2.7 add_convert_fusion.part
  336.5 4.7 convolution_convert_fusion
  341.3 2.0 pad_maximum_fusion.weights
  343.3 113.8 %last_stage.1 = (bf16[1024,1536]{1,0:T(8,128)(2,1)S(1)}, f32[2,1536]{1,0:T(2,128)S(1)}, bf16[1152,1536]{1,0:T(8,128)(2,1)}) custom-call(bf16[1024,1536]{1,0:T(8,128)(2,1)} %add_convert_fusion.part, bf16[1152,1536]{1,0:T(8,128)(2,1)} %pad_maximum_fusion.weights, bf16[1024,1536]{1,0:T(8,128)(2,1)} %x_ref.1, bf16[1024,1536]{1,0:T(8,128)(2,1)} %get-tuple-element.45.ga_ref, ...), custom_call_target="tpu_custom_call" | custom-call | flops 99999997952 | bytes 24000000 | tf_op jit(solution)/shard_map/last_stage/pallas_call | solution.py:492
  457.1 4.5 slice_convert_fusion.2
  461.7 1.9 copy.25
  463.6 0.6 slice_reduce_fusion
  464.2 2.9 convert_bitcast_fusion.2
  467.2 9.3 %convert_bitcast_fusion = (f32[1024,1536]{0,1:T(8,128)}, f32[1536,1024]{1,0:T(8,128)}, f32[1536,1024]{1,0:T(8,128)}) fusion(bf16[1536,3072]{1,0:T(8,128)(2,1)} %all-gather.5.cloned.1.call-done), kind=kLoop, calls=%fused_computation.6 | loop fusion | flops 4718592 | bytes 28311552 | tf_op jit(solution)/shard_map/convert_element_type | solution.py:964
  476.5 6.6 %copy.26 = f32[1024,1536]{1,0:T(8,128)} copy(f32[1024,1536]{0,1:T(8,128)} %get-tuple-element.75) | data formatting | bytes 12582912
  483.1 3.9 copy.30
  487.0 1.7 copy.31
  (52 shorter events, 0.3 us)
Async XLA Ops:
  7.2 8.7 %copy-start = (bf16[1536,384]{1,0:T(8,128)(2,1)S(1)}, bf16[1536,384]{1,0:T(8,128)(2,1)}, u32[]{:S(2)}) copy-start(bf16[1536,384]{1,0:T(8,128)(2,1)} %param.15) | copy-start | bytes 3538948
  7.2 8.7 %copy-start.19 = (f32[1536]{0:T(1024)S(1)}, f32[1536]{0:T(1024)}, u32[]{:S(2)}) copy-start(f32[1536]{0:T(1024)} %param.14) | copy-start | bytes 18436
  7.2 111.3 %all-gather.3.cloned.1.call-start = ((), (), s32[]{:S(2)}) async-start(), calls=%async_computation.1 | async-start | bytes 4866048 | tf_op jit(solution)/shard_map/all_gather | solution.py:891
  8.9 327.5 %reduce-scatter.2.cloned.1.call-start = ((), (), s32[]{:S(2)}) async-start(), calls=%async_computation.2 | async-start | bytes 10616832 | tf_op jit(solution)/shard_map/reduce_scatter | solution.py:925
  11.7 4.3 copy-start.11
  14.5 5.6 %copy-start.21 = (f32[1024]{0:T(1024)}, f32[1024]{0:T(1024)S(1)}, u32[]{:S(2)}) copy-start(f32[1024]{0:T(1024)S(1)} %add_rsqrt_fusion) | copy-start | bytes 12292
  15.9 4.0 copy-start.9
  17.6 1.1 copy-start.17
  18.6 1.4 copy-start.15
  116.9 1.7 copy-start.3
  118.5 110.1 %copy-start.5 = (f32[4,1,1024]{2,1,0:T(1,128)}, f32[4,1,1024]{2,1,0:T(1,128)S(1)}, u32[]{:S(2)}) copy-start(f32[4,1,1024]{2,1,0:T(1,128)S(1)} %get-tuple-element.34.lse_ref) | copy-start | bytes 49156
  228.6 1.1 copy-start.4
  228.7 238.5 %all-gather.5.cloned.1.call-start = ((), (), s32[]{:S(2)}) async-start(), calls=%async_computation.3 | async-start | bytes 10616832 | tf_op jit(solution)/shard_map/all_gather | solution.py:954
  229.8 0.7 copy-start.6
  230.5 0.7 copy-start.7
  328.1 0.9 copy-start.10
  328.1 1.0 copy-start.12
  328.2 1.6 copy-start.13
  329.8 1.1 copy-start.18
  331.8 1.9 copy-start.16
  333.7 2.8 copy-start.20
  333.7 2.8 copy-start.22
  336.5 4.7 copy-start.14
  341.3 2.0 copy-start.8
  457.1 4.5 copy-start.1
  483.1 3.9 copy-start.2
Sparse Core Ops, SparseCore 0:
  11.5 69.2 all-gather.2
  228.8 97.0 reduce-scatter.1
  336.6 83.1 all-gather.4

commit v3 on v2

--- a/solution.py
+++ b/solution.py
@@ -53,180 +53,6 @@
     )
 
 
-def forward_kernel(
-    nz, q_ref, kv_ref, bias_ref, att, kv_all, lse_ref, acc, top, total, ktok, gs, gr, zs, zr
-):
-    heads = q_ref.shape[0]
-    kvh = heads // 2
-    d, z = lax.axis_index("dp"), lax.axis_index("tensor")
-    peer = lambda m: (jnp.bitwise_xor(d, m), z)
-    greet(
-        [peer(1), peer(2), peer(4), peer(6)]
-        + [(d, lax.rem(z + 1, nz)), (d, lax.rem(z + nz - 1, nz))]
-    )
-    own = kv_ref.at[:, :, pl.ds(0, PB)]
-    firsts = [remote(own, kv_all.at[m], gs.at[m], gr.at[m], peer(m)) for m in (1, 2, 4, 6)]
-    for copy in firsts:
-        copy.start()
-    kv_all[0] = kv_ref[:, :, 0:PB]
-    for h in range(kvh):
-        ktok[8, h] = kv_ref[h, :, PB : PB + CL].T
-        ktok[0, h] = kv_ref[h, :, 0:PB].T
-    acc[...] = jnp.zeros_like(acc)
-    top[...] = jnp.full_like(top, NEG)
-    total[...] = jnp.zeros_like(total)
-
-    def block(head, half, key, value, mask, bias):
-        cols = pl.ds(half * PB, PB)
-        s = dot(key, q_ref[head, :, cols])
-        if mask:
-            s = causal(s)
-        if bias is not None:
-            s = s + bias
-        old = top[head, :, cols]
-        new = jnp.maximum(old, jnp.max(s, axis=0, keepdims=True))
-        p = jnp.exp2(s - new)
-        shrink = jnp.exp2(old - new)
-        total[head, :, cols] = total[head, :, cols] * shrink + jnp.sum(p, axis=0, keepdims=True)
-        acc[head, :, cols] = acc[head, :, cols] * shrink + dot(value, p.astype(BF16))
-        top[head, :, cols] = new
-
-    def slot_step(slot, half, mask=False, bias=None):
-        for head in range(heads):
-            block(head, half, ktok[slot, head // 2], kv_all[slot, kvh + head // 2], mask, bias)
-
-    slot_step(0, 1)
-    for head in range(heads):
-        block(head, 1, ktok[8, head // 2], kv_ref[kvh + head // 2, :, PB : PB + CL], True, None)
-
-    def arrive(m):
-        remote(kv_all.at[m], kv_all.at[m], gs.at[m], gr.at[m], peer(1)).wait_recv()
-
-    def hand_on(m):
-        return remote(kv_all.at[m], kv_all.at[m + 1], gs.at[m + 1], gr.at[m + 1], peer(1))
-
-    def tail_slot(m, carry):
-        arrive(m)
-
-        @pl.when(lax.rem(m, 2) == 0)
-        def _():
-            hand_on(m).start()
-
-        for h in range(kvh):
-            ktok[m, h] = kv_all[m, h].T
-        slot_step(m, 1)
-        return carry
-
-    tail_slot(1, 0)
-    slot_step(0, 0, mask=True)
-    slot_step(1, 0, bias=bias_ref[1])
-    lax.fori_loop(2, GROUP_DEVS, tail_slot, 0)
-
-    rows = heads * HEAD_DIM
-
-    def finish(half):
-        cols = pl.ds(half * PB, PB)
-        for head in range(heads):
-            att[z, pl.ds(head * HEAD_DIM, HEAD_DIM), cols] = (
-                acc[head, :, cols] / total[head, :, cols]
-            ).astype(BF16)
-            lse_ref[head, :, cols] = top[head, :, cols] + jnp.log2(total[head, :, cols])
-
-    def piece(index, half):
-        return att.at[index, :, pl.ds(half * PB, PB)]
-
-    def z_send(right, half, s):
-        index, target = (z - s, z + 1) if right else (z + s, z - 1)
-        there = (z - s >= 0) & (z < nz - 1) if right else (z + s < nz) & (z > 0)
-        where = piece(index, half)
-        return there, remote(
-            where, where, zs.at[half, int(right), s], zr.at[half, int(right), s], (d, target)
-        )
-
-    def z_arrive(right, half, s):
-        index = z - 1 - s if right else z + 1 + s
-        there = index >= 0 if right else index < nz
-        where = piece(index, half)
-
-        @pl.when(there)
-        def _():
-            remote(
-                where, where, zs.at[half, int(right), s], zr.at[half, int(right), s], (d, z)
-            ).wait_recv()
-
-    def z_start(half, s):
-        for right in (True, False):
-            if s > 0:
-                z_arrive(right, half, s - 1)
-            there, copy = z_send(right, half, s)
-            pl.when(there)(copy.start)
-
-    def z_finish(half):
-        for right in (True, False):
-            z_arrive(right, half, nz - 2)
-            for s in range(nz - 1):
-                there, copy = z_send(right, half, s)
-                pl.when(there)(copy.wait_send)
-
-    def prompt_slot(m, carry):
-        slot_step(m, 0, bias=bias_ref[m])
-        return carry
-
-    finish(1)
-    z_start(1, 0)
-    lax.fori_loop(2, 6, prompt_slot, 0)
-    z_start(1, 1)
-    lax.fori_loop(6, GROUP_DEVS, prompt_slot, 0)
-    finish(0)
-    z_start(0, 0)
-    for s in range(2, nz - 1):
-        z_start(1, s)
-    for s in range(1, nz - 1):
-        z_start(0, s)
-    z_finish(1)
-    z_finish(0)
-    for copy in firsts:
-        copy.wait_send()
-    for m in (2, 4, 6):
-        hand_on(m).wait_send()
-
-
-def forward_attention(nz, q, kv, bias):
-    heads, tokens = q.shape[0], q.shape[2]
-    kvh = heads // 2
-    return pl.pallas_call(
-        functools.partial(forward_kernel, nz),
-        out_shape=(
-            jax.ShapeDtypeStruct((nz, heads * HEAD_DIM, tokens), BF16),
-            jax.ShapeDtypeStruct((GROUP_DEVS, 2 * kvh, HEAD_DIM, PB), BF16),
-            jax.ShapeDtypeStruct((heads, 1, tokens), F32),
-        ),
-        in_specs=[
-            pl.BlockSpec(memory_space=VM),
-            pl.BlockSpec(memory_space=VM),
-            pl.BlockSpec(memory_space=pltpu.SMEM),
-        ],
-        out_specs=(pl.BlockSpec(memory_space=VM),) * 3,
-        scratch_shapes=[
-            VM((heads, HEAD_DIM, tokens), F32),
-            VM((heads, 1, tokens), F32),
-            VM((heads, 1, tokens), F32),
-            VM((GROUP_DEVS + 1, kvh, PB, HEAD_DIM), BF16),
-            pltpu.SemaphoreType.DMA((GROUP_DEVS,)),
-            pltpu.SemaphoreType.DMA((GROUP_DEVS,)),
-            pltpu.SemaphoreType.DMA((2, 2, nz - 1)),
-            pltpu.SemaphoreType.DMA((2, 2, nz - 1)),
-        ],
-        compiler_params=pltpu.CompilerParams(
-            collective_id=0, has_side_effects=True, vmem_limit_bytes=48 << 20
-        ),
-        cost_estimate=pl.CostEstimate(
-            flops=40_000_000_000, bytes_accessed=12_000_000, transcendentals=19_000_000
-        ),
-        name="forward_attention",
-    )(q, kv, bias)
-
-
 class Line:
     def __init__(self, nz, chunk, part, out, held, sems):
         self.d, self.z = lax.axis_index("dp"), lax.axis_index("tensor")
@@ -237,6 +63,9 @@
 
     def rows(self, c):
         return pl.ds(pl.multiple_of(c * self.chunk, self.chunk), self.chunk)
+
+    def batch(self, i, n):
+        return pl.ds(pl.multiple_of(i * self.chunk * n, self.chunk * n), self.chunk * n)
 
     def toward(self, c, side, src):
         rows = self.rows(c)
@@ -351,95 +180,188 @@
     return jnp.sum(values.reshape(values.shape[0] // 8, 8, values.shape[1]), axis=0)
 
 
-class PlaneSum:
-    def __init__(self, part, out, near, far, sems):
+class Plane:
+    def __init__(self, height, width, sems):
         self.d, self.z = lax.axis_index("dp"), lax.axis_index("tensor")
         member = lax.rem(self.d, GROUP_DEVS)
-        self.chip, self.core = member // 2, lax.rem(member, 2)
-        self.part, self.out, self.near, self.far, self.sems = part, out, near, far, sems
-        self.height = part.shape[0] // GROUP_DEVS
+        self.core = lax.rem(member, 2)
+        self.chip = member // 2
+        self.bit = (lax.rem(self.chip, 2), self.chip // 2)
+        self.height, self.half, self.sems = height, width // 2, sems
 
     def rows(self, chip, core):
-        return pl.ds(pl.multiple_of((chip * 2 + core) * self.height, self.height), self.height)
-
-    def target(self, mask):
-        return (jnp.bitwise_xor(self.d, mask), self.z)
-
-    def copy(self, kind, i, src, dst, mask):
+        return pl.ds(pl.multiple_of((chip * 2 + core) * self.height, 16), self.height)
+
+    def cols(self, colour):
+        return pl.ds(colour * self.half, self.half)
+
+    def at(self, first, x, y):
+        return x + 2 * y if first == 0 else y + 2 * x
+
+    def copy(self, i, src, dst, mask):
         return remote(
-            src, dst, self.sems.at[2 * kind, i], self.sems.at[2 * kind + 1, i], self.target(mask)
+            src, dst, self.sems.at[0, i], self.sems.at[1, i], (jnp.bitwise_xor(self.d, mask), self.z)
         )
 
+
+class PlaneReduce(Plane):
+    def __init__(self, src, mine, near, far, last, sems):
+        super().__init__(near.shape[1], near.shape[2], sems)
+        self.src, self.mine, self.near, self.far, self.last = src, mine, near, far, last
+
     def to_core(self, i):
-        return self.copy(0, i, self.part.at[self.rows(i, 1 - self.core)], self.near.at[i], 1)
-
-    def to_chip(self, k):
-        return self.copy(1, k, self.near.at[jnp.bitwise_xor(self.chip, k)], self.far.at[k], 2 * k)
-
-    def home(self, k):
-        mine = self.out.at[self.rows(self.chip, self.core)]
-        return self.copy(2, k, mine, mine, 2 * k)
-
-    def share(self, k):
-        piece = self.out.at[self.rows(jnp.bitwise_xor(self.chip, k), self.core)]
-        return self.copy(3, k, piece, piece, 1)
+        return self.copy(i, self.src.at[self.rows(i, 1 - self.core)], self.near.at[i], 1)
+
+    def fetch(self, i):
+        rows = self.src.at[self.rows(i, self.core)]
+        return pltpu.make_async_copy(rows, self.mine.at[i], self.sems.at[0, 10 + i])
+
+    def first(self, colour, k):
+        i = self.at(colour, 1 - self.bit[colour], k)
+        piece = self.near.at[i, :, self.cols(colour)]
+        return self.copy(4 + 2 * colour + k, piece, self.far.at[colour, k], 2 << colour)
+
+    def second(self, colour):
+        i = self.at(colour, self.bit[colour], 1 - self.bit[1 - colour])
+        piece = self.near.at[i, :, self.cols(colour)]
+        return self.copy(8 + colour, piece, self.last.at[colour], 4 >> colour)
 
     def start(self):
         for i in range(4):
             self.to_core(i).start()
-
-    def between(self):
+            if self.mine is not None:
+                self.fetch(i).start()
+
+    def after_core(self):
         for i in range(4):
             self.to_core(i).wait_recv()
-            mine = self.part[self.rows(i, self.core)].astype(F32)
-            self.near[i] = (mine + self.near[i].astype(F32)).astype(BF16)
+            if self.mine is not None:
+                self.fetch(i).wait()
+                own = self.mine[i]
+            else:
+                own = self.src[self.rows(i, self.core)]
+            self.near[i] = (own.astype(F32) + self.near[i].astype(F32)).astype(BF16)
+        for colour in range(2):
+            for k in range(2):
+                self.first(colour, k).start()
+
+    def after_first(self):
+        for colour in range(2):
+            for k in range(2):
+                self.first(colour, k).wait_recv()
+                i = self.at(colour, self.bit[colour], k)
+                cols = self.cols(colour)
+                self.near[i, :, cols] = (
+                    self.near[i, :, cols].astype(F32) + self.far[colour, k].astype(F32)
+                ).astype(BF16)
+        for colour in range(2):
+            self.second(colour).start()
+
+    def result(self, out):
+        for colour in range(2):
+            self.second(colour).wait_recv()
+            cols = self.cols(colour)
+            out[:, cols] = (
+                self.near[self.chip, :, cols].astype(F32) + self.last[colour].astype(F32)
+            ).astype(BF16)
+
+    def finish(self):
+        for i in range(4):
+            self.to_core(i).wait_send()
+        for colour in range(2):
+            self.second(colour).wait_send()
+            for k in range(2):
+                self.first(colour, k).wait_send()
+
+
+def reduce_scratch(height, width, fetched):
+    piece = [VM((4, height, width), BF16)]
+    return (
+        (piece if fetched else [])
+        + piece
+        + [
+            VM((2, 2, height, width // 2), BF16),
+            VM((2, height, width // 2), BF16),
+            pltpu.SemaphoreType.DMA((2, 14)),
+        ]
+    )
+
+
+class PlaneGather(Plane):
+    def __init__(self, piece, out, sems):
+        super().__init__(piece.shape[0], piece.shape[1], sems)
+        self.piece, self.out = piece, out
+
+    def place(self, dx, dy, colour):
+        chip = jnp.bitwise_xor(self.chip, dx + 2 * dy)
+        return self.out.at[self.rows(chip, self.core), self.cols(colour)]
+
+    def keep(self):
+        own = self.out.at[self.rows(self.chip, self.core)]
+        return pltpu.make_async_copy(self.piece, own, self.sems.at[0, 10])
+
+    def first(self, colour):
+        dst = self.place(0, 0, colour)
+        return self.copy(colour, self.piece.at[:, self.cols(colour)], dst, 4 >> colour)
+
+    def second(self, colour, k):
+        there = self.place(0, k, colour) if colour == 0 else self.place(k, 0, colour)
+        src = self.piece.at[:, self.cols(colour)] if k == 0 else there
+        return self.copy(2 + 2 * colour + k, src, there, 2 << colour)
+
+    def share(self, k):
+        rows = self.out.at[self.rows(jnp.bitwise_xor(self.chip, k), self.core)]
+        return self.copy(6 + k, self.piece if k == 0 else rows, rows, 1)
+
+    def start(self):
+        self.keep().start()
+        for colour in range(2):
+            self.first(colour).start()
+            self.second(colour, 0).start()
+        self.share(0).start()
+
+    def after_first(self):
+        for colour in range(2):
+            self.first(colour).wait_recv()
+            self.second(colour, 1).start()
+
+    def after_second(self):
+        for colour in range(2):
+            for k in range(2):
+                self.second(colour, k).wait_recv()
         for k in (1, 2, 3):
-            self.to_chip(k).start()
-
-    def back(self):
-        result = self.near[self.chip].astype(F32)
-        for k in (1, 2, 3):
-            self.to_chip(k).wait_recv()
-            result = result + self.far[k].astype(F32)
-        self.out[self.rows(self.chip, self.core)] = result.astype(BF16)
-        for k in (1, 2, 3):
-            self.home(k).start()
-        self.share(0).start()
-
-    def spread(self):
-        for k in (1, 2, 3):
-            self.home(k).wait_recv()
             self.share(k).start()
 
     def finish(self):
+        self.keep().wait()
         for k in range(4):
             self.share(k).wait()
-            self.to_core(k).wait_send()
-        for k in (1, 2, 3):
-            self.home(k).wait_send()
-            self.to_chip(k).wait_send()
-
-
-def plane_scratch(shape):
-    piece = (4, shape[0] // GROUP_DEVS, shape[1])
-    return [VM(piece, BF16), VM(piece, BF16), pltpu.SemaphoreType.DMA((8, 4))]
+        for colour in range(2):
+            self.first(colour).wait_send()
+            for k in range(2):
+                self.second(colour, k).wait_send()
 
 
 def last_kernel(
-    nz, chunk, part, weights, x_ref, ga_ref, gain_ref, gain_two, gt, gains, summed,
-    total, accum, box, held, ss, rr, fs, fr, bs, br, near, far, sems,
+    nz, chunk, part, weights, x_ref, ga_ref, gain_ref, gain_two, ffn_piece, gt, gains, summed, ffn,
+    total, accum, box, attn_piece, held, ss, rr, fs, fr, bs, br, near, far, far_last, reduce_sems,
+    gather_sems, ffn_sems,
 ):
     d = lax.axis_index("dp")
     member = lax.rem(d, GROUP_DEVS)
     masks = range(1, GROUP_DEVS)
     greet(neighbours(nz) + plane(masks))
     line = Line(nz, chunk, part, total, held, (ss, rr, fs, fr))
-    plane_sum = PlaneSum(weights, summed, near, far, sems)
+    reduce = PlaneReduce(weights, None, near, far, far_last, reduce_sems)
+    gather = PlaneGather(attn_piece, summed, gather_sems)
+    gather_ffn = PlaneGather(ffn_piece, ffn, ffn_sems)
     loop(0, line.count, line.issue)
-    plane_sum.start()
+    reduce.start()
+    gather_ffn.start()
     accum[...] = jnp.zeros_like(accum)
     gain = gain_ref[...]
-    lag = 2
+    lag = 10
+    batch = 4
 
     def body(s):
         @pl.when(s < line.count)
@@ -448,9 +370,11 @@
 
         @pl.when(s >= lag)
         def _():
-            c = s - lag
-            line.ready(c)
-            rows = line.rows(c)
+            line.ready(s - lag)
+
+        @pl.when((s >= lag) & (lax.rem(s - lag, batch) == batch - 1))
+        def _():
+            rows = line.batch((s - lag) // batch, batch)
             x = x_ref[rows].astype(F32)
             inverse = lax.rsqrt(jnp.mean(x * x, axis=-1, keepdims=True) + EPSILON)
             upstream = total[rows].astype(F32)
@@ -461,14 +385,32 @@
             gt[rows] = (ga_ref[rows].astype(F32) + through).astype(BF16)
             accum[...] += fold_rows(upstream * x * inverse)
 
-    marks = [0, line.count // 8, line.count // 2, line.count - line.count // 8, line.count + lag]
-    loop(marks[0], marks[1], body)
-    plane_sum.between()
-    loop(marks[1], marks[2], body)
-    plane_sum.back()
-    loop(marks[2], marks[3], body)
-    plane_sum.spread()
-    loop(marks[3], marks[4], body)
+        @pl.when(s == 5)
+        def _():
+            reduce.after_core()
+
+        @pl.when(s == 24)
+        def _():
+            gather_ffn.after_first()
+
+        @pl.when(s == 36)
+        def _():
+            reduce.after_first()
+
+        @pl.when(s == 50)
+        def _():
+            reduce.result(attn_piece)
+            gather.start()
+
+        @pl.when(s == 56)
+        def _():
+            gather_ffn.after_second()
+
+        @pl.when(s == 64)
+        def _():
+            gather.after_first()
+
+    loop(0, line.count + lag, body)
     box[member, 0:1] = jnp.sum(accum[...], axis=0, keepdims=True)
     box[member, 1:2] = gain_two[...]
     copies = [
@@ -477,8 +419,11 @@
     ]
     for copy in copies:
         copy.start()
+    gather.after_second()
     line.drain()
-    plane_sum.finish()
+    reduce.finish()
+    gather_ffn.finish()
+    gather.finish()
     for copy in copies:
         copy.wait()
     result = box[0]
@@ -487,25 +432,29 @@
     gains[...] = result
 
 
-def last_stage(nz, part, weights, x, ga, gain, gain_two, chunk=64):
+def last_stage(nz, part, weights, x, ga, gain, gain_two, ffn_piece, chunk=16):
     width = part.shape[1]
+    height = weights.shape[0] // GROUP_DEVS
     return pl.pallas_call(
         functools.partial(last_kernel, nz, chunk),
         out_shape=(
             jax.ShapeDtypeStruct(part.shape, BF16),
             jax.ShapeDtypeStruct((2, width), F32),
             jax.ShapeDtypeStruct(weights.shape, BF16),
-        ),
-        in_specs=[pl.BlockSpec(memory_space=VM)] * 6,
-        out_specs=(pl.BlockSpec(memory_space=VM),) * 3,
+            jax.ShapeDtypeStruct((ffn_piece.shape[0] * GROUP_DEVS, ffn_piece.shape[1]), BF16),
+        ),
+        in_specs=[pl.BlockSpec(memory_space=VM)] * 7,
+        out_specs=(pl.BlockSpec(memory_space=VM),) * 2 + (pl.BlockSpec(memory_space=pl.ANY),) * 2,
         scratch_shapes=[
             VM(part.shape, BF16),
             VM((8, width), F32),
             VM((GROUP_DEVS, 2, width), F32),
+            VM((height, width), BF16),
         ]
         + line_scratch(part.shape, chunk)
         + [pltpu.SemaphoreType.DMA((GROUP_DEVS,))] * 2
-        + plane_scratch(weights.shape),
+        + reduce_scratch(height, width, False)
+        + [pltpu.SemaphoreType.DMA((2, 11))] * 2,
         compiler_params=pltpu.CompilerParams(
             collective_id=3, has_side_effects=True, vmem_limit_bytes=48 << 20
         ),
@@ -513,31 +462,272 @@
             flops=100_000_000_000, bytes_accessed=24_000_000, transcendentals=0
         ),
         name="last_stage",
-    )(part, weights, x, ga, gain, gain_two)
+    )(part, weights, x, ga, gain, gain_two, ffn_piece)
+
+
+class LineGather:
+    def __init__(self, nz, place, send, recv):
+        self.d, self.z = lax.axis_index("dp"), lax.axis_index("tensor")
+        self.nz, self.place, self.send, self.recv = nz, place, send, recv
+
+    def step(self, right, s):
+        index, target = (self.z - s, self.z + 1) if right else (self.z + s, self.z - 1)
+        there = (index >= 0) & (index < self.nz) & (target >= 0) & (target < self.nz)
+        where = self.place(index)
+        way = int(right)
+        return there, remote(where, where, self.send.at[way, s], self.recv.at[way, s], (self.d, target))
+
+    def arrive(self, right, s):
+        index = self.z - 1 - s if right else self.z + 1 + s
+        where = self.place(index)
+        way = int(right)
+
+        @pl.when((index >= 0) & (index < self.nz))
+        def _():
+            remote(
+                where, where, self.send.at[way, s], self.recv.at[way, s], (self.d, self.z)
+            ).wait_recv()
+
+    def start(self, s):
+        for right in (True, False):
+            if s > 0:
+                self.arrive(right, s - 1)
+            there, copy = self.step(right, s)
+            pl.when(there)(copy.start)
+
+    def last(self):
+        for right in (True, False):
+            self.arrive(right, self.nz - 2)
+
+    def drain(self):
+        for right in (True, False):
+            for s in range(self.nz - 1):
+                there, copy = self.step(right, s)
+                pl.when(there)(copy.wait_send)
+
+
+def forward_kernel(
+    nz, q_ref, kv_ref, wo_ref, bias_ref, att, kv_all, lse_ref, wo_all, acc, top, total, ktok, mine,
+    gs, gr, zs, zr, ws, wr, wp, load,
+):
+    heads = q_ref.shape[0]
+    kvh = heads // 2
+    d, z = lax.axis_index("dp"), lax.axis_index("tensor")
+    some = mine.shape[0] // nz
+    member = lax.rem(d, GROUP_DEVS)
+
+    def own_place(index):
+        return mine.at[pl.ds(pl.multiple_of(index * some, 16), some)]
+
+    first_rows = pltpu.make_async_copy(
+        wo_ref.at[pl.ds(pl.multiple_of(member * some, 16), some)], own_place(z), load.at[0]
+    )
+    first_rows.start()
+    greet(plane((1, 2, 4, 6)) + neighbours(nz))
+    own = kv_ref.at[:, :, pl.ds(0, PB)]
+    firsts = [
+        remote(own, kv_all.at[m], gs.at[m], gr.at[m], target)
+        for m, target in zip((1, 2, 4, 6), plane((1, 2, 4, 6)))
+    ]
+    for copy in firsts:
+        copy.start()
+    w_line = LineGather(nz, own_place, ws, wr)
+    w_plane = PlaneGather(mine, wo_all, wp)
+    first_rows.wait()
+    w_line.start(0)
+    kv_all[0] = kv_ref[:, :, 0:PB]
+    for h in range(kvh):
+        ktok[8, h] = kv_ref[h, :, PB : PB + CL].T
+        ktok[0, h] = kv_ref[h, :, 0:PB].T
+    acc[...] = jnp.zeros_like(acc)
+    top[...] = jnp.full_like(top, NEG)
+    total[...] = jnp.zeros_like(total)
+
+    def block(head, half, key, value, mask, bias):
+        cols = pl.ds(half * PB, PB)
+        s = dot(key, q_ref[head, :, cols])
+        if mask:
+            s = causal(s)
+        old = top[head, :, cols]
+        high = jnp.max(s, axis=0, keepdims=True)
+        new = jnp.maximum(old, high if bias is None else high + bias)
+        p = jnp.exp2(s - (new if bias is None else new - bias))
+        shrink = jnp.exp2(old - new)
+        total[head, :, cols] = total[head, :, cols] * shrink + jnp.sum(p, axis=0, keepdims=True)
+        acc[head, :, cols] = acc[head, :, cols] * shrink + dot(value, p.astype(BF16))
+        top[head, :, cols] = new
+
+    def slot_step(slot, half, mask=False, bias=None):
+        for head in range(heads):
+            block(head, half, ktok[slot, head // 2], kv_all[slot, kvh + head // 2], mask, bias)
+
+    for head in range(heads):
+        block(head, 1, ktok[8, head // 2], kv_ref[kvh + head // 2, :, PB : PB + CL], True, None)
+
+    def arrive(m):
+        remote(kv_all.at[m], kv_all.at[m], gs.at[m], gr.at[m], (d, z)).wait_recv()
+
+    def hand_on(m):
+        return remote(kv_all.at[m], kv_all.at[m + 1], gs.at[m + 1], gr.at[m + 1], plane((1,))[0])
+
+    def tail_slot(m):
+        @pl.when(m > 0)
+        def _():
+            arrive(m)
+            for h in range(kvh):
+                ktok[m, h] = kv_all[m, h].T
+
+        @pl.when((m > 0) & (lax.rem(m, 2) == 0))
+        def _():
+            hand_on(m).start()
+
+        for s in range(1, nz - 1):
+
+            @pl.when(m == 2 * s)
+            def _():
+                w_line.start(s)
+
+        @pl.when(m == GROUP_DEVS - 1)
+        def _():
+            w_line.last()
+            w_plane.start()
+
+        slot_step(m, 1)
+
+    loop(0, GROUP_DEVS, tail_slot)
+
+    def finish(half):
+        cols = pl.ds(half * PB, PB)
+        for head in range(heads):
+            att[z, pl.ds(head * HEAD_DIM, HEAD_DIM), cols] = (
+                acc[head, :, cols] / total[head, :, cols]
+            ).astype(BF16)
+            lse_ref[head, :, cols] = top[head, :, cols] + jnp.log2(total[head, :, cols])
+
+    lines = [
+        LineGather(
+            nz,
+            lambda index, half=half: att.at[index, :, pl.ds(half * PB, PB)],
+            zs.at[half],
+            zr.at[half],
+        )
+        for half in range(2)
+    ]
+    finish(1)
+    lines[1].start(0)
+    slot_step(0, 0, mask=True)
+
+    def prompt_slot(m):
+        slot_step(m, 0, bias=bias_ref[m])
+
+        @pl.when(m == 4)
+        def _():
+            w_plane.after_first()
+            lines[1].start(1)
+
+    loop(1, GROUP_DEVS, prompt_slot)
+    finish(0)
+    lines[0].start(0)
+    w_plane.after_second()
+    for s in range(2, nz - 1):
+        lines[1].start(s)
+    for s in range(1, nz - 1):
+        lines[0].start(s)
+    for line in lines:
+        line.last()
+    for line in lines + [w_line]:
+        line.drain()
+    w_plane.finish()
+    for copy in firsts:
+        copy.wait_send()
+    for m in (2, 4, 6):
+        hand_on(m).wait_send()
+
+
+def forward_attention(nz, q, kv, w_out, bias):
+    heads, tokens = q.shape[0], q.shape[2]
+    kvh = heads // 2
+    own, width = w_out.shape
+    return pl.pallas_call(
+        functools.partial(forward_kernel, nz),
+        out_shape=(
+            jax.ShapeDtypeStruct((nz, heads * HEAD_DIM, tokens), BF16),
+            jax.ShapeDtypeStruct((GROUP_DEVS, 2 * kvh, HEAD_DIM, PB), BF16),
+            jax.ShapeDtypeStruct((heads, 1, tokens), F32),
+            jax.ShapeDtypeStruct((nz * own, width), BF16),
+        ),
+        in_specs=[
+            pl.BlockSpec(memory_space=VM),
+            pl.BlockSpec(memory_space=VM),
+            pl.BlockSpec(memory_space=pl.ANY),
+            pl.BlockSpec(memory_space=pltpu.SMEM),
+        ],
+        out_specs=(pl.BlockSpec(memory_space=VM),) * 3 + (pl.BlockSpec(memory_space=pl.ANY),),
+        scratch_shapes=[
+            VM((heads, HEAD_DIM, tokens), F32),
+            VM((heads, 1, tokens), F32),
+            VM((heads, 1, tokens), F32),
+            VM((GROUP_DEVS + 1, kvh, PB, HEAD_DIM), BF16),
+            VM((nz * own // GROUP_DEVS, width), BF16),
+            pltpu.SemaphoreType.DMA((GROUP_DEVS,)),
+            pltpu.SemaphoreType.DMA((GROUP_DEVS,)),
+            pltpu.SemaphoreType.DMA((2, 2, nz - 1)),
+            pltpu.SemaphoreType.DMA((2, 2, nz - 1)),
+            pltpu.SemaphoreType.DMA((2, nz - 1)),
+            pltpu.SemaphoreType.DMA((2, nz - 1)),
+            pltpu.SemaphoreType.DMA((2, 11)),
+            pltpu.SemaphoreType.DMA((1,)),
+        ],
+        compiler_params=pltpu.CompilerParams(
+            collective_id=0, has_side_effects=True, vmem_limit_bytes=48 << 20
+        ),
+        cost_estimate=pl.CostEstimate(
+            flops=40_000_000_000, bytes_accessed=12_000_000, transcendentals=19_000_000
+        ),
+        name="forward_attention",
+    )(q, kv, w_out, bias)
 
 
 def backward_kernel(
-    nz, chunk, q_ref, kv_ref, kv_all, do_ref, bias_ref, lse_ref, inner_ref, feed, mid_ref,
-    dq, dkv_home, dkv_tail, act,
+    nz, chunk, q_ref, kv_ref, kv_all, do_ref, bias_ref, lse_ref, inner_ref, feed, mid_ref, ffn,
+    dq, dkv_home, dkv_tail, act, ffn_piece,
     dkv, near, far, ktok, vtok, total, held, ss, rr, fs, fr, ns, nr, ps, pr,
+    f_mine, f_near, f_far, f_last, f_sems,
 ):
     heads = q_ref.shape[0]
     kvh = heads // 2
     greet(neighbours(nz) + plane((1, 2, 4, 6)))
     line = Line(nz, chunk, feed, total, held, (ss, rr, fs, fr))
+    reduce = PlaneReduce(ffn, f_mine, f_near, f_far, f_last, f_sems)
     loop(0, line.count, line.issue)
-    lag = 3
+    reduce.start()
+    lag = 12
+    ply = 4
+
+    def ripple(s):
+        @pl.when(s < line.count)
+        def _():
+            line.service(s)
+
+        @pl.when(s >= lag)
+        def _():
+            line.ready(s - lag)
+
+        @pl.when((s >= lag) & (lax.rem(s - lag, ply) == ply - 1))
+        def _():
+            rows = line.batch((s - lag) // ply, ply)
+            act[rows] = (mid_ref[rows].astype(F32) + total[rows].astype(F32)).astype(BF16)
 
     def background(s):
-        @pl.when(s < line.count)
-        def _():
-            line.service(s)
-
-        @pl.when((s >= lag) & (s < line.count + lag))
-        def _():
-            line.ready(s - lag)
-            rows = line.rows(s - lag)
-            act[rows] = (mid_ref[rows].astype(F32) + total[rows].astype(F32)).astype(BF16)
+        @pl.when(s == 3)
+        def _():
+            reduce.after_core()
+
+        @pl.when(s == 12)
+        def _():
+            reduce.after_first()
+
+        loop(s * ply, s * ply + ply, ripple)
 
     dq[...] = jnp.zeros_like(dq)
 
@@ -611,10 +801,12 @@
     slot_step(0, True, GROUP_DEVS - 1)
     to_near(0).wait_recv()
     dkv_home[...] = dkv[0].astype(F32) + near[0].astype(F32)
-    loop(2 * GROUP_DEVS, line.count + lag, background)
+    loop(2 * GROUP_DEVS * ply, line.count + lag, ripple)
+    reduce.result(ffn_piece)
     for i in range(1, quarter):
         to_far(i).wait_recv()
         dkv_home[...] += far[i].astype(F32)
+    reduce.finish()
     for i in range(quarter):
         to_near(i).wait_send()
     for i in range(1, quarter):
@@ -622,7 +814,9 @@
     line.drain()
 
 
-def backward_attention(nz, q, kv, kv_all, do, bias, lse, inner, feed, middle, chunk=64):
+def backward_attention(
+    nz, q, kv, kv_all, do, bias, lse, inner, feed, middle, ffn, chunk=16
+):
     heads, tokens = q.shape[0], q.shape[2]
     kvh = heads // 2
     slot = (2 * kvh, HEAD_DIM, PB)
@@ -633,11 +827,13 @@
             jax.ShapeDtypeStruct(slot, F32),
             jax.ShapeDtypeStruct((2 * kvh, HEAD_DIM, CL), F32),
             jax.ShapeDtypeStruct(feed.shape, BF16),
+            jax.ShapeDtypeStruct((ffn.shape[0] // GROUP_DEVS, ffn.shape[1]), BF16),
         ),
         in_specs=[pl.BlockSpec(memory_space=VM)] * 4
         + [pl.BlockSpec(memory_space=pltpu.SMEM)]
-        + [pl.BlockSpec(memory_space=VM)] * 4,
-        out_specs=(pl.BlockSpec(memory_space=VM),) * 4,
+        + [pl.BlockSpec(memory_space=VM)] * 4
+        + [pl.BlockSpec(memory_space=pl.ANY)],
+        out_specs=(pl.BlockSpec(memory_space=VM),) * 5,
         scratch_shapes=[
             VM((GROUP_DEVS,) + slot, BF16),
             VM((GROUP_DEVS // 2,) + slot, BF16),
@@ -647,15 +843,16 @@
             VM(feed.shape, BF16),
         ]
         + line_scratch(feed.shape, chunk)
-        + [pltpu.SemaphoreType.DMA((GROUP_DEVS // 2,))] * 4,
+        + [pltpu.SemaphoreType.DMA((GROUP_DEVS // 2,))] * 4
+        + reduce_scratch(ffn.shape[0] // GROUP_DEVS, ffn.shape[1], True),
         compiler_params=pltpu.CompilerParams(
-            collective_id=1, has_side_effects=True, vmem_limit_bytes=50 << 20
+            collective_id=1, has_side_effects=True, vmem_limit_bytes=56 << 20
         ),
         cost_estimate=pl.CostEstimate(
             flops=200_000_000_000, bytes_accessed=24_000_000, transcendentals=19_000_000
         ),
         name="backward_attention",
-    )(q, kv, kv_all, do, bias, lse, inner, feed, middle)
+    )(q, kv, kv_all, do, bias, lse, inner, feed, middle, ffn)
 
 
 def middle_kernel(
@@ -665,26 +862,38 @@
     held, ss, rr, fs, fr,
 ):
     z = lax.axis_index("tensor")
-    pairs = ((x_hbm, mid), (att_hbm, att), (wo_hbm, wo), (wg_hbm, wg), (wu_hbm, wu), (cot_hbm, cot), (wd_hbm, wd))
+    pairs = ((x_hbm, mid), (att_hbm, att), (wg_hbm, wg), (wu_hbm, wu), (cot_hbm, cot), (wd_hbm, wd))
     loads = [pltpu.make_async_copy(src, dst, load.at[i]) for i, (src, dst) in enumerate(pairs)]
-    for copy in loads:
+    own = gatt.shape[0]
+    some = own // GROUP_DEVS
+
+    def wo_rows(i):
+        src = pl.ds(pl.multiple_of(i * some, 16), some)
+        dst = pl.ds(pl.multiple_of(lax.rem(i, nz) * own + i // nz * some, 16), some)
+        pltpu.make_async_copy(wo_hbm.at[src], wo.at[dst], load.at[len(pairs)]).start()
+
+    for copy in loads[:2]:
+        copy.start()
+    loop(0, nz * GROUP_DEVS, wo_rows)
+    for copy in loads[2:]:
         copy.start()
     greet(neighbours(nz))
     tokens, width = mid.shape
     ff = wg.shape[1]
-    own = gatt.shape[0]
     heads = own // HEAD_DIM
     group = 256
     per = group // chunk
+    ply = 4
+    quarters = per // ply
     tile = 512
     gain = gain_ref[...]
     accum[...] = jnp.zeros_like(accum)
     line = Line(nz, chunk, part, total, held, (ss, rr, fs, fr))
     mine = pl.ds(pl.multiple_of(z * own, own), own)
-    lag = 3
+    lag = 12
 
     def settle(c):
-        rows = line.rows(c)
+        rows = line.batch(c, ply)
         m = mid[rows].astype(F32)
         inverse = lax.rsqrt(jnp.mean(m * m, axis=-1, keepdims=True) + EPSILON)
         upstream = total[rows].astype(F32)
@@ -693,9 +902,9 @@
         ga[rows] = (cot[rows].astype(F32) + through).astype(BF16)
         accum[...] += fold_rows(upstream * m * inverse)
 
-        @pl.when(lax.rem(c, per) == per - 1)
-        def _():
-            block = pl.ds(pl.multiple_of((c // per) * group, group), group)
+        @pl.when(lax.rem(c, quarters) == quarters - 1)
+        def _():
+            block = pl.ds(pl.multiple_of((c // quarters) * group, group), group)
             back = dot_nt(wo[mine], ga[block])
             gatt[:, block] = back.astype(BF16)
             for head in range(heads):
@@ -705,18 +914,27 @@
                     gatt[some, block].astype(F32) * there.astype(F32), axis=0, keepdims=True
                 )
 
+    def ripple(s):
+        @pl.when(s < line.count)
+        def _():
+            line.service(s)
+
+        @pl.when(s >= lag)
+        def _():
+            line.ready(s - lag)
+
+        @pl.when((s >= lag) & (lax.rem(s - lag, ply) == ply - 1))
+        def _():
+            settle((s - lag) // ply)
+
     def tick(s):
-        @pl.when((s >= 0) & (s < line.count))
-        def _():
-            line.service(s)
-
-        @pl.when((s >= lag) & (s < line.count + lag))
-        def _():
-            line.ready(s - lag)
-            settle(s - lag)
-
-    for copy in loads[:3]:
+        @pl.when(s >= 0)
+        def _():
+            loop(s * ply, s * ply + ply, ripple)
+
+    for copy in loads[:2]:
         copy.wait()
+    pltpu.make_async_copy(wo_hbm, wo, load.at[len(pairs)]).wait()
 
     def forward(j):
         rows = pl.ds(pl.multiple_of(j * group, group), group)
@@ -731,7 +949,7 @@
 
         @pl.when(j == 0)
         def _():
-            for copy in loads[3:]:
+            for copy in loads[2:]:
                 copy.wait()
 
         tick(2 * j - 3)
@@ -784,7 +1002,7 @@
             tick(done + t // 2)
 
     loop(0, slabs, weights)
-    loop(done + slabs // 2, line.count + lag, tick)
+    loop((done + slabs // 2) * ply, line.count + lag, ripple)
     for t in range(width // tile):
         cols = pl.ds(t * tile, tile)
         gwo[:, cols] = dot(att[mine], ga[:, cols]).astype(BF16)
@@ -794,7 +1012,7 @@
     line.drain()
 
 
-def middle_stage(nz, att_all, w_out_all, x, w_gate, w_up, w_down, cot, gain, chunk=64):
+def middle_stage(nz, att_all, w_out_all, x, w_gate, w_up, w_down, cot, gain, chunk=16):
     tokens, width = x.shape
     ff = w_gate.shape[1]
     own = w_out_all.shape[0] // nz
@@ -843,6 +1061,57 @@
         ),
         name="middle_stage",
     )(att_all, w_out_all, x, w_gate, w_up, w_down, cot, gain)
+
+
+def finish_kernel(nq, nk, ffn, attn, gt, act, gate, up, down, q, k, v, o, gt_out, act_out):
+    ff = gate.shape[1]
+    gate[...] = ffn[:, 0:ff].astype(F32)
+    up[...] = ffn[:, ff : 2 * ff].astype(F32)
+    down[...] = ffn[:, 2 * ff : 3 * ff].astype(F32).T
+    q[...] = attn[0:nq].astype(F32).T
+    k[...] = attn[nq : nq + nk].astype(F32)
+    v[...] = attn[nq + nk : nq + 2 * nk].astype(F32)
+    o[...] = attn[nq + 2 * nk :].astype(F32)
+    gt_out[...] = gt[...]
+    act_out[...] = act[...]
+
+
+def finish(ffn, attn, gt, act, nq, nk):
+    width, ff = ffn.shape[0], ffn.shape[1] // 3
+    tokens, own = gt.shape[0], attn.shape[0] - nq - 2 * nk
+    tile = 256
+    wide = lambda *shape: jax.ShapeDtypeStruct(shape, F32)
+    down = lambda rows: pl.BlockSpec((tile, rows), lambda i: (i, 0))
+    side = lambda rows: pl.BlockSpec((rows, tile), lambda i: (0, i))
+    return pl.pallas_call(
+        functools.partial(finish_kernel, nq, nk),
+        grid=(width // tile,),
+        out_shape=(
+            wide(width, ff),
+            wide(width, ff),
+            wide(ff, width),
+            wide(width, nq),
+            wide(nk, width),
+            wide(nk, width),
+            wide(own, width),
+            jax.ShapeDtypeStruct(gt.shape, gt.dtype),
+            jax.ShapeDtypeStruct(act.shape, act.dtype),
+        ),
+        in_specs=[down(3 * ff), side(attn.shape[0]), side(tokens), side(tokens)],
+        out_specs=(
+            down(ff),
+            down(ff),
+            side(ff),
+            down(nq),
+            side(nk),
+            side(nk),
+            side(own),
+            side(tokens),
+            side(tokens),
+        ),
+        compiler_params=pltpu.CompilerParams(vmem_limit_bytes=40 << 20),
+        name="finish",
+    )(ffn, attn, gt, act)
 
 
 def rms_inverse(inputs):
@@ -886,10 +1155,6 @@
     angle = frequency[:, None] * places.astype(F32)[None, :]
     cosine, sine = jnp.cos(angle)[None], jnp.sin(angle)[None]
 
-    rows = w_out.shape[0] // n_dp
-    w_piece = lax.dynamic_slice_in_dim(w_out, device * rows, rows, 0)
-    w_out_all = lax.all_gather(w_piece, ("tensor", "dp"), axis=0, tiled=True)
-
     count = tokens.shape[0]
     factor = HEAD_DIM ** (-0.5)
     inputs = tokens.astype(F32)
@@ -908,7 +1173,7 @@
     kv = jnp.concatenate([keys, values], axis=0)
     heads, kvh = queries.shape[0], keys.shape[0]
 
-    att_all, kv_all, lse = forward_attention(nz, queries, kv, bias)
+    att_all, kv_all, lse, w_out_all = forward_attention(nz, queries, kv, w_out, bias)
     grad_attention, middle, feed_part, grad_attended, row_inner, grad_w_out, grad_gain_two, grad_ffn = (
         middle_stage(
             nz,
@@ -922,8 +1187,7 @@
             mlp_gain[None],
         )
     )
-    grad_ffn = lax.psum_scatter(grad_ffn, "dp", scatter_dimension=0, tiled=True)
-    grad_queries, grad_kv_prompt, grad_kv_tail, activations = backward_attention(
+    grad_queries, grad_kv_prompt, grad_kv_tail, activations, ffn_piece = backward_attention(
         nz,
         queries,
         kv,
@@ -934,6 +1198,7 @@
         row_inner,
         feed_part,
         middle,
+        grad_ffn,
     )
     grad_kv = jnp.concatenate([grad_kv_prompt, grad_kv_tail], axis=2)
     grad_query_low = rotate(grad_queries * factor, cosine, -sine).astype(BF16).reshape(-1, count)
@@ -950,31 +1215,37 @@
     grad_attn = jnp.concatenate(
         [dot(grads_low, normed).astype(BF16), grad_w_out], axis=0
     )
-    partial_one, grad_ffn = lax.optimization_barrier((partial_one, grad_ffn))
-    grad_ffn = lax.all_gather(grad_ffn, "dp", axis=0, tiled=True)
-    grad_tokens, gains, grad_attn = last_stage(
-        nz, partial_one, grad_attn, tokens, grad_attention, attn_gain[None], grad_gain_two
+    grad_tokens, gains, grad_attn, grad_ffn = last_stage(
+        nz,
+        partial_one,
+        grad_attn,
+        tokens,
+        grad_attention,
+        attn_gain[None],
+        grad_gain_two,
+        ffn_piece,
     )
     if n_dp > GROUP_DEVS:
         gains = lax.psum(gains, "dp") * (1.0 / GROUP_DEVS)
         grad_attn = lax.psum(grad_attn.astype(F32), "dp") * (1.0 / GROUP_DEVS)
-    nq, nk, nf = w_query.shape[1], w_key.shape[1], w_gate.shape[1]
-
-    def wide(values):
-        return values.astype(F32)
-
+        grad_ffn = lax.psum(grad_ffn.astype(F32), "dp") * (1.0 / GROUP_DEVS)
+    nq, nk = w_query.shape[1], w_key.shape[1]
+
+    gate, up, down, query, key, value, out, grad_tokens, activations = finish(
+        grad_ffn, grad_attn, grad_tokens, activations, nq, nk
+    )
     return (
         activations,
         grad_tokens,
         gains[0],
-        wide(grad_attn[:nq].T),
-        wide(grad_attn[nq : nq + nk].T),
-        wide(grad_attn[nq + nk : nq + 2 * nk].T),
-        wide(grad_attn[nq + 2 * nk :]),
+        query,
+        key.T,
+        value.T,
+        out,
         gains[1],
-        wide(grad_ffn[:, :nf]),
-        wide(grad_ffn[:, nf : 2 * nf]),
-        wide(grad_ffn[:, 2 * nf :].T),
+        gate,
+        up,
+        down,
     )
 
 

time: 505 us -> 455 us (0.901)
  other arithmetic: 24.2 us -> 7.34 us
  local copies, waits for them, and re-layouts: 25.9 us -> 11.2 us
  between operations: 14.7 us -> 1.5 us
    convert_element_type x3 -> x0, other arithmetic: 16.8 us -> none  [wide(): return values.astype(F32)]
    pallas_call x0 -> x1, Pallas kernels: none -> 13.9 us  [finish(): pl.pallas_call(functools.partial(finish_kernel, nq, nk), grid=(width // t...]
    unnamed x51 -> x55, local copies, waits for them, and re-layouts: 20.9 us -> 7.31 us
    pallas_call x1, Pallas kernels: 95.4 us -> 83.3 us  [forward_attention(): pl.pallas_call(functools.partial(forward_kernel, nz), out_shape=(jax.Shap...]
    pallas_call x1, Pallas kernels: 114 us -> 103 us  [last_stage(): pl.pallas_call(functools.partial(last_kernel, nz, chunk), out_shape=(jax....]
    pallas_call x1, Pallas kernels: 96.9 us -> 103 us  [backward_attention(): pl.pallas_call(functools.partial(backward_kernel, nz, chunk), out_shape=(...]
  transfers between devices with their start and end apart: 3 -> 0, of which waited for: 0 -> 0; matrix products, arithmetic and copies ran while one was open for 7% -> 0% of each run, Pallas kernels for 62% -> 0%
where the time goes in v3:
time: 455 us; the launch traced here: 450 us
  Pallas kernels  417 us (92%)
  matrix products  12.7 us (3%)
  local copies, waits for them, and re-layouts  11.2 us (2%)
  other arithmetic  7.34 us (2%)
    pallas_call x1, Pallas kernels, middle_stage(): pl.pallas_call(functools.partial(middle_kernel, nz, chunk), out_shape=(wi...  114 us
    pallas_call x1, Pallas kernels, last_stage(): pl.pallas_call(functools.partial(last_kernel, nz, chunk), out_shape=(jax....  103 us
    pallas_call x1, Pallas kernels, backward_attention(): pl.pallas_call(functools.partial(backward_kernel, nz, chunk), out_shape=(...  103 us
    pallas_call x1, Pallas kernels, forward_attention(): pl.pallas_call(functools.partial(forward_kernel, nz), out_shape=(jax.Shap...  83.3 us
    pallas_call x1, Pallas kernels, finish(): pl.pallas_call(functools.partial(finish_kernel, nq, nk), grid=(width // t...  13.9 us

profile of v3, /device:TPU:25, one launch (start us, length us, event | category | flops | bytes accessed | tf_op | source)
XLA Modules:
  0.0 449.9 jit_solution(5301028385938650040)
XLA Ops:
  0.6 0.0 copy-start
  0.7 0.0 copy-start.23
  0.7 0.0 copy-start.20
  0.7 1.4 gather_fusion
  2.2 0.0 copy-start.13
  2.2 1.5 fusion.9
  3.7 2.6 fusion
  6.4 0.0 copy-start.25
  6.4 0.0 copy-start.18
  6.4 1.3 fusion.14
  7.7 0.1 subtract_convert_fusion.2
  7.9 1.3 convolution_convert_fusion.1
  9.2 0.1 pad_maximum_fusion.1.kv_ref
  9.3 0.0 copy-start.3
  9.3 1.6 fusion.16
  10.9 0.0 copy-start.5
  10.9 0.2 multiply_subtract_fusion
  11.1 0.1 fusion.3.q_ref
  11.3 0.0 copy-start.4
  11.3 0.8 copy-done.5
  12.2 83.3 %forward_attention.1 = (bf16[4,384,1024]{2,1,0:T(8,128)(2,1)S(1)}, bf16[8,4,96,512]{3,2,1,0:T(8,128)(2,1)}, f32[4,1,1024]{2,1,0:T(1,128)S(1)}, bf16[1536,1536]{1,0:T(8,128)(2,1)}) custom-call(bf16[4,96,1024]{2,1,0:T(8,128)(2,1)S(1)} %fusion.3.q_ref, bf16[4,96,1024]{2,1,0:T(8,128)(2,1)S(1)} %pad_maximum_fusion.1.kv_ref, bf16[384,1536]{1,0:T(8,128)(2,1)S(1)} %copy-done.5, ...), custom_call_target="tpu_custom_call" | custom-call | flops 40000000000 | bytes 12000000 | tf_op jit(solution)/shard_map/forward_attention/pallas_call | solution.py:651
  95.5 0.0 copy-start.6
  95.5 1.7 copy-done.6
  97.1 0.6 broadcast_in_dim.23.gain_ref
  97.7 114.1 %middle_stage.1 = (bf16[1024,1536]{1,0:T(8,128)(2,1)}, bf16[1024,1536]{1,0:T(8,128)(2,1)}, bf16[1024,1536]{1,0:T(8,128)(2,1)}, bf16[384,1024]{1,0:T(8,128)(2,1)}...) custom-call(bf16[1536,1024]{1,0:T(8,128)(2,1)} %bitcast.30, ...), custom_call_target="tpu_custom_call" | custom-call | flops 99999997952 | bytes 50000000 | tf_op jit(solution)/shard_map/middle_stage/pallas_call | solution.py:1022
  211.9 102.9 %backward_attention.1 = (f32[4,96,1024]{2,1,0:T(8,128)}, f32[4,96,512]{2,1,0:T(8,128)}, f32[4,96,512]{2,1,0:T(8,128)}, bf16[1024,1536]{1,0:T(8,128)(2,1)}, bf16[192,3072]{1,0:T(8,128)(2,1)}) custom-call(bf16[4,96,1024]{2,1,0:T(8,128)(2,1)} %copy-done.4, bf16[4,96,1024]{2,1,0:T(8,128)(2,1)} %copy-done.3, bf16[8,4,96,512]{3,2,1,0:T(8,128)(2,1)} %get-tuple-element.41.kv_all, ...), custom_call_target="tpu_custom_call" | custom-call | flops 199999995904 | bytes 24000000 | tf_op jit(solution)/shard_map/backward_attention/pallas_call | solution.py:823
  314.8 0.0 copy-start.12
  314.8 0.0 copy-start.15
  314.8 1.3 constant_dynamic-update-slice_fusion.1
  316.2 1.2 constant_dynamic-update-slice_fusion
  317.4 0.1 subtract_convert_fusion.1
  317.6 0.0 copy-start.14
  317.6 0.0 copy-start.24
  317.6 0.0 copy-start.26
  317.7 0.1 broadcast_multiply_fusion
  317.8 0.3 subtract_convert_fusion
  318.1 0.1 pad_maximum_fusion.2
  318.1 1.4 copy-done.14
  319.5 2.8 convolution_convert_fusion
  322.3 0.0 copy-start.21
  322.3 2.0 pad_maximum_fusion.weights
  324.4 1.0 fusion.19
  325.4 1.9 fusion.18
  327.3 2.8 add_convert_fusion.part
  330.1 103.0 %last_stage.1 = (bf16[1024,1536]{1,0:T(8,128)(2,1)S(1)}, f32[2,1536]{1,0:T(2,128)S(1)}, bf16[1152,1536]{1,0:T(8,128)(2,1)}, bf16[1536,3072]{1,0:T(8,128)(2,1)}) custom-call(bf16[1024,1536]{1,0:T(8,128)(2,1)} %add_convert_fusion.part, bf16[1152,1536]{1,0:T(8,128)(2,1)} %pad_maximum_fusion.weights, bf16[1024,1536]{1,0:T(8,128)(2,1)} %x_ref.1, ...), custom_call_target="tpu_custom_call" | custom-call | flops 99999997952 | bytes 24000000 | tf_op jit(solution)/shard_map/last_stage/pallas_call | solution.py:438
  433.1 2.0 copy-done.1
  435.1 13.9 %finish.1 = (f32[1536,1024]{1,0:T(8,128)}, f32[1536,1024]{1,0:T(8,128)}, f32[1024,1536]{1,0:T(8,128)}, f32[1536,384]{1,0:T(8,128)}, f32[192,1536]{1,0:T(8,128)},...) custom-call(bf16[1536,3072]{1,0:T(8,128)(2,1)} %get-tuple-element.57.ffn, ...), custom_call_target="tpu_custom_call" | custom-call | tf_op jit(solution)/shard_map/finish/pallas_call | solution.py:1086
  449.0 0.6 slice_reduce_fusion
  (44 shorter events, 0.2 us)
Async XLA Ops:
  0.6 8.6 %copy-start = (bf16[1536,384]{1,0:T(8,128)(2,1)S(1)}, bf16[1536,384]{1,0:T(8,128)(2,1)}, u32[]{:S(2)}) copy-start(bf16[1536,384]{1,0:T(8,128)(2,1)} %param.15) | copy-start | bytes 3538948
  0.7 5.7 %copy-start.23 = (f32[1536]{0:T(1024)S(1)}, f32[1536]{0:T(1024)}, u32[]{:S(2)}) copy-start(f32[1536]{0:T(1024)} %param.14) | copy-start | bytes 18436
  0.7 5.7 %copy-start.20 = (bf16[1536,192]{0,1:T(8,128)(2,1)S(1)}, bf16[1536,192]{0,1:T(8,128)(2,1)}, u32[]{:S(2)}) copy-start(bf16[1536,192]{0,1:T(8,128)(2,1)} %param.16) | copy-start | bytes 1769476
  2.2 4.2 copy-start.13
  3.7 7.2 %copy-start.11 = (f32[48,1024]{1,0:T(8,128)}, f32[48,1024]{1,0:T(8,128)S(1)}, u32[]{:S(2)}) copy-start(f32[48,1024]{1,0:T(8,128)S(1)} %get-tuple-element.83) | copy-start | bytes 589828
  6.4 2.9 copy-start.25
  6.4 1.5 copy-start.18
  9.3 2.1 copy-start.3
  10.9 1.3 copy-start.5
  11.3 84.2 %copy-start.4 = (bf16[4,96,1024]{2,1,0:T(8,128)(2,1)}, bf16[4,96,1024]{2,1,0:T(8,128)(2,1)S(1)}, u32[]{:S(2)}) copy-start(bf16[4,96,1024]{2,1,0:T(8,128)(2,1)S(1)} %fusion.3.q_ref) | copy-start | bytes 2359300
  12.2 83.3 %copy-start.7 = (f32[8]{0:T(128)}, f32[8]{0:T(128)S(1)}, u32[]{:S(2)}) copy-start(f32[8]{0:T(128)S(1)} %compare_select_fusion.1.bias_ref) | copy-start | bytes 100
  12.2 85.0 %copy-start.22 = (f32[1536]{0:T(1024)S(1)}, f32[1536]{0:T(1024)}, u32[]{:S(2)}) copy-start(f32[1536]{0:T(1024)} %param.19) | copy-start | bytes 18436
  95.5 1.7 copy-start.6
  97.1 114.7 %copy-start.9 = (f32[4,1,1024]{2,1,0:T(1,128)}, f32[4,1,1024]{2,1,0:T(1,128)S(1)}, u32[]{:S(2)}) copy-start(f32[4,1,1024]{2,1,0:T(1,128)S(1)} %get-tuple-element.45.lse_ref) | copy-start | bytes 49156
  314.8 2.6 copy-start.12
  314.8 2.6 copy-start.15
  314.8 2.8 copy-start.16
  317.6 1.9 copy-start.14
  317.6 1.9 copy-start.24
  317.6 1.9 copy-start.26
  319.5 2.8 copy-start.17
  322.3 2.0 copy-start.21
  325.4 1.9 copy-start.19
  327.3 2.8 copy-start.8
  327.3 2.8 copy-start.10
  330.1 103.0 %copy-start.2 = (bf16[1024,1536]{1,0:T(8,128)(2,1)S(1)}, bf16[1024,1536]{1,0:T(8,128)(2,1)}, u32[]{:S(2)}) copy-start(bf16[1024,1536]{1,0:T(8,128)(2,1)} %get-tuple-element.60.act) | copy-start | bytes 9437188
  433.1 2.0 copy-start.1

commit v4 on v3

--- a/solution.py
+++ b/solution.py
@@ -54,17 +54,22 @@
 
 
 class Line:
-    def __init__(self, nz, chunk, part, out, held, sems):
+    def __init__(self, nz, chunk, part, out, held, sems, shift=0):
         self.d, self.z = lax.axis_index("dp"), lax.axis_index("tensor")
+        self.shift = shift
         self.chunk, self.part, self.out, self.held = chunk, part, out, held
         self.ss, self.rr, self.fs, self.fr = sems
         self.count = part.shape[0] // chunk
         self.root, self.last = nz // 2 - 1, nz - 1
 
     def rows(self, c):
+        if self.shift:
+            c = lax.rem(c + self.shift, self.count)
         return pl.ds(pl.multiple_of(c * self.chunk, self.chunk), self.chunk)
 
     def batch(self, i, n):
+        if self.shift:
+            i = lax.rem(i + self.shift // n, self.count // n)
         return pl.ds(pl.multiple_of(i * self.chunk * n, self.chunk * n), self.chunk * n)
 
     def toward(self, c, side, src):
@@ -206,41 +211,47 @@
 
 class PlaneReduce(Plane):
     def __init__(self, src, mine, near, far, last, sems):
-        super().__init__(near.shape[1], near.shape[2], sems)
+        super().__init__(src.shape[0] // GROUP_DEVS, src.shape[1], sems)
         self.src, self.mine, self.near, self.far, self.last = src, mine, near, far, last
 
     def to_core(self, i):
-        return self.copy(i, self.src.at[self.rows(i, 1 - self.core)], self.near.at[i], 1)
+        return self.copy(i, self.src.at[self.rows(i, 1 - self.core)], self.near(i), 1)
 
     def fetch(self, i):
         rows = self.src.at[self.rows(i, self.core)]
-        return pltpu.make_async_copy(rows, self.mine.at[i], self.sems.at[0, 10 + i])
+        return pltpu.make_async_copy(rows, self.mine, self.sems.at[0, 10])
+
+    def part_of(self, i, colour):
+        return self.near(i).at[:, self.cols(colour)]
 
     def first(self, colour, k):
         i = self.at(colour, 1 - self.bit[colour], k)
-        piece = self.near.at[i, :, self.cols(colour)]
-        return self.copy(4 + 2 * colour + k, piece, self.far.at[colour, k], 2 << colour)
+        return self.copy(
+            4 + 2 * colour + k, self.part_of(i, colour), self.far(colour, k), 2 << colour
+        )
 
     def second(self, colour):
         i = self.at(colour, self.bit[colour], 1 - self.bit[1 - colour])
-        piece = self.near.at[i, :, self.cols(colour)]
-        return self.copy(8 + colour, piece, self.last.at[colour], 4 >> colour)
+        return self.copy(8 + colour, self.part_of(i, colour), self.last(colour), 4 >> colour)
 
     def start(self):
         for i in range(4):
             self.to_core(i).start()
-            if self.mine is not None:
-                self.fetch(i).start()
+        if self.mine is not None:
+            self.fetch(0).start()
 
     def after_core(self):
         for i in range(4):
             self.to_core(i).wait_recv()
             if self.mine is not None:
                 self.fetch(i).wait()
-                own = self.mine[i]
+                own = self.mine[...]
             else:
                 own = self.src[self.rows(i, self.core)]
-            self.near[i] = (own.astype(F32) + self.near[i].astype(F32)).astype(BF16)
+            near = self.near(i)
+            near[...] = (own.astype(F32) + near[...].astype(F32)).astype(BF16)
+            if self.mine is not None and i < 3:
+                self.fetch(i + 1).start()
         for colour in range(2):
             for k in range(2):
                 self.first(colour, k).start()
@@ -249,10 +260,9 @@
         for colour in range(2):
             for k in range(2):
                 self.first(colour, k).wait_recv()
-                i = self.at(colour, self.bit[colour], k)
-                cols = self.cols(colour)
-                self.near[i, :, cols] = (
-                    self.near[i, :, cols].astype(F32) + self.far[colour, k].astype(F32)
+                mine = self.part_of(self.at(colour, self.bit[colour], k), colour)
+                mine[...] = (
+                    mine[...].astype(F32) + self.far(colour, k)[...].astype(F32)
                 ).astype(BF16)
         for colour in range(2):
             self.second(colour).start()
@@ -260,9 +270,9 @@
     def result(self, out):
         for colour in range(2):
             self.second(colour).wait_recv()
-            cols = self.cols(colour)
-            out[:, cols] = (
-                self.near[self.chip, :, cols].astype(F32) + self.last[colour].astype(F32)
+            out[:, self.cols(colour)] = (
+                self.part_of(self.chip, colour)[...].astype(F32)
+                + self.last(colour)[...].astype(F32)
             ).astype(BF16)
 
     def finish(self):
@@ -274,19 +284,6 @@
                 self.first(colour, k).wait_send()
 
 
-def reduce_scratch(height, width, fetched):
-    piece = [VM((4, height, width), BF16)]
-    return (
-        (piece if fetched else [])
-        + piece
-        + [
-            VM((2, 2, height, width // 2), BF16),
-            VM((2, height, width // 2), BF16),
-            pltpu.SemaphoreType.DMA((2, 14)),
-        ]
-    )
-
-
 class PlaneGather(Plane):
     def __init__(self, piece, out, sems):
         super().__init__(piece.shape[0], piece.shape[1], sems)
@@ -317,11 +314,11 @@
         self.keep().start()
         for colour in range(2):
             self.first(colour).start()
-            self.second(colour, 0).start()
         self.share(0).start()
 
     def after_first(self):
         for colour in range(2):
+            self.second(colour, 0).start()
             self.first(colour).wait_recv()
             self.second(colour, 1).start()
 
@@ -340,129 +337,6 @@
             self.first(colour).wait_send()
             for k in range(2):
                 self.second(colour, k).wait_send()
-
-
-def last_kernel(
-    nz, chunk, part, weights, x_ref, ga_ref, gain_ref, gain_two, ffn_piece, gt, gains, summed, ffn,
-    total, accum, box, attn_piece, held, ss, rr, fs, fr, bs, br, near, far, far_last, reduce_sems,
-    gather_sems, ffn_sems,
-):
-    d = lax.axis_index("dp")
-    member = lax.rem(d, GROUP_DEVS)
-    masks = range(1, GROUP_DEVS)
-    greet(neighbours(nz) + plane(masks))
-    line = Line(nz, chunk, part, total, held, (ss, rr, fs, fr))
-    reduce = PlaneReduce(weights, None, near, far, far_last, reduce_sems)
-    gather = PlaneGather(attn_piece, summed, gather_sems)
-    gather_ffn = PlaneGather(ffn_piece, ffn, ffn_sems)
-    loop(0, line.count, line.issue)
-    reduce.start()
-    gather_ffn.start()
-    accum[...] = jnp.zeros_like(accum)
-    gain = gain_ref[...]
-    lag = 10
-    batch = 4
-
-    def body(s):
-        @pl.when(s < line.count)
-        def _():
-            line.service(s)
-
-        @pl.when(s >= lag)
-        def _():
-            line.ready(s - lag)
-
-        @pl.when((s >= lag) & (lax.rem(s - lag, batch) == batch - 1))
-        def _():
-            rows = line.batch((s - lag) // batch, batch)
-            x = x_ref[rows].astype(F32)
-            inverse = lax.rsqrt(jnp.mean(x * x, axis=-1, keepdims=True) + EPSILON)
-            upstream = total[rows].astype(F32)
-            inner = upstream * gain
-            through = inverse * inner - x * inverse**3 * jnp.mean(
-                inner * x, axis=-1, keepdims=True
-            )
-            gt[rows] = (ga_ref[rows].astype(F32) + through).astype(BF16)
-            accum[...] += fold_rows(upstream * x * inverse)
-
-        @pl.when(s == 5)
-        def _():
-            reduce.after_core()
-
-        @pl.when(s == 24)
-        def _():
-            gather_ffn.after_first()
-
-        @pl.when(s == 36)
-        def _():
-            reduce.after_first()
-
-        @pl.when(s == 50)
-        def _():
-            reduce.result(attn_piece)
-            gather.start()
-
-        @pl.when(s == 56)
-        def _():
-            gather_ffn.after_second()
-
-        @pl.when(s == 64)
-        def _():
-            gather.after_first()
-
-    loop(0, line.count + lag, body)
-    box[member, 0:1] = jnp.sum(accum[...], axis=0, keepdims=True)
-    box[member, 1:2] = gain_two[...]
-    copies = [
-        remote(box.at[member], box.at[member], bs.at[m], br.at[m], target)
-        for m, target in zip(masks, plane(masks))
-    ]
-    for copy in copies:
-        copy.start()
-    gather.after_second()
-    line.drain()
-    reduce.finish()
-    gather_ffn.finish()
-    gather.finish()
-    for copy in copies:
-        copy.wait()
-    result = box[0]
-    for m in masks:
-        result = result + box[m]
-    gains[...] = result
-
-
-def last_stage(nz, part, weights, x, ga, gain, gain_two, ffn_piece, chunk=16):
-    width = part.shape[1]
-    height = weights.shape[0] // GROUP_DEVS
-    return pl.pallas_call(
-        functools.partial(last_kernel, nz, chunk),
-        out_shape=(
-            jax.ShapeDtypeStruct(part.shape, BF16),
-            jax.ShapeDtypeStruct((2, width), F32),
-            jax.ShapeDtypeStruct(weights.shape, BF16),
-            jax.ShapeDtypeStruct((ffn_piece.shape[0] * GROUP_DEVS, ffn_piece.shape[1]), BF16),
-        ),
-        in_specs=[pl.BlockSpec(memory_space=VM)] * 7,
-        out_specs=(pl.BlockSpec(memory_space=VM),) * 2 + (pl.BlockSpec(memory_space=pl.ANY),) * 2,
-        scratch_shapes=[
-            VM(part.shape, BF16),
-            VM((8, width), F32),
-            VM((GROUP_DEVS, 2, width), F32),
-            VM((height, width), BF16),
-        ]
-        + line_scratch(part.shape, chunk)
-        + [pltpu.SemaphoreType.DMA((GROUP_DEVS,))] * 2
-        + reduce_scratch(height, width, False)
-        + [pltpu.SemaphoreType.DMA((2, 11))] * 2,
-        compiler_params=pltpu.CompilerParams(
-            collective_id=3, has_side_effects=True, vmem_limit_bytes=48 << 20
-        ),
-        cost_estimate=pl.CostEstimate(
-            flops=100_000_000_000, bytes_accessed=24_000_000, transcendentals=0
-        ),
-        name="last_stage",
-    )(part, weights, x, ga, gain, gain_two, ffn_piece)
 
 
 class LineGather:
@@ -688,21 +562,117 @@
     )(q, kv, w_out, bias)
 
 
-def backward_kernel(
-    nz, chunk, q_ref, kv_ref, kv_all, do_ref, bias_ref, lse_ref, inner_ref, feed, mid_ref, ffn,
-    dq, dkv_home, dkv_tail, act, ffn_piece,
-    dkv, near, far, ktok, vtok, total, held, ss, rr, fs, fr, ns, nr, ps, pr,
-    f_mine, f_near, f_far, f_last, f_sems,
+class Stream:
+    def __init__(self, rows, count, ins, out):
+        self.rows, self.count, self.ins, self.out = rows, count, ins, out
+
+    def load(self, i):
+        slot = lax.rem(i, 2)
+        return [
+            pltpu.make_async_copy(src.at[self.rows(i)], buf.at[slot], sem.at[slot])
+            for src, buf, sem in self.ins
+        ]
+
+    def store(self, i):
+        dst, buf, sem = self.out
+        slot = lax.rem(i, 2)
+        return pltpu.make_async_copy(buf.at[slot], dst.at[self.rows(i)], sem.at[slot])
+
+    def prime(self):
+        for i in range(2):
+            for copy in self.load(i):
+                copy.start()
+
+    def take(self, i):
+        for copy in self.load(i):
+            copy.wait()
+
+        @pl.when(i >= 2)
+        def _():
+            self.store(i - 2).wait()
+
+    def give(self, i):
+        self.store(i).start()
+
+        @pl.when(i + 2 < self.count)
+        def _():
+            for copy in self.load(i + 2):
+                copy.start()
+
+    def flush(self):
+        for i in range(self.count - 2, self.count):
+            self.store(i).wait()
+
+
+def tail_kernel(
+    nz, chunk, q_ref, kv_ref, do_ref, bias_ref, lse_ref, inner_ref, feed, cos_ref, sin_ref,
+    gain_ref, gain_two, kv_all, mid_hbm, ffn_hbm, normed_hbm, x_hbm, ga_hbm, wq_hbm, wk_hbm, wv_hbm,
+    gwo_hbm,
+    act, gt, gains, summed, ffn_sum,
+    kvs, wq, wk, wv, dq, dkv, near, far, ktok, vtok, low, total, held, f_piece, part, total_one, held_one, weights, a_near, a_far, a_last, a_piece, tile_in,
+    mid_in, act_out, x_in, ga_in, gt_out, accum, box,
+    ss, rr, fs, fr, ss1, rr1, fs1, fr1, ns, nr, ps, pr, a_sems, ag_sems, fg_sems, bs, br,
+    loads, kv_sem, m_sem, act_sem, x_sem, g_sem, gt_sem,
 ):
     heads = q_ref.shape[0]
     kvh = heads // 2
-    greet(neighbours(nz) + plane((1, 2, 4, 6)))
+    d, z = lax.axis_index("dp"), lax.axis_index("tensor")
+    member = lax.rem(d, GROUP_DEVS)
+    masks = range(1, GROUP_DEVS)
+    nq = heads * HEAD_DIM
+    nkv = kvh * HEAD_DIM
+    tokens, width = feed.shape
+    pairs = (
+        (wq_hbm, wq),
+        (wk_hbm, wk),
+        (wv_hbm, wv),
+        (gwo_hbm, weights.at[pl.ds(nq + 2 * nkv, gwo_hbm.shape[0])]),
+    )
+    fetches = [pltpu.make_async_copy(src, dst, loads.at[i]) for i, (src, dst) in enumerate(pairs)]
+
+    def kv_load(t):
+        slot = lax.rem(2 * t + 1 + t // 4, GROUP_DEVS)
+        return pltpu.make_async_copy(
+            kv_all.at[slot], kvs.at[lax.rem(t, 2)], kv_sem.at[lax.rem(t, 2)]
+        )
+
+    kv_load(0).start()
+    first_piece = pltpu.make_async_copy(ffn_hbm, f_piece, loads.at[len(pairs)])
+    first_piece.start()
+    batch = 4
     line = Line(nz, chunk, feed, total, held, (ss, rr, fs, fr))
-    reduce = PlaneReduce(ffn, f_mine, f_near, f_far, f_last, f_sems)
+    line_one = Line(
+        nz, chunk, part, total_one, held_one, (ss1, rr1, fs1, fr1), shift=tokens // chunk // 2
+    )
+    batches = line.count // batch
+    acts = Stream(
+        lambda i: line.batch(i, batch), batches, [(mid_hbm, mid_in, m_sem)], (act, act_out, act_sem)
+    )
+    outs = Stream(
+        lambda i: line_one.batch(i, batch),
+        batches,
+        [(x_hbm, x_in, x_sem), (ga_hbm, ga_in, g_sem)],
+        (gt, gt_out, gt_sem),
+    )
+    acts.prime()
+    greet(neighbours(nz) + plane(masks))
+    reduce_attn = PlaneReduce(
+        weights,
+        None,
+        lambda i: a_near.at[i],
+        lambda c, k: a_far.at[c, k],
+        lambda c: a_last.at[c],
+        a_sems,
+    )
+    gather_attn = PlaneGather(a_piece, summed, ag_sems)
+    gather_ffn = PlaneGather(f_piece, ffn_sum, fg_sems)
     loop(0, line.count, line.issue)
-    reduce.start()
+    first_piece.wait()
+    gather_ffn.start()
+    for copy in fetches:
+        copy.start()
     lag = 12
-    ply = 4
+    ply = 3
 
     def ripple(s):
         @pl.when(s < line.count)
@@ -713,35 +683,39 @@
         def _():
             line.ready(s - lag)
 
-        @pl.when((s >= lag) & (lax.rem(s - lag, ply) == ply - 1))
-        def _():
-            rows = line.batch((s - lag) // ply, ply)
-            act[rows] = (mid_ref[rows].astype(F32) + total[rows].astype(F32)).astype(BF16)
+        @pl.when((s >= lag) & (lax.rem(s - lag, batch) == batch - 1))
+        def _():
+            i = (s - lag) // batch
+            acts.take(i)
+            act_out[lax.rem(i, 2)] = (
+                mid_in[lax.rem(i, 2)].astype(F32) + total[line.batch(i, batch)].astype(F32)
+            ).astype(BF16)
+            acts.give(i)
 
     def background(s):
-        @pl.when(s == 3)
-        def _():
-            reduce.after_core()
-
-        @pl.when(s == 12)
-        def _():
-            reduce.after_first()
+        @pl.when(s == 4)
+        def _():
+            gather_ffn.after_first()
+
+        @pl.when(s == 11)
+        def _():
+            gather_ffn.after_second()
 
         loop(s * ply, s * ply + ply, ripple)
 
     dq[...] = jnp.zeros_like(dq)
 
-    def block(head, half, keyt, slot, mask, bias):
+    def block(head, half, keyt, mask, bias):
         h = head // 2
         cols = pl.ds(half * PB, PB)
-        s = dot(ktok[slot, h], q_ref[head, :, cols])
+        s = dot(ktok[h], q_ref[head, :, cols])
         if mask:
             s = causal(s)
         shift = lse_ref[head, :, cols]
         if bias is not None:
             shift = shift - bias
         p = jnp.exp2(s - shift)
-        dp = dot(vtok[slot, h], do_ref[head, :, cols])
+        dp = dot(vtok[h], do_ref[head, :, cols])
         ds = (p * (dp - inner_ref[head, :, cols])).astype(BF16)
         dq[head, :, cols] += dot(keyt, ds)
         dv = dot_nt(do_ref[head, :, cols], p.astype(BF16))
@@ -750,116 +724,286 @@
 
     def total_of(parts):
         out = parts[0]
-        for part in parts[1:]:
-            out = out + part
+        for piece in parts[1:]:
+            out = out + piece
         return out
 
+    def turn_back(u, half):
+        cols = pl.ds(half * PB, PB)
+        cosine, sine = cos_ref[:, cols], sin_ref[:, cols]
+        lower, upper = u[: HEAD_DIM // 2], u[HEAD_DIM // 2 :]
+        return lower * cosine + upper * sine, upper * cosine - lower * sine
+
+    def put_low(row, half, u, turned):
+        cols = pl.ds(half * PB, PB)
+        if not turned:
+            low[pl.ds(row, HEAD_DIM), cols] = u.astype(BF16)
+            return
+        first, second = turn_back(u, half)
+        low[pl.ds(row, HEAD_DIM // 2), cols] = first.astype(BF16)
+        low[pl.ds(row + HEAD_DIM // 2, HEAD_DIM // 2), cols] = second.astype(BF16)
+
     for h in range(kvh):
-        ktok[1, h] = kv_ref[h, :, PB : PB + CL].T
-        vtok[1, h] = kv_ref[kvh + h, :, PB : PB + CL].T
+        ktok[h] = kv_ref[h, :, PB : PB + CL].T
+        vtok[h] = kv_ref[kvh + h, :, PB : PB + CL].T
     for h in range(kvh):
-        pairs = [
-            block(2 * h + r, 1, kv_ref[h, :, PB : PB + CL], 1, True, None) for r in range(2)
-        ]
-        dkv_tail[h] = total_of([p[0] for p in pairs]) * (1.0 / LOG2E)
-        dkv_tail[kvh + h] = total_of([p[1] for p in pairs])
-
-    def slot_step(m, first, tick):
+        both = [block(2 * h + r, 1, kv_ref[h, :, PB : PB + CL], True, None) for r in range(2)]
+        put_low(nq + h * HEAD_DIM, 1, total_of([b[0] for b in both]) * (1.0 / LOG2E), True)
+        put_low(nq + nkv + h * HEAD_DIM, 1, total_of([b[1] for b in both]), False)
+
+    quarter = GROUP_DEVS // 2
+
+    def slot_step(t, where, first):
+        kv_load(t).wait()
+        now = lax.rem(t, 2)
         for h in range(kvh):
-            ktok[0, h] = kv_all[m, h].T
-            vtok[0, h] = kv_all[m, kvh + h].T
+            ktok[h] = kvs[now, h].T
+            vtok[h] = kvs[now, kvh + h].T
+        bias = None if first else bias_ref[lax.rem(2 * t + 1 + t // 4, GROUP_DEVS)]
         for h in range(kvh):
-            background(tick * 2 + h)
-            pairs = []
+            background(t * 2 + h)
+            both = []
             for r in range(2):
-                pairs.append(block(2 * h + r, 1, kv_all[m, h], 0, False, None))
-                pairs.append(
-                    block(2 * h + r, 0, kv_all[m, h], 0, first, None if first else bias_ref[m])
-                )
-            dkv[m, h] = (total_of([p[0] for p in pairs]) * (1.0 / LOG2E)).astype(BF16)
-            dkv[m, kvh + h] = total_of([p[1] for p in pairs]).astype(BF16)
+                both.append(block(2 * h + r, 1, kvs[now, h], False, None))
+                both.append(block(2 * h + r, 0, kvs[now, h], first, bias))
+            dkv[where, h] = (total_of([b[0] for b in both]) * (1.0 / LOG2E)).astype(BF16)
+            dkv[where, kvh + h] = total_of([b[1] for b in both]).astype(BF16)
 
     def to_near(i):
-        return remote(dkv.at[2 * i + 1], near.at[i], ns.at[i], nr.at[i], plane((1,))[0])
+        return remote(dkv.at[i], near.at[i], ns.at[i], nr.at[i], plane((1,))[0])
 
     def to_far(i):
-        return remote(near.at[i], far.at[i], ps.at[i], pr.at[i], plane((2 * i,))[0])
-
-    def odd(i):
-        slot_step(2 * i + 1, False, i)
-        to_near(i).start()
-
-    def even(i):
-        slot_step(2 * i, False, i + 3)
-        to_near(i).wait_recv()
-        near[i] = (dkv[2 * i].astype(F32) + near[i].astype(F32)).astype(BF16)
-        to_far(i).start()
-
-    quarter = GROUP_DEVS // 2
-    loop(0, quarter, odd)
-    loop(1, quarter, even)
-    slot_step(0, True, GROUP_DEVS - 1)
+        return remote(near.at[i], far.at[i], ps.at[i], pr.at[i], (jnp.bitwise_xor(d, 2 * i), z))
+
+    def step(t):
+        kv_load(t + 1).start()
+        slot_step(t, t - t // quarter * (t - quarter), False)
+
+        @pl.when(t < quarter)
+        def _():
+            to_near(t).start()
+
+        @pl.when(t >= quarter)
+        def _():
+            i = t - quarter + 1
+            to_near(i).wait_recv()
+            near[i] = (dkv[quarter].astype(F32) + near[i].astype(F32)).astype(BF16)
+            to_far(i).start()
+
+    last = GROUP_DEVS - 1
+    loop(0, last, step)
+    slot_step(last, quarter, True)
+
+    def back(j):
+        group = tokens // 4
+        rows = pl.ds(pl.multiple_of(j * group, group), group)
+        a = [low[pl.ds(at, n), rows].T for at, n in ((0, nq), (nq, nkv), (nq + nkv, nkv))]
+        size = 512
+        for t in range(width // size):
+            cols = pl.ds(t * size, size)
+            part[rows, cols] = (
+                dot_nt(a[0], wq[cols]) + dot_nt(a[1], wk[cols]) + dot_nt(a[2], wv[cols])
+            ).astype(BF16)
+
+    for copy in fetches:
+        copy.wait()
+    done = 2 * GROUP_DEVS * ply
+    left = line.count + lag - done
+    share = left // 4
+    half_count = line.count // 2
+    for head in range(heads):
+        put_low(head * HEAD_DIM, 1, dq[head, :, PB : PB + CL] * HEAD_DIM ** (-0.5), True)
+    loop(2, 4, back)
+    loop(0, half_count, line_one.issue)
+    loop(done, done + share, ripple)
+    for head in range(heads):
+        put_low(head * HEAD_DIM, 0, dq[head, :, 0:PB] * HEAD_DIM ** (-0.5), True)
     to_near(0).wait_recv()
-    dkv_home[...] = dkv[0].astype(F32) + near[0].astype(F32)
-    loop(2 * GROUP_DEVS * ply, line.count + lag, ripple)
-    reduce.result(ffn_piece)
     for i in range(1, quarter):
         to_far(i).wait_recv()
-        dkv_home[...] += far[i].astype(F32)
-    reduce.finish()
+    for h in range(2 * kvh):
+        home = dkv[quarter, h].astype(F32)
+        home = home + near[0, h].astype(F32)
+        for i in range(1, quarter):
+            home = home + far[i, h].astype(F32)
+        put_low(nq + h * HEAD_DIM, 0, home, h < kvh)
+    loop(0, 2, back)
+    loop(half_count, line.count, line_one.issue)
+    loop(done + share, done + 2 * share, ripple)
+    outs.prime()
+    size = tile_in.shape[1]
+    for t in range(width // size):
+        cols = pl.ds(t * size, size)
+        copy = pltpu.make_async_copy(normed_hbm.at[:, cols], tile_in, loads.at[len(pairs)])
+        copy.start()
+        copy.wait()
+        weights[0 : nq + 2 * nkv, cols] = dot(low[...], tile_in[...]).astype(BF16)
+    reduce_attn.start()
+    loop(done + 2 * share, done + left, ripple)
+    acts.flush()
+    accum[...] = jnp.zeros_like(accum)
+    gain = gain_ref[...]
+    lag_one = 10
+
+    def body(s):
+        @pl.when(s < line_one.count)
+        def _():
+            line_one.service(s)
+
+        @pl.when(s >= lag_one)
+        def _():
+            line_one.ready(s - lag_one)
+
+        @pl.when((s >= lag_one) & (lax.rem(s - lag_one, batch) == batch - 1))
+        def _():
+            i = (s - lag_one) // batch
+            outs.take(i)
+            slot = lax.rem(i, 2)
+            x = x_in[slot].astype(F32)
+            inverse = lax.rsqrt(jnp.mean(x * x, axis=-1, keepdims=True) + EPSILON)
+            upstream = total_one[line_one.batch(i, batch)].astype(F32)
+            inner = upstream * gain
+            through = inverse * inner - x * inverse**3 * jnp.mean(
+                inner * x, axis=-1, keepdims=True
+            )
+            gt_out[slot] = (ga_in[slot].astype(F32) + through).astype(BF16)
+            accum[...] += fold_rows(upstream * x * inverse)
+            outs.give(i)
+
+        @pl.when(s == 5)
+        def _():
+            reduce_attn.after_core()
+
+        @pl.when(s == 18)
+        def _():
+            reduce_attn.after_first()
+
+        @pl.when(s == 27)
+        def _():
+            reduce_attn.result(a_piece)
+            gather_attn.start()
+
+        @pl.when(s == 34)
+        def _():
+            gather_attn.after_first()
+
+        @pl.when(s == 46)
+        def _():
+            gather_attn.after_second()
+
+    loop(0, line_one.count + lag_one, body)
+    box[member, 0:1] = jnp.sum(accum[...], axis=0, keepdims=True)
+    box[member, 1:2] = gain_two[...]
+    copies = [
+        remote(box.at[member], box.at[member], bs.at[m], br.at[m], target)
+        for m, target in zip(masks, plane(masks))
+    ]
+    for copy in copies:
+        copy.start()
+    outs.flush()
     for i in range(quarter):
         to_near(i).wait_send()
     for i in range(1, quarter):
         to_far(i).wait_send()
     line.drain()
-
-
-def backward_attention(
-    nz, q, kv, kv_all, do, bias, lse, inner, feed, middle, ffn, chunk=16
+    line_one.drain()
+    reduce_attn.finish()
+    gather_ffn.finish()
+    gather_attn.finish()
+    for copy in copies:
+        copy.wait()
+    result = box[0]
+    for m in masks:
+        result = result + box[m]
+    gains[...] = result
+
+
+def tail_stage(
+    nz, q, kv, do, bias, lse, inner, feed, cosine, sine, gain, gain_two, kv_all, middle, ffn, normed,
+    x, ga, w_query, w_key, w_value, grad_w_out, chunk=16,
 ):
-    heads, tokens = q.shape[0], q.shape[2]
+    heads = q.shape[0]
     kvh = heads // 2
+    tokens, width = feed.shape
     slot = (2 * kvh, HEAD_DIM, PB)
+    n_attn = (heads + 2 * kvh) * HEAD_DIM + grad_w_out.shape[0]
+    high, wide = ffn.shape
+    low_high = n_attn // GROUP_DEVS
+    count = tokens // chunk
+    rows = 4 * chunk
+    quarter = GROUP_DEVS // 2
+    dma = lambda *shape: pltpu.SemaphoreType.DMA(shape)
+    lines = [dma(2, count)] * 3 + [dma(count)]
+    block = VM((2, rows, width), BF16)
+    anywhere = pl.BlockSpec(memory_space=pl.ANY)
+    vmem = pl.BlockSpec(memory_space=VM)
     return pl.pallas_call(
-        functools.partial(backward_kernel, nz, chunk),
+        functools.partial(tail_kernel, nz, chunk),
         out_shape=(
-            jax.ShapeDtypeStruct((heads, HEAD_DIM, tokens), F32),
-            jax.ShapeDtypeStruct(slot, F32),
-            jax.ShapeDtypeStruct((2 * kvh, HEAD_DIM, CL), F32),
             jax.ShapeDtypeStruct(feed.shape, BF16),
-            jax.ShapeDtypeStruct((ffn.shape[0] // GROUP_DEVS, ffn.shape[1]), BF16),
+            jax.ShapeDtypeStruct(feed.shape, BF16),
+            jax.ShapeDtypeStruct((2, width), F32),
+            jax.ShapeDtypeStruct((n_attn, width), BF16),
+            jax.ShapeDtypeStruct((high * GROUP_DEVS, wide), BF16),
         ),
-        in_specs=[pl.BlockSpec(memory_space=VM)] * 4
-        + [pl.BlockSpec(memory_space=pltpu.SMEM)]
-        + [pl.BlockSpec(memory_space=VM)] * 4
-        + [pl.BlockSpec(memory_space=pl.ANY)],
-        out_specs=(pl.BlockSpec(memory_space=VM),) * 5,
+        in_specs=[vmem] * 3 + [pl.BlockSpec(memory_space=pltpu.SMEM)] + [vmem] * 7 + [anywhere] * 10,
+        out_specs=(anywhere, anywhere, vmem, anywhere, anywhere),
         scratch_shapes=[
-            VM((GROUP_DEVS,) + slot, BF16),
-            VM((GROUP_DEVS // 2,) + slot, BF16),
-            VM((GROUP_DEVS // 2,) + slot, BF16),
-            VM((2, kvh, PB, HEAD_DIM), BF16),
-            VM((2, kvh, PB, HEAD_DIM), BF16),
+            VM((2,) + slot, BF16),
+            VM(w_query.shape, BF16),
+            VM(w_key.shape, BF16),
+            VM(w_value.shape, BF16),
+            VM((heads, HEAD_DIM, tokens), F32),
+            VM((quarter + 1,) + slot, BF16),
+            VM((quarter,) + slot, BF16),
+            VM((quarter,) + slot, BF16),
+            VM((kvh, PB, HEAD_DIM), BF16),
+            VM((kvh, PB, HEAD_DIM), BF16),
+            VM(((heads + 2 * kvh) * HEAD_DIM, tokens), BF16),
             VM(feed.shape, BF16),
+            VM(feed.shape, BF16),
+            VM((high, wide), BF16),
+            VM(feed.shape, BF16),
+            VM(feed.shape, BF16),
+            VM(feed.shape, BF16),
+            VM((n_attn, width), BF16),
+            VM((4, low_high, width), BF16),
+            VM((2, 2, low_high, width // 2), BF16),
+            VM((2, low_high, width // 2), BF16),
+            VM((low_high, width), BF16),
+            VM((tokens, 512), BF16),
+            block,
+            block,
+            block,
+            block,
+            block,
+            VM((8, width), F32),
+            VM((GROUP_DEVS, 2, width), F32),
         ]
-        + line_scratch(feed.shape, chunk)
-        + [pltpu.SemaphoreType.DMA((GROUP_DEVS // 2,))] * 4
-        + reduce_scratch(ffn.shape[0] // GROUP_DEVS, ffn.shape[1], True),
+        + lines * 2
+        + [dma(quarter)] * 4
+        + [dma(2, 11)] * 3
+        + [dma(GROUP_DEVS)] * 2
+        + [dma(5)]
+        + [dma(2)] * 6,
         compiler_params=pltpu.CompilerParams(
-            collective_id=1, has_side_effects=True, vmem_limit_bytes=56 << 20
+            collective_id=1, has_side_effects=True, vmem_limit_bytes=60 << 20
         ),
         cost_estimate=pl.CostEstimate(
-            flops=200_000_000_000, bytes_accessed=24_000_000, transcendentals=19_000_000
+            flops=200_000_000_000, bytes_accessed=50_000_000, transcendentals=19_000_000
         ),
-        name="backward_attention",
-    )(q, kv, kv_all, do, bias, lse, inner, feed, middle, ffn)
+        name="tail_stage",
+    )(
+        q, kv, do, bias, lse, inner, feed, cosine, sine, gain, gain_two, kv_all, middle, ffn, normed,
+        x, ga, w_query, w_key, w_value, grad_w_out,
+    )
 
 
 def middle_kernel(
     nz, chunk, att_hbm, wo_hbm, x_hbm, wg_hbm, wu_hbm, wd_hbm, cot_hbm, gain_ref,
-    ga, mid, feed, gatt, inner_out, gwo, gain_two, gffn,
+    ga, mid, feed, gatt, inner_out, gwo, gain_two, gffn, piece,
     att, wo, wg, wu, wd, cot, mid32, nt2, hidden, gg, gu, part, total, accum, stage, load, store,
-    held, ss, rr, fs, fr,
+    r_sems, spent, held, ss, rr, fs, fr,
 ):
     z = lax.axis_index("tensor")
     pairs = ((x_hbm, mid), (att_hbm, att), (wg_hbm, wg), (wu_hbm, wu), (cot_hbm, cot), (wd_hbm, wd))
@@ -877,7 +1021,7 @@
     loop(0, nz * GROUP_DEVS, wo_rows)
     for copy in loads[2:]:
         copy.start()
-    greet(neighbours(nz))
+    greet(neighbours(nz) + plane((1, 2, 4)))
     tokens, width = mid.shape
     ff = wg.shape[1]
     heads = own // HEAD_DIM
@@ -974,6 +1118,37 @@
 
     steps = tokens // group
     loop(0, steps, forward)
+    for target in plane((1, 2, 4)):
+        pl.semaphore_signal(spent, inc=1, device_id=target, device_id_type=MESH)
+    high, half = width // GROUP_DEVS, ff // 2
+
+    def rows_of(n):
+        return pl.ds(pl.multiple_of(n * high, 16), high)
+
+    def reduce_of(q):
+        src = gffn.at[:, pl.ds(q * ff, ff)]
+        own = stage.at[0, pl.ds(0, high), pl.ds(q * ff, ff)]
+        sems = r_sems.at[q]
+        if q < 2:
+            room = (wg, wu)[q]
+            return PlaneReduce(
+                src,
+                own,
+                lambda i: room.at[rows_of(i)],
+                lambda c, n: room.at[rows_of(4 + n), pl.ds(c * half, half)],
+                lambda c: room.at[rows_of(6), pl.ds(c * half, half)],
+                sems,
+            )
+        return PlaneReduce(
+            src,
+            own,
+            lambda i: wd.at[rows_of(i), pl.ds(0, ff)],
+            lambda c, n: wd.at[rows_of(2 * c + n), pl.ds(ff, half)],
+            lambda c: wd.at[rows_of(4), pl.ds(c * half, half)],
+            sems,
+        )
+
+    reduces = [reduce_of(q) for q in range(3)]
     done = 2 * steps - 3
     slabs = width // group
 
@@ -1002,14 +1177,32 @@
             tick(done + t // 2)
 
     loop(0, slabs, weights)
-    loop((done + slabs // 2) * ply, line.count + lag, ripple)
+    for t in (slabs - 2, slabs - 1):
+        put(t).wait()
+    pl.semaphore_wait(spent, 3)
+    for reduce in reduces:
+        reduce.start()
+    begin, end = (done + slabs // 2) * ply, line.count + lag
+    marks = (begin, begin + 9, begin + 32, end)
+    loop(marks[0], marks[1], ripple)
+    for reduce in reduces:
+        reduce.after_core()
+    loop(marks[1], marks[2], ripple)
+    for reduce in reduces:
+        reduce.after_first()
+    loop(marks[2], marks[3], ripple)
     for t in range(width // tile):
         cols = pl.ds(t * tile, tile)
         gwo[:, cols] = dot(att[mine], ga[:, cols]).astype(BF16)
     gain_two[...] = jnp.sum(accum[...], axis=0, keepdims=True)
-    for t in (slabs - 2, slabs - 1):
-        put(t).wait()
+    for q in range(3):
+        reduces[q].result(stage.at[1, pl.ds(0, high), pl.ds(q * ff, ff)])
+    out = pltpu.make_async_copy(stage.at[1, pl.ds(0, high)], piece, store.at[0])
+    out.start()
+    for reduce in reduces:
+        reduce.finish()
     line.drain()
+    out.wait()
 
 
 def middle_stage(nz, att_all, w_out_all, x, w_gate, w_up, w_down, cot, gain, chunk=16):
@@ -1030,9 +1223,10 @@
             jax.ShapeDtypeStruct((own, width), BF16),
             jax.ShapeDtypeStruct((1, width), F32),
             jax.ShapeDtypeStruct((width, 3 * ff), BF16),
+            jax.ShapeDtypeStruct((width // GROUP_DEVS, 3 * ff), BF16),
         ),
         in_specs=[pl.BlockSpec(memory_space=pl.ANY)] * 7 + [pl.BlockSpec(memory_space=VM)],
-        out_specs=(pl.BlockSpec(memory_space=VM),) * 7 + (pl.BlockSpec(memory_space=pl.ANY),),
+        out_specs=(pl.BlockSpec(memory_space=VM),) * 7 + (pl.BlockSpec(memory_space=pl.ANY),) * 2,
         scratch_shapes=[
             VM(w_out_all.shape[:1] + (tokens,), BF16),
             VM(w_out_all.shape, BF16),
@@ -1051,6 +1245,8 @@
             VM((2, group, 3 * ff), BF16),
             pltpu.SemaphoreType.DMA((7,)),
             pltpu.SemaphoreType.DMA((2,)),
+            pltpu.SemaphoreType.DMA((3, 2, 11)),
+            pltpu.SemaphoreType.REGULAR,
         ]
         + line_scratch((tokens, width), chunk),
         compiler_params=pltpu.CompilerParams(
@@ -1174,7 +1370,7 @@
     heads, kvh = queries.shape[0], keys.shape[0]
 
     att_all, kv_all, lse, w_out_all = forward_attention(nz, queries, kv, w_out, bias)
-    grad_attention, middle, feed_part, grad_attended, row_inner, grad_w_out, grad_gain_two, grad_ffn = (
+    grad_attention, middle, feed_part, grad_attended, row_inner, grad_w_out, grad_gain_two, _, ffn_piece = (
         middle_stage(
             nz,
             att_all.reshape(-1, count),
@@ -1187,43 +1383,29 @@
             mlp_gain[None],
         )
     )
-    grad_queries, grad_kv_prompt, grad_kv_tail, activations, ffn_piece = backward_attention(
+    activations, grad_tokens, gains, grad_attn, grad_ffn = tail_stage(
         nz,
         queries,
         kv,
-        kv_all,
         grad_attended.reshape(heads, HEAD_DIM, count),
         bias,
         lse,
         row_inner,
         feed_part,
+        cosine[0],
+        sine[0],
+        attn_gain[None],
+        grad_gain_two,
+        kv_all,
         middle,
-        grad_ffn,
-    )
-    grad_kv = jnp.concatenate([grad_kv_prompt, grad_kv_tail], axis=2)
-    grad_query_low = rotate(grad_queries * factor, cosine, -sine).astype(BF16).reshape(-1, count)
-    grad_key_low = rotate(grad_kv[:kvh], cosine, -sine).astype(BF16).reshape(-1, count)
-    grad_value_low = grad_kv[kvh:].astype(BF16).reshape(-1, count)
-
-    def back(grad, weight):
-        return lax.dot_general(grad, weight, (((0,), (1,)), ((), ())), preferred_element_type=F32)
-
-    partial_one = (
-        back(grad_query_low, w_query) + back(grad_key_low, w_key) + back(grad_value_low, w_value)
-    ).astype(BF16)
-    grads_low = jnp.concatenate([grad_query_low, grad_key_low, grad_value_low], axis=0)
-    grad_attn = jnp.concatenate(
-        [dot(grads_low, normed).astype(BF16), grad_w_out], axis=0
-    )
-    grad_tokens, gains, grad_attn, grad_ffn = last_stage(
-        nz,
-        partial_one,
-        grad_attn,
+        ffn_piece,
+        normed,
         tokens,
         grad_attention,
-        attn_gain[None],
-        grad_gain_two,
-        ffn_piece,
+        w_query,
+        w_key,
+        w_value,
+        grad_w_out,
     )
     if n_dp > GROUP_DEVS:
         gains = lax.psum(gains, "dp") * (1.0 / GROUP_DEVS)

time: 455 us -> 432 us (0.949)
  Pallas kernels: 417 us -> 401 us
  matrix products: 12.7 us -> 3.78 us
    pallas_call x2 -> x1, Pallas kernels: 206 us -> 186 us  [tail_stage(): pl.pallas_call(functools.partial(tail_kernel, nz, chunk), out_shape=(jax....]
    dot_general x4 -> x0, matrix products: 8.42 us -> none  [the longest x3 5.64 us: back(): lax.dot_general(grad, weight, (((0,), (1,)), ((), ())), preferred_element...]
    pallas_call x1, Pallas kernels: 114 us -> 119 us  [middle_stage(): pl.pallas_call(functools.partial(middle_kernel, nz, chunk), out_shape=(wi...]
    unnamed x55 -> x50, local copies, waits for them, and re-layouts: 7.31 us -> 12.3 us
where the time goes in v4:
time: 432 us; the launch traced here: 426 us
  Pallas kernels  401 us (93%)
  local copies, waits for them, and re-layouts  14.7 us (3%)
  other arithmetic  4.87 us (1%)
    pallas_call x1, Pallas kernels, tail_stage(): pl.pallas_call(functools.partial(tail_kernel, nz, chunk), out_shape=(jax....  186 us
    pallas_call x1, Pallas kernels, middle_stage(): pl.pallas_call(functools.partial(middle_kernel, nz, chunk), out_shape=(wi...  119 us
    pallas_call x1, Pallas kernels, forward_attention(): pl.pallas_call(functools.partial(forward_kernel, nz), out_shape=(jax.Shap...  82.3 us
    pallas_call x1, Pallas kernels, finish(): pl.pallas_call(functools.partial(finish_kernel, nq, nk), grid=(width // t...  13.9 us
    unnamed x50, local copies, waits for them, and re-layouts  12.3 us

profile of v4, /device:TPU:25, one launch (start us, length us, event | category | flops | bytes accessed | tf_op | source)
XLA Modules:
  0.0 425.9 jit_solution(17824803161714692113)
XLA Ops:
  0.6 0.0 copy-start
  0.7 0.0 copy-start.11
  0.7 0.0 copy-start.19
  0.7 0.6 copy-done
  1.3 0.6 gather_fusion
  2.0 0.8 multiply_cosine_fusion
  2.8 0.0 copy-start.13
  2.8 0.0 copy-start.14
  2.8 2.7 fusion
  5.6 0.0 copy-done.11
  5.6 0.0 copy-done.19
  5.6 0.0 copy-start.15
  5.6 0.8 fusion.2.normed_hbm
  6.4 0.3 copy-done.15
  6.6 1.2 fusion.6
  7.8 0.1 subtract_convert_fusion
  7.9 0.2 copy-done.17
  8.1 1.2 convolution_convert_fusion
  9.3 0.1 pad_maximum_fusion.kv_ref
  9.4 0.0 copy-done.12
  9.4 0.0 copy-done.23
  9.4 1.4 fusion.5
  10.8 0.0 copy-start.7
  10.9 0.0 copy-done.13
  10.9 0.0 copy-done.14
  10.9 0.2 multiply_subtract_fusion
  11.1 0.1 fusion.3.q_ref
  11.2 0.0 copy-start.6
  11.3 0.0 copy-done.5
  11.3 0.8 copy-done.7
  12.1 82.3 %forward_attention.1 = (bf16[4,384,1024]{2,1,0:T(8,128)(2,1)S(1)}, bf16[8,4,96,512]{3,2,1,0:T(8,128)(2,1)}, f32[4,1,1024]{2,1,0:T(1,128)S(1)}, bf16[1536,1536]{1,0:T(8,128)(2,1)}) custom-call(bf16[4,96,1024]{2,1,0:T(8,128)(2,1)S(1)} %fusion.3.q_ref, bf16[4,96,1024]{2,1,0:T(8,128)(2,1)S(1)} %pad_maximum_fusion.kv_ref, bf16[384,1536]{1,0:T(8,128)(2,1)S(1)} %copy-done.7, ...), custom_call_target="tpu_custom_call" | custom-call | flops 40000000000 | bytes 12000000 | tf_op jit(solution)/shard_map/forward_attention/pallas_call | solution.py:525
  94.4 0.0 copy-done.6
  94.5 0.0 copy-done.9
  94.5 0.0 copy-start.8
  94.5 1.7 copy-done.8
  96.1 0.6 copy-done.10
  96.7 0.0 copy-done.22
  96.7 0.6 broadcast_in_dim.23.gain_ref
  97.3 119.3 %middle_stage.1 = (bf16[1024,1536]{1,0:T(8,128)(2,1)}, bf16[1024,1536]{1,0:T(8,128)(2,1)}, bf16[1024,1536]{1,0:T(8,128)(2,1)}, bf16[384,1024]{1,0:T(8,128)(2,1)}...) custom-call(bf16[1536,1024]{1,0:T(8,128)(2,1)} %bitcast.25, ...), custom_call_target="tpu_custom_call" | custom-call | flops 99999997952 | bytes 50000000 | tf_op jit(solution)/shard_map/middle_stage/pallas_call | solution.py:1215
  216.7 1.2 copy.25.wk_hbm
  217.8 1.2 copy.26.wv_hbm
  219.0 0.6 broadcast_in_dim.24.gain_ref
  219.6 185.7 %tail_stage.1 = (bf16[1024,1536]{1,0:T(8,128)(2,1)}, bf16[1024,1536]{1,0:T(8,128)(2,1)}, f32[2,1536]{1,0:T(2,128)}, bf16[1152,1536]{1,0:T(8,128)(2,1)}, bf16[1536,3072]{1,0:T(8,128)(2,1)}) custom-call(bf16[4,96,1024]{2,1,0:T(8,128)(2,1)} %copy-done.6, bf16[4,96,1024]{2,1,0:T(8,128)(2,1)} %copy-done.5, bf16[4,96,1024]{2,1,0:T(8,128)(2,1)} %bitcast.33, ...), custom_call_target="tpu_custom_call" | custom-call | flops 199999995904 | bytes 50000000 | tf_op jit(solution)/shard_map/tail_stage/pallas_call | solution.py:940
  405.3 2.0 copy-done.2
  407.3 1.9 copy-done.3
  409.2 1.9 copy-done.4
  411.1 13.9 %finish.1 = (f32[1536,1024]{1,0:T(8,128)}, f32[1536,1024]{1,0:T(8,128)}, f32[1024,1536]{1,0:T(8,128)}, f32[1536,384]{1,0:T(8,128)}, f32[192,1536]{1,0:T(8,128)},...) custom-call(bf16[1536,3072]{1,0:T(8,128)(2,1)} %get-tuple-element.49.ffn, ...), custom_call_target="tpu_custom_call" | custom-call | tf_op jit(solution)/shard_map/finish/pallas_call | solution.py:1282
  425.0 0.6 slice_reduce_fusion
  (27 shorter events, 0.1 us)
Async XLA Ops:
  0.6 0.7 copy-start
  0.7 4.9 %copy-start.11 = (bf16[1024,1536]{1,0:T(8,128)(2,1)S(1)}, bf16[1024,1536]{1,0:T(8,128)(2,1)}, u32[]{:S(2)}) copy-start(bf16[1024,1536]{1,0:T(8,128)(2,1)} %x_hbm.3) | copy-start | bytes 9437188
  0.7 4.9 %copy-start.19 = (f32[1536]{0:T(1024)S(1)}, f32[1536]{0:T(1024)}, u32[]{:S(2)}) copy-start(f32[1536]{0:T(1024)} %param.14) | copy-start | bytes 18436
  2.8 8.0 %copy-start.13 = (f32[48,1024]{1,0:T(8,128)}, f32[48,1024]{1,0:T(8,128)S(1)}, u32[]{:S(2)}) copy-start(f32[48,1024]{1,0:T(8,128)S(1)} %get-tuple-element.69.cos_ref) | copy-start | bytes 589828
  2.8 8.0 %copy-start.14 = (f32[48,1024]{1,0:T(8,128)}, f32[48,1024]{1,0:T(8,128)S(1)}, u32[]{:S(2)}) copy-start(f32[48,1024]{1,0:T(8,128)S(1)} %get-tuple-element.70.sin_ref) | copy-start | bytes 589828
  5.6 1.1 copy-start.15
  6.6 2.7 copy-start.12
  6.6 1.5 copy-start.17
  8.1 1.3 copy-start.23
  9.4 1.9 copy-start.5
  10.8 1.3 copy-start.7
  11.2 83.2 %copy-start.6 = (bf16[4,96,1024]{2,1,0:T(8,128)(2,1)}, bf16[4,96,1024]{2,1,0:T(8,128)(2,1)S(1)}, u32[]{:S(2)}) copy-start(bf16[4,96,1024]{2,1,0:T(8,128)(2,1)S(1)} %fusion.3.q_ref) | copy-start | bytes 2359300
  12.1 82.3 %copy-start.9 = (f32[8]{0:T(128)}, f32[8]{0:T(128)S(1)}, u32[]{:S(2)}) copy-start(f32[8]{0:T(128)S(1)} %compare_select_fusion.1.bias_ref) | copy-start | bytes 100
  12.1 84.6 %copy-start.22 = (f32[1536]{0:T(1024)S(1)}, f32[1536]{0:T(1024)}, u32[]{:S(2)}) copy-start(f32[1536]{0:T(1024)} %param.19) | copy-start | bytes 18436
  94.5 1.7 copy-start.8
  96.1 0.6 copy-start.10
  97.3 119.3 %copy-start.16 = (bf16[1536,192]{0,1:T(8,128)(2,1)S(1)}, bf16[1536,192]{0,1:T(8,128)(2,1)}, u32[]{:S(2)}) copy-start(bf16[1536,192]{0,1:T(8,128)(2,1)} %param.16) | copy-start | bytes 1769476
  97.3 120.5 %copy-start.18 = (bf16[1536,192]{0,1:T(8,128)(2,1)S(1)}, bf16[1536,192]{0,1:T(8,128)(2,1)}, u32[]{:S(2)}) copy-start(bf16[1536,192]{0,1:T(8,128)(2,1)} %param.17) | copy-start | bytes 1769476
  97.3 121.6 %copy-start.20 = (f32[1536]{0:T(1024)S(1)}, f32[1536]{0:T(1024)}, u32[]{:S(2)}) copy-start(f32[1536]{0:T(1024)} %param.14) | copy-start | bytes 18436
  405.3 2.0 copy-start.2
  407.3 1.9 copy-start.3
  409.2 1.9 copy-start.4
  411.1 13.9 %copy-start.21 = (f32[2,1536]{1,0:T(2,128)S(1)}, f32[2,1536]{1,0:T(2,128)}, u32[]{:S(2)}) copy-start(f32[2,1536]{1,0:T(2,128)} %get-tuple-element.55) | copy-start | bytes 36868
  411.1 14.5 %copy-start.1 = (s32[1,8]{1,0:T(1,128)S(1)}, s32[1,8]{1,0:T(1,128)}, u32[]{:S(2)}) copy-start(s32[1,8]{1,0:T(1,128)} %param.13) | copy-start | bytes 100

commit v5 on v4

--- a/solution.py
+++ b/solution.py
@@ -381,8 +381,8 @@
 
 
 def forward_kernel(
-    nz, q_ref, kv_ref, wo_ref, bias_ref, att, kv_all, lse_ref, wo_all, acc, top, total, ktok, mine,
-    gs, gr, zs, zr, ws, wr, wp, load,
+    nz, q_ref, kv_ref, wo_ref, bias_ref, att_hbm, kv_hbm, lse_ref, wo_all, att, kv_all, acc, top, total, ktok, mine,
+    gs, gr, zs, zr, ws, wr, wp, load, leave,
 ):
     heads = q_ref.shape[0]
     kvh = heads // 2
@@ -487,6 +487,13 @@
         )
         for half in range(2)
     ]
+    kv_out = pltpu.make_async_copy(kv_all, kv_hbm, leave.at[2])
+    kv_out.start()
+
+    def att_out(half):
+        there = (slice(None), slice(None), pl.ds(half * PB, PB))
+        return pltpu.make_async_copy(att.at[there], att_hbm.at[there], leave.at[half])
+
     finish(1)
     lines[1].start(0)
     slot_step(0, 0, mask=True)
@@ -507,8 +514,9 @@
         lines[1].start(s)
     for s in range(1, nz - 1):
         lines[0].start(s)
-    for line in lines:
-        line.last()
+    for half in (1, 0):
+        lines[half].last()
+        att_out(half).start()
     for line in lines + [w_line]:
         line.drain()
     w_plane.finish()
@@ -516,6 +524,9 @@
         copy.wait_send()
     for m in (2, 4, 6):
         hand_on(m).wait_send()
+    kv_out.wait()
+    for half in range(2):
+        att_out(half).wait()
 
 
 def forward_attention(nz, q, kv, w_out, bias):
@@ -536,8 +547,15 @@
             pl.BlockSpec(memory_space=pl.ANY),
             pl.BlockSpec(memory_space=pltpu.SMEM),
         ],
-        out_specs=(pl.BlockSpec(memory_space=VM),) * 3 + (pl.BlockSpec(memory_space=pl.ANY),),
+        out_specs=(
+            pl.BlockSpec(memory_space=pl.ANY),
+            pl.BlockSpec(memory_space=pl.ANY),
+            pl.BlockSpec(memory_space=VM),
+            pl.BlockSpec(memory_space=pl.ANY),
+        ),
         scratch_shapes=[
+            VM((nz, heads * HEAD_DIM, tokens), BF16),
+            VM((GROUP_DEVS, 2 * kvh, HEAD_DIM, PB), BF16),
             VM((heads, HEAD_DIM, tokens), F32),
             VM((heads, 1, tokens), F32),
             VM((heads, 1, tokens), F32),
@@ -551,9 +569,10 @@
             pltpu.SemaphoreType.DMA((2, nz - 1)),
             pltpu.SemaphoreType.DMA((2, 11)),
             pltpu.SemaphoreType.DMA((1,)),
+            pltpu.SemaphoreType.DMA((3,)),
         ],
         compiler_params=pltpu.CompilerParams(
-            collective_id=0, has_side_effects=True, vmem_limit_bytes=48 << 20
+            collective_id=0, has_side_effects=True, vmem_limit_bytes=60 << 20
         ),
         cost_estimate=pl.CostEstimate(
             flops=40_000_000_000, bytes_accessed=12_000_000, transcendentals=19_000_000
@@ -672,7 +691,7 @@
     for copy in fetches:
         copy.start()
     lag = 12
-    ply = 3
+    ply = 2
 
     def ripple(s):
         @pl.when(s < line.count)
@@ -693,11 +712,11 @@
             acts.give(i)
 
     def background(s):
-        @pl.when(s == 4)
+        @pl.when(s == 8)
         def _():
             gather_ffn.after_first()
 
-        @pl.when(s == 11)
+        @pl.when(s == 22)
         def _():
             gather_ffn.after_second()
 
@@ -761,9 +780,9 @@
             vtok[h] = kvs[now, kvh + h].T
         bias = None if first else bias_ref[lax.rem(2 * t + 1 + t // 4, GROUP_DEVS)]
         for h in range(kvh):
-            background(t * 2 + h)
             both = []
             for r in range(2):
+                background(t * 4 + h * 2 + r)
                 both.append(block(2 * h + r, 1, kvs[now, h], False, None))
                 both.append(block(2 * h + r, 0, kvs[now, h], first, bias))
             dkv[where, h] = (total_of([b[0] for b in both]) * (1.0 / LOG2E)).astype(BF16)
@@ -802,12 +821,12 @@
         for t in range(width // size):
             cols = pl.ds(t * size, size)
             part[rows, cols] = (
-                dot_nt(a[0], wq[cols]) + dot_nt(a[1], wk[cols]) + dot_nt(a[2], wv[cols])
+                dot_nt(a[0], wq[cols]) + dot(a[1], wk[:, cols]) + dot(a[2], wv[:, cols])
             ).astype(BF16)
 
     for copy in fetches:
         copy.wait()
-    done = 2 * GROUP_DEVS * ply
+    done = 4 * GROUP_DEVS * ply
     left = line.count + lag - done
     share = left // 4
     half_count = line.count // 2
@@ -832,13 +851,19 @@
     loop(done + share, done + 2 * share, ripple)
     outs.prime()
     size = tile_in.shape[1]
-    for t in range(width // size):
-        cols = pl.ds(t * size, size)
-        copy = pltpu.make_async_copy(normed_hbm.at[:, cols], tile_in, loads.at[len(pairs)])
-        copy.start()
-        copy.wait()
-        weights[0 : nq + 2 * nkv, cols] = dot(low[...], tile_in[...]).astype(BF16)
-    reduce_attn.start()
+
+    def tile_load(t):
+        return pltpu.make_async_copy(
+            normed_hbm.at[:, pl.ds(t * size, size)], tile_in, loads.at[len(pairs)]
+        )
+
+    def tile_step(t):
+        tile_load(t).wait()
+        weights[0 : nq + 2 * nkv, pl.ds(t * size, size)] = dot(low[...], tile_in[...]).astype(BF16)
+        if t + 1 < width // size:
+            tile_load(t + 1).start()
+
+    tile_load(0).start()
     loop(done + 2 * share, done + left, ripple)
     acts.flush()
     accum[...] = jnp.zeros_like(accum)
@@ -870,24 +895,34 @@
             accum[...] += fold_rows(upstream * x * inverse)
             outs.give(i)
 
-        @pl.when(s == 5)
+        for t in range(width // size):
+
+            @pl.when(s == 4 + 5 * t)
+            def _():
+                tile_step(t)
+
+        @pl.when(s == 15)
+        def _():
+            reduce_attn.start()
+
+        @pl.when(s == 19)
         def _():
             reduce_attn.after_core()
 
-        @pl.when(s == 18)
+        @pl.when(s == 31)
         def _():
             reduce_attn.after_first()
 
-        @pl.when(s == 27)
+        @pl.when(s == 39)
         def _():
             reduce_attn.result(a_piece)
             gather_attn.start()
 
-        @pl.when(s == 34)
+        @pl.when(s == 46)
         def _():
             gather_attn.after_first()
 
-        @pl.when(s == 46)
+        @pl.when(s == 58)
         def _():
             gather_attn.after_second()
 
@@ -1001,12 +1036,24 @@
 
 def middle_kernel(
     nz, chunk, att_hbm, wo_hbm, x_hbm, wg_hbm, wu_hbm, wd_hbm, cot_hbm, gain_ref,
-    ga, mid, feed, gatt, inner_out, gwo, gain_two, gffn, piece,
-    att, wo, wg, wu, wd, cot, mid32, nt2, hidden, gg, gu, part, total, accum, stage, load, store,
-    r_sems, spent, held, ss, rr, fs, fr,
+    gatt, inner_out, gwo, gain_two, ga_hbm, mid_hbm, feed_hbm, gffn, piece,
+    ga, mid, feed, att, wo, wg, wu, wd, cot, mid32, nt2, hidden, gg, gu, part, total, accum, stage,
+    load, store, leave, r_sems, spent, held, ss, rr, fs, fr,
 ):
     z = lax.axis_index("tensor")
-    pairs = ((x_hbm, mid), (att_hbm, att), (wg_hbm, wg), (wu_hbm, wu), (cot_hbm, cot), (wd_hbm, wd))
+    group, slab = 256, 256
+    tokens, width = mid.shape
+    head, rest = pl.ds(0, group), pl.ds(group, tokens - group)
+    pairs = (
+        (x_hbm.at[head], mid.at[head]),
+        (att_hbm.at[:, head], att.at[:, head]),
+        (wg_hbm, wg),
+        (wu_hbm, wu),
+        (cot_hbm, cot),
+        (wd_hbm, wd),
+        (x_hbm.at[rest], mid.at[rest]),
+        (att_hbm.at[:, rest], att.at[:, rest]),
+    )
     loads = [pltpu.make_async_copy(src, dst, load.at[i]) for i, (src, dst) in enumerate(pairs)]
     own = gatt.shape[0]
     some = own // GROUP_DEVS
@@ -1022,10 +1069,8 @@
     for copy in loads[2:]:
         copy.start()
     greet(neighbours(nz) + plane((1, 2, 4)))
-    tokens, width = mid.shape
     ff = wg.shape[1]
     heads = own // HEAD_DIM
-    group = 256
     per = group // chunk
     ply = 4
     quarters = per // ply
@@ -1036,6 +1081,11 @@
     mine = pl.ds(pl.multiple_of(z * own, own), own)
     lag = 12
 
+    def out_of(n, g):
+        src, dst = ((mid, mid_hbm), (feed, feed_hbm), (ga, ga_hbm))[n]
+        rows = pl.ds(pl.multiple_of(g * group, group), group)
+        return pltpu.make_async_copy(src.at[rows], dst.at[rows], leave.at[n, g])
+
     def settle(c):
         rows = line.batch(c, ply)
         m = mid[rows].astype(F32)
@@ -1048,6 +1098,7 @@
 
         @pl.when(lax.rem(c, quarters) == quarters - 1)
         def _():
+            out_of(2, c // quarters).start()
             block = pl.ds(pl.multiple_of((c // quarters) * group, group), group)
             back = dot_nt(wo[mine], ga[block])
             gatt[:, block] = back.astype(BF16)
@@ -1081,6 +1132,11 @@
     pltpu.make_async_copy(wo_hbm, wo, load.at[len(pairs)]).wait()
 
     def forward(j):
+        @pl.when(j == 1)
+        def _():
+            for copy in loads[6:]:
+                copy.wait()
+
         rows = pl.ds(pl.multiple_of(j * group, group), group)
         a = att[:, rows].T
         for t in range(width // tile):
@@ -1093,7 +1149,7 @@
 
         @pl.when(j == 0)
         def _():
-            for copy in loads[2:]:
+            for copy in loads[2:6]:
                 copy.wait()
 
         tick(2 * j - 3)
@@ -1114,6 +1170,8 @@
         for t in range(width // tile):
             cols = pl.ds(t * tile, tile)
             feed[rows, cols] = dot(hidden[rows], wd[:, cols]).astype(BF16)
+        out_of(0, j).start()
+        out_of(1, j).start()
         tick(2 * j - 2)
 
     steps = tokens // group
@@ -1150,12 +1208,12 @@
 
     reduces = [reduce_of(q) for q in range(3)]
     done = 2 * steps - 3
-    slabs = width // group
+    slabs = width // slab
 
     def put(t):
         return pltpu.make_async_copy(
             stage.at[lax.rem(t, 2)],
-            gffn.at[pl.ds(pl.multiple_of(t * group, group), group)],
+            gffn.at[pl.ds(pl.multiple_of(t * slab, slab), slab)],
             store.at[lax.rem(t, 2)],
         )
 
@@ -1165,7 +1223,7 @@
             put(t - 2).wait()
 
         slot = lax.rem(t, 2)
-        cols = pl.ds(pl.multiple_of(t * group, group), group)
+        cols = pl.ds(pl.multiple_of(t * slab, slab), slab)
         a = nt2[:, cols].T
         stage[slot, :, 0:ff] = dot(a, gg[...]).astype(BF16)
         stage[slot, :, ff : 2 * ff] = dot(a, gu[...]).astype(BF16)
@@ -1203,6 +1261,8 @@
         reduce.finish()
     line.drain()
     out.wait()
+    for n in range(3):
+        loop(0, steps, lambda g, n=n: out_of(n, g).wait())
 
 
 def middle_stage(nz, att_all, w_out_all, x, w_gate, w_up, w_down, cot, gain, chunk=16):
@@ -1210,24 +1270,27 @@
     ff = w_gate.shape[1]
     own = w_out_all.shape[0] // nz
     heads = own // HEAD_DIM
-    group = 256
+    group, slab = 256, 256
     wide = jax.ShapeDtypeStruct((tokens, width), BF16)
     return pl.pallas_call(
         functools.partial(middle_kernel, nz, chunk),
         out_shape=(
-            wide,
-            wide,
-            wide,
             jax.ShapeDtypeStruct((own, tokens), BF16),
             jax.ShapeDtypeStruct((heads, 1, tokens), F32),
             jax.ShapeDtypeStruct((own, width), BF16),
             jax.ShapeDtypeStruct((1, width), F32),
+            wide,
+            wide,
+            wide,
             jax.ShapeDtypeStruct((width, 3 * ff), BF16),
             jax.ShapeDtypeStruct((width // GROUP_DEVS, 3 * ff), BF16),
         ),
         in_specs=[pl.BlockSpec(memory_space=pl.ANY)] * 7 + [pl.BlockSpec(memory_space=VM)],
-        out_specs=(pl.BlockSpec(memory_space=VM),) * 7 + (pl.BlockSpec(memory_space=pl.ANY),) * 2,
+        out_specs=(pl.BlockSpec(memory_space=VM),) * 4 + (pl.BlockSpec(memory_space=pl.ANY),) * 5,
         scratch_shapes=[
+            VM((tokens, width), BF16),
+            VM((tokens, width), BF16),
+            VM((tokens, width), BF16),
             VM(w_out_all.shape[:1] + (tokens,), BF16),
             VM(w_out_all.shape, BF16),
             VM((width, ff), BF16),
@@ -1242,9 +1305,10 @@
             VM((tokens, width), BF16),
             VM((tokens, width), BF16),
             VM((8, width), F32),
-            VM((2, group, 3 * ff), BF16),
-            pltpu.SemaphoreType.DMA((7,)),
+            VM((2, slab, 3 * ff), BF16),
+            pltpu.SemaphoreType.DMA((9,)),
             pltpu.SemaphoreType.DMA((2,)),
+            pltpu.SemaphoreType.DMA((3, tokens // group)),
             pltpu.SemaphoreType.DMA((3, 2, 11)),
             pltpu.SemaphoreType.REGULAR,
         ]
@@ -1305,7 +1369,7 @@
             side(tokens),
             side(tokens),
         ),
-        compiler_params=pltpu.CompilerParams(vmem_limit_bytes=40 << 20),
+        compiler_params=pltpu.CompilerParams(vmem_limit_bytes=60 << 20),
         name="finish",
     )(ffn, attn, gt, act)
 
@@ -1370,7 +1434,7 @@
     heads, kvh = queries.shape[0], keys.shape[0]
 
     att_all, kv_all, lse, w_out_all = forward_attention(nz, queries, kv, w_out, bias)
-    grad_attention, middle, feed_part, grad_attended, row_inner, grad_w_out, grad_gain_two, _, ffn_piece = (
+    grad_attended, row_inner, grad_w_out, grad_gain_two, grad_attention, middle, feed_part, _, ffn_piece = (
         middle_stage(
             nz,
             att_all.reshape(-1, count),
@@ -1403,8 +1467,8 @@
         tokens,
         grad_attention,
         w_query,
-        w_key,
-        w_value,
+        w_key.T,
+        w_value.T,
         grad_w_out,
     )
     if n_dp > GROUP_DEVS:

time: 432 us -> 420 us (0.972)
  local copies, waits for them, and re-layouts: 14.7 us -> 3.56 us
    unnamed x50 -> x26, local copies, waits for them, and re-layouts: 12.3 us -> 1.09 us
    pallas_call x1, Pallas kernels: 119 us -> 114 us  [middle_stage(): pl.pallas_call(functools.partial(middle_kernel, nz, chunk), out_shape=(ja...]
    pallas_call x1, Pallas kernels: 13.9 us -> 18.5 us  [finish(): pl.pallas_call(functools.partial(finish_kernel, nq, nk), grid=(width // t...]
where the time goes in v5:
time: 420 us; the launch traced here: 414 us
  Pallas kernels  398 us (95%)
  other arithmetic  7.12 us (2%)
    pallas_call x1, Pallas kernels, tail_stage(): pl.pallas_call(functools.partial(tail_kernel, nz, chunk), out_shape=(jax....  182 us
    pallas_call x1, Pallas kernels, middle_stage(): pl.pallas_call(functools.partial(middle_kernel, nz, chunk), out_shape=(ja...  114 us
    pallas_call x1, Pallas kernels, forward_attention(): pl.pallas_call(functools.partial(forward_kernel, nz), out_shape=(jax.Shap...  82.9 us
    pallas_call x1, Pallas kernels, finish(): pl.pallas_call(functools.partial(finish_kernel, nq, nk), grid=(width // t...  18.5 us

profile of v5, /device:TPU:25, one launch (start us, length us, event | category | flops | bytes accessed | tf_op | source)
XLA Modules:
  0.0 413.6 jit_solution(16271155579943636499)
XLA Ops:
  0.6 0.0 copy-start
  0.7 0.0 copy-start.2
  0.7 0.0 copy-start.6
  0.7 0.6 copy-done
  1.3 0.6 gather_fusion
  2.0 0.8 multiply_cosine_fusion
  2.8 0.0 copy-start.4
  2.8 0.0 copy-start.5
  2.8 2.7 fusion
  5.6 0.0 copy-done.2
  5.6 0.0 copy-done.6
  5.6 0.0 copy-start.12
  5.6 0.8 fusion.2.normed_hbm
  6.4 0.3 copy-done.12
  6.6 0.0 copy-start.3
  6.6 0.0 copy-start.11
  6.6 1.2 fusion.6
  7.8 0.1 subtract_convert_fusion
  7.9 0.2 copy-done.11
  8.1 0.0 copy-start.10
  8.1 1.2 convolution_convert_fusion
  9.3 0.9 pad_maximum_fusion.kv_ref
  10.2 0.0 copy-done.3
  10.2 0.0 copy-done.10
  10.2 1.5 fusion.5
  11.7 0.0 copy-done.4
  11.7 0.0 copy-done.5
  11.7 0.2 multiply_subtract_fusion
  11.9 1.0 fusion.3.q_ref
  12.9 0.5 compare_select_fusion.1.bias_ref
  13.5 0.0 copy-start.9
  13.5 82.9 %forward_attention.1 = (bf16[4,384,1024]{2,1,0:T(8,128)(2,1)}, bf16[8,4,96,512]{3,2,1,0:T(8,128)(2,1)}, f32[4,1,1024]{2,1,0:T(1,128)}, bf16[1536,1536]{1,0:T(8,128)(2,1)}) custom-call(bf16[4,96,1024]{2,1,0:T(8,128)(2,1)} %fusion.3.q_ref, bf16[4,96,1024]{2,1,0:T(8,128)(2,1)} %pad_maximum_fusion.kv_ref, bf16[384,1536]{1,0:T(8,128)(2,1)} %wo_ref.1, ...), custom_call_target="tpu_custom_call" | custom-call | flops 40000000000 | bytes 12000000 | tf_op jit(solution)/shard_map/forward_attention/pallas_call | solution.py:536
  96.4 0.0 copy-done.9
  96.4 0.6 broadcast_in_dim.23.gain_ref
  97.0 0.0 copy-start.7
  97.0 114.5 %middle_stage.1 = (bf16[384,1024]{1,0:T(8,128)(2,1)}, f32[4,1,1024]{2,1,0:T(1,128)}, bf16[384,1536]{1,0:T(8,128)(2,1)}, f32[1,1536]{1,0:T(1,128)}, bf16[1024,153...) custom-call(bf16[1536,1024]{1,0:T(8,128)(2,1)} %bitcast.36, ...), custom_call_target="tpu_custom_call" | custom-call | flops 99999997952 | bytes 50000000 | tf_op jit(solution)/shard_map/middle_stage/pallas_call | solution.py:1275
  211.5 0.0 copy-done.7
  211.5 0.6 broadcast_in_dim.24.gain_ref
  212.1 181.9 %tail_stage.1 = (bf16[1024,1536]{1,0:T(8,128)(2,1)}, bf16[1024,1536]{1,0:T(8,128)(2,1)}, f32[2,1536]{1,0:T(2,128)}, bf16[1152,1536]{1,0:T(8,128)(2,1)}, bf16[1536,3072]{1,0:T(8,128)(2,1)}) custom-call(bf16[4,96,1024]{2,1,0:T(8,128)(2,1)} %fusion.3.q_ref, bf16[4,96,1024]{2,1,0:T(8,128)(2,1)} %pad_maximum_fusion.kv_ref, bf16[4,96,1024]{2,1,0:T(8,128)(2,1)} %bitcast.37, ...), custom_call_target="tpu_custom_call" | custom-call | flops 199999995904 | bytes 50000000 | tf_op jit(solution)/shard_map/tail_stage/pallas_call | solution.py:975
  394.0 0.0 copy-start.8
  394.0 0.0 copy-start.1
  394.0 18.5 %finish.1 = (f32[1536,1024]{1,0:T(8,128)}, f32[1536,1024]{1,0:T(8,128)}, f32[1024,1536]{1,0:T(8,128)}, f32[1536,384]{1,0:T(8,128)}, f32[192,1536]{1,0:T(8,128)},...) custom-call(bf16[1536,3072]{1,0:T(8,128)(2,1)} %get-tuple-element.49.ffn, ...), custom_call_target="tpu_custom_call" | custom-call | tf_op jit(solution)/shard_map/finish/pallas_call | solution.py:1346
  412.5 0.0 copy-done.8
  412.5 0.6 slice_reduce_fusion
  413.1 0.0 copy-done.1
  (6 shorter events, 0.0 us)
Async XLA Ops:
  0.6 0.7 copy-start
  0.7 4.9 %copy-start.2 = (bf16[1024,1536]{1,0:T(8,128)(2,1)S(1)}, bf16[1024,1536]{1,0:T(8,128)(2,1)}, u32[]{:S(2)}) copy-start(bf16[1024,1536]{1,0:T(8,128)(2,1)} %x_hbm.3) | copy-start | bytes 9437188
  0.7 4.9 %copy-start.6 = (f32[1536]{0:T(1024)S(1)}, f32[1536]{0:T(1024)}, u32[]{:S(2)}) copy-start(f32[1536]{0:T(1024)} %param.14) | copy-start | bytes 18436
  2.8 8.9 %copy-start.4 = (f32[48,1024]{1,0:T(8,128)}, f32[48,1024]{1,0:T(8,128)S(1)}, u32[]{:S(2)}) copy-start(f32[48,1024]{1,0:T(8,128)S(1)} %get-tuple-element.69.cos_ref) | copy-start | bytes 589828
  2.8 8.9 %copy-start.5 = (f32[48,1024]{1,0:T(8,128)}, f32[48,1024]{1,0:T(8,128)S(1)}, u32[]{:S(2)}) copy-start(f32[48,1024]{1,0:T(8,128)S(1)} %get-tuple-element.70.sin_ref) | copy-start | bytes 589828
  5.6 1.1 copy-start.12
  6.6 3.6 copy-start.3
  6.6 1.5 copy-start.11
  8.1 2.1 copy-start.10
  13.5 82.9 %copy-start.9 = (f32[1536]{0:T(1024)S(1)}, f32[1536]{0:T(1024)}, u32[]{:S(2)}) copy-start(f32[1536]{0:T(1024)} %param.19) | copy-start | bytes 18436
  97.0 114.5 %copy-start.7 = (f32[1536]{0:T(1024)S(1)}, f32[1536]{0:T(1024)}, u32[]{:S(2)}) copy-start(f32[1536]{0:T(1024)} %param.14) | copy-start | bytes 18436
  394.0 18.5 %copy-start.8 = (f32[2,1536]{1,0:T(2,128)S(1)}, f32[2,1536]{1,0:T(2,128)}, u32[]{:S(2)}) copy-start(f32[2,1536]{1,0:T(2,128)} %get-tuple-element.55) | copy-start | bytes 36868
  394.0 19.1 %copy-start.1 = (s32[1,8]{1,0:T(1,128)S(1)}, s32[1,8]{1,0:T(1,128)}, u32[]{:S(2)}) copy-start(s32[1,8]{1,0:T(1,128)} %param.13) | copy-start | bytes 100

commit v6 on v5

--- a/solution.py
+++ b/solution.py
@@ -381,8 +381,10 @@
 
 
 def forward_kernel(
-    nz, q_ref, kv_ref, wo_ref, bias_ref, att_hbm, kv_hbm, lse_ref, wo_all, att, kv_all, acc, top, total, ktok, mine,
-    gs, gr, zs, zr, ws, wr, wp, load, leave,
+    nz, x_hbm, wq_hbm, wk_hbm, wv_hbm, cos_ref, sin_ref, gain_ref, wo_ref, bias_ref,
+    q_ref, kv_ref, normed_hbm, att_hbm, kv_hbm, lse_ref, wo_all,
+    x_in, normed, wq, wk, wv, att, kv_all, acc, top, total, ktok, mine,
+    gs, gr, zs, zr, ws, wr, wp, load, leave, fetch, keep,
 ):
     heads = q_ref.shape[0]
     kvh = heads // 2
@@ -397,6 +399,57 @@
         wo_ref.at[pl.ds(pl.multiple_of(member * some, 16), some)], own_place(z), load.at[0]
     )
     first_rows.start()
+    tokens = x_in.shape[0]
+    group = 256
+    groups = tokens // group
+
+    def rows_of(j):
+        return pl.ds(pl.multiple_of(j * group, group), group)
+
+    x_loads = [
+        pltpu.make_async_copy(x_hbm.at[rows_of(j)], x_in.at[rows_of(j)], fetch.at[j])
+        for j in range(groups)
+    ]
+    w_loads = [
+        pltpu.make_async_copy(src, dst, fetch.at[groups + n])
+        for n, (src, dst) in enumerate(((wk_hbm, wk), (wv_hbm, wv), (wq_hbm, wq)))
+    ]
+    for copy in x_loads[:2] + w_loads[:2] + x_loads[2:] + w_loads[2:]:
+        copy.start()
+
+    def normed_out(j):
+        return pltpu.make_async_copy(
+            normed.at[rows_of(j)], normed_hbm.at[rows_of(j)], keep.at[j]
+        )
+
+    def turn(u, cols):
+        half = HEAD_DIM // 2
+        lower, upper = u[:half], u[half:]
+        cosine, sine = cos_ref[:, cols], sin_ref[:, cols]
+        return lower * cosine - upper * sine, upper * cosine + lower * sine
+
+    def put_turned(ref, n, u, cols, scale):
+        first, second = turn(u, cols)
+        half = HEAD_DIM // 2
+        ref[n, 0:half, cols] = (first * scale).astype(BF16)
+        ref[n, half:HEAD_DIM, cols] = (second * scale).astype(BF16)
+
+    def keys_values(j):
+        cols = rows_of(j)
+        x = x_in[cols].astype(F32)
+        inverse = lax.rsqrt(jnp.mean(x * x, axis=-1, keepdims=True) + EPSILON)
+        n = (x * inverse * gain_ref[...]).astype(BF16)
+        normed[cols] = n
+        normed_out(j).start()
+        keys, values = dot_nt(wk[...], n), dot_nt(wv[...], n)
+        for h in range(kvh):
+            some = slice(h * HEAD_DIM, (h + 1) * HEAD_DIM)
+            put_turned(kv_ref, h, keys[some], cols, 1.0)
+            kv_ref[kvh + h, :, cols] = values[some].astype(BF16)
+
+    for copy in x_loads[:2] + w_loads[:2]:
+        copy.wait()
+    loop(0, groups // 2, keys_values)
     greet(plane((1, 2, 4, 6)) + neighbours(nz))
     own = kv_ref.at[:, :, pl.ds(0, PB)]
     firsts = [
@@ -409,6 +462,20 @@
     w_plane = PlaneGather(mine, wo_all, wp)
     first_rows.wait()
     w_line.start(0)
+    for copy in x_loads[2:] + w_loads[2:]:
+        copy.wait()
+    loop(groups // 2, groups, keys_values)
+    w_rows = wq[...].T
+
+    def queries(j):
+        cols = rows_of(j)
+        u = dot_nt(w_rows, normed[cols])
+        for head in range(heads):
+            some = slice(head * HEAD_DIM, (head + 1) * HEAD_DIM)
+            put_turned(q_ref, head, u[some], cols, HEAD_DIM ** (-0.5) * LOG2E)
+
+    for j in range(groups):
+        queries(j)
     kv_all[0] = kv_ref[:, :, 0:PB]
     for h in range(kvh):
         ktok[8, h] = kv_ref[h, :, PB : PB + CL].T
@@ -525,35 +592,39 @@
     for m in (2, 4, 6):
         hand_on(m).wait_send()
     kv_out.wait()
+    for j in range(groups):
+        normed_out(j).wait()
     for half in range(2):
         att_out(half).wait()
 
 
-def forward_attention(nz, q, kv, w_out, bias):
-    heads, tokens = q.shape[0], q.shape[2]
-    kvh = heads // 2
+def forward_attention(nz, x, w_query, w_key, w_value, cosine, sine, gain, w_out, bias):
+    tokens = x.shape[0]
+    heads, kvh = w_query.shape[1] // HEAD_DIM, w_key.shape[0] // HEAD_DIM
     own, width = w_out.shape
+    anywhere = pl.BlockSpec(memory_space=pl.ANY)
+    vmem = pl.BlockSpec(memory_space=VM)
     return pl.pallas_call(
         functools.partial(forward_kernel, nz),
         out_shape=(
+            jax.ShapeDtypeStruct((heads, HEAD_DIM, tokens), BF16),
+            jax.ShapeDtypeStruct((2 * kvh, HEAD_DIM, tokens), BF16),
+            jax.ShapeDtypeStruct(x.shape, BF16),
             jax.ShapeDtypeStruct((nz, heads * HEAD_DIM, tokens), BF16),
             jax.ShapeDtypeStruct((GROUP_DEVS, 2 * kvh, HEAD_DIM, PB), BF16),
             jax.ShapeDtypeStruct((heads, 1, tokens), F32),
             jax.ShapeDtypeStruct((nz * own, width), BF16),
         ),
-        in_specs=[
-            pl.BlockSpec(memory_space=VM),
-            pl.BlockSpec(memory_space=VM),
-            pl.BlockSpec(memory_space=pl.ANY),
-            pl.BlockSpec(memory_space=pltpu.SMEM),
-        ],
-        out_specs=(
-            pl.BlockSpec(memory_space=pl.ANY),
-            pl.BlockSpec(memory_space=pl.ANY),
-            pl.BlockSpec(memory_space=VM),
-            pl.BlockSpec(memory_space=pl.ANY),
-        ),
+        in_specs=[anywhere] * 4
+        + [vmem] * 3
+        + [anywhere, pl.BlockSpec(memory_space=pltpu.SMEM)],
+        out_specs=(vmem, vmem, anywhere, anywhere, anywhere, vmem, anywhere),
         scratch_shapes=[
+            VM(x.shape, BF16),
+            VM(x.shape, BF16),
+            VM(w_query.shape, BF16),
+            VM(w_key.shape, BF16),
+            VM(w_value.shape, BF16),
             VM((nz, heads * HEAD_DIM, tokens), BF16),
             VM((GROUP_DEVS, 2 * kvh, HEAD_DIM, PB), BF16),
             VM((heads, HEAD_DIM, tokens), F32),
@@ -570,6 +641,8 @@
             pltpu.SemaphoreType.DMA((2, 11)),
             pltpu.SemaphoreType.DMA((1,)),
             pltpu.SemaphoreType.DMA((3,)),
+            pltpu.SemaphoreType.DMA((tokens // 256 + 3,)),
+            pltpu.SemaphoreType.DMA((tokens // 256,)),
         ],
         compiler_params=pltpu.CompilerParams(
             collective_id=0, has_side_effects=True, vmem_limit_bytes=60 << 20
@@ -578,7 +651,7 @@
             flops=40_000_000_000, bytes_accessed=12_000_000, transcendentals=19_000_000
         ),
         name="forward_attention",
-    )(q, kv, w_out, bias)
+    )(x, w_query, w_key, w_value, cosine, sine, gain, w_out, bias)
 
 
 class Stream:
@@ -1374,18 +1447,6 @@
     )(ffn, attn, gt, act)
 
 
-def rms_inverse(inputs):
-    return lax.rsqrt(jnp.mean(inputs * inputs, axis=-1, keepdims=True) + EPSILON)
-
-
-def rotate(u, cosine, sine):
-    half = HEAD_DIM // 2
-    lower, upper = u[:, :half], u[:, half:]
-    return jnp.concatenate(
-        [lower * cosine - upper * sine, upper * cosine + lower * sine], axis=1
-    )
-
-
 def shards(
     nz,
     tokens,
@@ -1413,27 +1474,22 @@
     halfway = HEAD_DIM // 2
     frequency = ROTARY_BASE ** (-(jnp.arange(halfway, dtype=F32) * 2.0) / HEAD_DIM)
     angle = frequency[:, None] * places.astype(F32)[None, :]
-    cosine, sine = jnp.cos(angle)[None], jnp.sin(angle)[None]
+    cosine, sine = jnp.cos(angle), jnp.sin(angle)
 
     count = tokens.shape[0]
-    factor = HEAD_DIM ** (-0.5)
-    inputs = tokens.astype(F32)
-    inverse_one = rms_inverse(inputs)
-    normed = (inputs * inverse_one * attn_gain).astype(BF16)
-
-    def project(weight):
-        out = lax.dot_general(
-            weight, normed, (((0,), (1,)), ((), ())), preferred_element_type=F32
-        )
-        return out.reshape(-1, HEAD_DIM, count)
-
-    queries = (rotate(project(w_query), cosine, sine) * (factor * LOG2E)).astype(BF16)
-    keys = rotate(project(w_key), cosine, sine).astype(BF16)
-    values = project(w_value).astype(BF16)
-    kv = jnp.concatenate([keys, values], axis=0)
-    heads, kvh = queries.shape[0], keys.shape[0]
-
-    att_all, kv_all, lse, w_out_all = forward_attention(nz, queries, kv, w_out, bias)
+    heads = w_query.shape[1] // HEAD_DIM
+    queries, kv, normed, att_all, kv_all, lse, w_out_all = forward_attention(
+        nz,
+        tokens,
+        w_query,
+        w_key.T,
+        w_value.T,
+        cosine,
+        sine,
+        attn_gain[None],
+        w_out,
+        bias,
+    )
     grad_attended, row_inner, grad_w_out, grad_gain_two, grad_attention, middle, feed_part, _, ffn_piece = (
         middle_stage(
             nz,
@@ -1456,8 +1512,8 @@
         lse,
         row_inner,
         feed_part,
-        cosine[0],
-        sine[0],
+        cosine,
+        sine,
         attn_gain[None],
         grad_gain_two,
         kv_all,

time: 420 us -> 416 us (level)
  other arithmetic: 7.12 us -> 2.09 us
where the time goes in v6:
time: 416 us; the launch traced here: 409 us
  Pallas kernels  401 us (96%)
    pallas_call x1, Pallas kernels, tail_stage(): pl.pallas_call(functools.partial(tail_kernel, nz, chunk), out_shape=(jax....  182 us
    pallas_call x1, Pallas kernels, middle_stage(): pl.pallas_call(functools.partial(middle_kernel, nz, chunk), out_shape=(ja...  114 us
    pallas_call x1, Pallas kernels, forward_attention(): pl.pallas_call(functools.partial(forward_kernel, nz), out_shape=(jax.Shap...  86.6 us
    pallas_call x1, Pallas kernels, finish(): pl.pallas_call(functools.partial(finish_kernel, nq, nk), grid=(width // t...  18.5 us

profile of v6, /device:TPU:25, one launch (start us, length us, event | category | flops | bytes accessed | tf_op | source)
XLA Modules:
  0.0 408.6 jit_solution(14748039974615736627)
XLA Ops:
  0.6 0.0 copy-start
  0.7 0.6 copy-done
  1.3 0.6 gather_fusion
  2.0 1.5 multiply_sine_fusion
  3.6 0.5 compare_select_fusion.1.bias_ref
  4.1 1.3 broadcast_in_dim.18.gain_ref
  5.4 0.0 copy-start.3
  5.4 86.6 %forward_attention.1 = (bf16[4,96,1024]{2,1,0:T(8,128)(2,1)}, bf16[4,96,1024]{2,1,0:T(8,128)(2,1)}, bf16[1024,1536]{1,0:T(8,128)(2,1)}, bf16[4,384,1024]{2,1,0:T...) custom-call(bf16[1024,1536]{1,0:T(8,128)(2,1)} %x_hbm.5, ...), custom_call_target="tpu_custom_call" | custom-call | flops 40000000000 | bytes 12000000 | tf_op jit(solution)/shard_map/forward_attention/pallas_call | solution.py:607
  92.0 0.0 copy-done.3
  92.0 0.6 broadcast_in_dim.21.gain_ref
  92.6 114.2 %middle_stage.1 = (bf16[384,1024]{1,0:T(8,128)(2,1)}, f32[4,1,1024]{2,1,0:T(1,128)}, bf16[384,1536]{1,0:T(8,128)(2,1)}, f32[1,1536]{1,0:T(1,128)}, bf16[1024,153...) custom-call(bf16[1536,1024]{1,0:T(8,128)(2,1)} %bitcast.20, ...), custom_call_target="tpu_custom_call" | custom-call | flops 99999997952 | bytes 50000000 | tf_op jit(solution)/shard_map/middle_stage/pallas_call | solution.py:1348
  206.9 182.1 %tail_stage.1 = (bf16[1024,1536]{1,0:T(8,128)(2,1)}, bf16[1024,1536]{1,0:T(8,128)(2,1)}, f32[2,1536]{1,0:T(2,128)}, bf16[1152,1536]{1,0:T(8,128)(2,1)}, bf16[1536,3072]{1,0:T(8,128)(2,1)}) custom-call(bf16[4,96,1024]{2,1,0:T(8,128)(2,1)} %get-tuple-element.40.q_ref, bf16[4,96,1024]{2,1,0:T(8,128)(2,1)} %get-tuple-element.41.kv_ref, ...), custom_call_target="tpu_custom_call" | custom-call | flops 199999995904 | bytes 50000000 | tf_op jit(solution)/shard_map/tail_stage/pallas_call | solution.py:1048
  389.0 0.0 copy-start.2
  389.0 0.0 copy-start.1
  389.0 18.5 %finish.1 = (f32[1536,1024]{1,0:T(8,128)}, f32[1536,1024]{1,0:T(8,128)}, f32[1024,1536]{1,0:T(8,128)}, f32[1536,384]{1,0:T(8,128)}, f32[192,1536]{1,0:T(8,128)},...) custom-call(bf16[1536,3072]{1,0:T(8,128)(2,1)} %get-tuple-element.55.ffn, ...), custom_call_target="tpu_custom_call" | custom-call | tf_op jit(solution)/shard_map/finish/pallas_call | solution.py:1419
  407.5 0.0 copy-done.2
  407.5 0.6 slice_reduce_fusion
  408.1 0.0 copy-done.1
  (5 shorter events, 0.0 us)
Async XLA Ops:
  0.6 0.7 copy-start
  5.4 86.6 %copy-start.3 = (f32[1536]{0:T(1024)S(1)}, f32[1536]{0:T(1024)}, u32[]{:S(2)}) copy-start(f32[1536]{0:T(1024)} %param.19) | copy-start | bytes 18436
  389.0 18.5 %copy-start.2 = (f32[2,1536]{1,0:T(2,128)S(1)}, f32[2,1536]{1,0:T(2,128)}, u32[]{:S(2)}) copy-start(f32[2,1536]{1,0:T(2,128)} %get-tuple-element.61) | copy-start | bytes 36868
  389.0 19.1 %copy-start.1 = (s32[1,8]{1,0:T(1,128)S(1)}, s32[1,8]{1,0:T(1,128)}, u32[]{:S(2)}) copy-start(s32[1,8]{1,0:T(1,128)} %param.13) | copy-start | bytes 100

commit v7 on v6

--- a/solution.py
+++ b/solution.py
@@ -1314,7 +1314,7 @@
     for reduce in reduces:
         reduce.start()
     begin, end = (done + slabs // 2) * ply, line.count + lag
-    marks = (begin, begin + 9, begin + 32, end)
+    marks = (begin, begin + 7, begin + 29, end)
     loop(marks[0], marks[1], ripple)
     for reduce in reduces:
         reduce.after_core()

time: 416 us -> 416 us (level)
  no operation moved by 1% of the time
where the time goes in v7:
time: 416 us; the launch traced here: 409 us
  Pallas kernels  401 us (96%)
    pallas_call x1, Pallas kernels, tail_stage(): pl.pallas_call(functools.partial(tail_kernel, nz, chunk), out_shape=(jax....  182 us
    pallas_call x1, Pallas kernels, middle_stage(): pl.pallas_call(functools.partial(middle_kernel, nz, chunk), out_shape=(ja...  114 us
    pallas_call x1, Pallas kernels, forward_attention(): pl.pallas_call(functools.partial(forward_kernel, nz), out_shape=(jax.Shap...  86.6 us
    pallas_call x1, Pallas kernels, finish(): pl.pallas_call(functools.partial(finish_kernel, nq, nk), grid=(width // t...  18.5 us

profile of v7, /device:TPU:25, one launch (start us, length us, event | category | flops | bytes accessed | tf_op | source)
XLA Modules:
  0.0 408.6 jit_solution(17973927700127272109)
XLA Ops:
  0.6 0.0 copy-start
  0.7 0.6 copy-done
  1.3 0.6 gather_fusion
  2.0 1.5 multiply_sine_fusion
  3.6 0.5 compare_select_fusion.1.bias_ref
  4.1 1.3 broadcast_in_dim.18.gain_ref
  5.4 0.0 copy-start.3
  5.4 86.6 %forward_attention.1 = (bf16[4,96,1024]{2,1,0:T(8,128)(2,1)}, bf16[4,96,1024]{2,1,0:T(8,128)(2,1)}, bf16[1024,1536]{1,0:T(8,128)(2,1)}, bf16[4,384,1024]{2,1,0:T...) custom-call(bf16[1024,1536]{1,0:T(8,128)(2,1)} %x_hbm.5, ...), custom_call_target="tpu_custom_call" | custom-call | flops 40000000000 | bytes 12000000 | tf_op jit(solution)/shard_map/forward_attention/pallas_call | solution.py:607
  92.0 0.0 copy-done.3
  92.0 0.6 broadcast_in_dim.21.gain_ref
  92.6 114.2 %middle_stage.1 = (bf16[384,1024]{1,0:T(8,128)(2,1)}, f32[4,1,1024]{2,1,0:T(1,128)}, bf16[384,1536]{1,0:T(8,128)(2,1)}, f32[1,1536]{1,0:T(1,128)}, bf16[1024,153...) custom-call(bf16[1536,1024]{1,0:T(8,128)(2,1)} %bitcast.20, ...), custom_call_target="tpu_custom_call" | custom-call | flops 99999997952 | bytes 50000000 | tf_op jit(solution)/shard_map/middle_stage/pallas_call | solution.py:1348
  206.9 182.1 %tail_stage.1 = (bf16[1024,1536]{1,0:T(8,128)(2,1)}, bf16[1024,1536]{1,0:T(8,128)(2,1)}, f32[2,1536]{1,0:T(2,128)}, bf16[1152,1536]{1,0:T(8,128)(2,1)}, bf16[1536,3072]{1,0:T(8,128)(2,1)}) custom-call(bf16[4,96,1024]{2,1,0:T(8,128)(2,1)} %get-tuple-element.40.q_ref, bf16[4,96,1024]{2,1,0:T(8,128)(2,1)} %get-tuple-element.41.kv_ref, ...), custom_call_target="tpu_custom_call" | custom-call | flops 199999995904 | bytes 50000000 | tf_op jit(solution)/shard_map/tail_stage/pallas_call | solution.py:1048
  389.0 0.0 copy-start.2
  389.0 0.0 copy-start.1
  389.0 18.5 %finish.1 = (f32[1536,1024]{1,0:T(8,128)}, f32[1536,1024]{1,0:T(8,128)}, f32[1024,1536]{1,0:T(8,128)}, f32[1536,384]{1,0:T(8,128)}, f32[192,1536]{1,0:T(8,128)},...) custom-call(bf16[1536,3072]{1,0:T(8,128)(2,1)} %get-tuple-element.55.ffn, ...), custom_call_target="tpu_custom_call" | custom-call | tf_op jit(solution)/shard_map/finish/pallas_call | solution.py:1419
  407.5 0.0 copy-done.2
  407.5 0.6 slice_reduce_fusion
  408.1 0.0 copy-done.1
  (5 shorter events, 0.0 us)
Async XLA Ops:
  0.6 0.7 copy-start
  5.4 86.6 %copy-start.3 = (f32[1536]{0:T(1024)S(1)}, f32[1536]{0:T(1024)}, u32[]{:S(2)}) copy-start(f32[1536]{0:T(1024)} %param.19) | copy-start | bytes 18436
  389.0 18.5 %copy-start.2 = (f32[2,1536]{1,0:T(2,128)S(1)}, f32[2,1536]{1,0:T(2,128)}, u32[]{:S(2)}) copy-start(f32[2,1536]{1,0:T(2,128)} %get-tuple-element.61) | copy-start | bytes 36868
  389.0 19.1 %copy-start.1 = (s32[1,8]{1,0:T(1,128)S(1)}, s32[1,8]{1,0:T(1,128)}, u32[]{:S(2)}) copy-start(s32[1,8]{1,0:T(1,128)} %param.13) | copy-start | bytes 100
